TPU v7x, 128 devices: a whole 4x4x4 slice. The times are simulated.
128 devices in a mesh: section: 2 (over x_hi), seq: 16 (over z, y), mp: 4 (over x_lo, core).
Axes of the slice: x: 4 (x_hi: 2, x_lo: 2; x = x_hi * 2 + x_lo), y: 4, z: 4, core: 2. Of those that a mesh axis runs over, the one named last changes fastest.
Arguments:
- video: bfloat16 [2, 4, 128, 3072], P(None, None, 'seq'), may hold values from -6 to 6
- text: bfloat16 [2, 128, 3072], P(None, 'seq'), may hold values from -6 to 6
- patch_lengths: int32 [2, 4], replicated, may hold values from 1 to 128, 384 in all within a row
- text_len: int32 [2], replicated, may hold values from 64 to 128, as said below
- timestep: int32 [1], replicated, may hold values from 0 to 999
- w_mod: bfloat16 [2, 512, 9216], P('section', None, 'mp'), may hold values from -0.25 to 0.25
- w_qkv: bfloat16 [2, 3072, 3, 3072], P('section', None, None, 'mp')
- w_out: bfloat16 [2, 3072, 3072], P('section', 'mp'), may hold values from -0.109375 to 0.109375
- stale_cache: bfloat16 [2, 2, 4, 128, 2, 3072], P('section', None, None, 'seq', None, 'mp'), may hold values from -6 to 6
Outputs:
- hidden_video: bfloat16 [2, 2, 4, 128, 3072], P('section', None, None, 'seq')
- hidden_text: bfloat16 [2, 2, 128, 3072], P('section', None, 'seq')
- cache_video: bfloat16 [2, 2, 4, 128, 2, 3072], P('section', None, None, 'seq', None, 'mp')
- cache_text: bfloat16 [2, 2, 128, 2, 3072], P('section', None, 'seq', None, 'mp')
Inputs may be any that keep to these rules, and one draw needn't show every extreme that they name: `patch_lengths`: 4 patch lengths per request summing to 384; in every request the largest is 128. `text_len`: exactly one request has 128, every other fewer.
All inputs are finite; a program needn't handle non-finite values.
Results may differ from a plain program's by a relative error of at most 0.01.
Values may be sent and summed in bfloat16 or wider, within the bound.
No kernel may reach another device: no remote copies, remote signals or barrier semaphores. Data moves between devices by JAX's collectives and lax.ppermute only.
A program may use at most 192 MiB of HBM per device.

v0:
```python
import math

import jax
import jax.numpy as jnp
from jax import lax
from jax.sharding import PartitionSpec as P

HEAD = 64


EPS = 1e-05
NEG = -1e30


def passed_along(value, axis, steps):
    count = lax.axis_size(axis)
    leading, last = (max(0, -steps), min(count, count - steps))
    return lax.ppermute(value, axis, [(source, source + steps) for source in range(leading, last)])


def modulation(timestep, weight):
    half_width = weight.shape[0] // 2
    frequency = jnp.exp(-math.log(10000.0) * jnp.arange(half_width, dtype=jnp.float32) / half_width)
    phases = timestep.astype(jnp.float32)[0] * frequency
    embedding = jnp.concatenate([jnp.cos(phases), jnp.sin(phases)])
    active = jax.nn.silu(embedding).astype(jnp.bfloat16)
    return jnp.dot(active[None, :], weight, preferred_element_type=jnp.float32)[0]


def normalize(token_rows, shift_vec, scale_vec):
    values = token_rows.astype(jnp.float32)
    center = values - jnp.mean(values, axis=-1, keepdims=True)
    spread = jnp.mean(center * center, axis=-1, keepdims=True)
    return (center * lax.rsqrt(spread + EPS) * (1.0 + scale_vec) + shift_vec).astype(jnp.bfloat16)


def scores_of(query_heads, key_value, head_count):
    requests, key_count = (key_value.shape[0], key_value.shape[1])
    key_heads = key_value[:, :, 0].reshape(requests, key_count, head_count, HEAD)
    value_heads = key_value[:, :, 1].reshape(requests, key_count, head_count, HEAD)
    scores = jnp.einsum(
        "rqhe,rkhe->rhqk", query_heads, key_heads, preferred_element_type=jnp.float32
    ) * HEAD ** (-0.5)
    return (scores, value_heads)


def masked_max(scores, key_mask):
    return jnp.max(jnp.where(key_mask[:, None, None, :], scores, NEG), axis=-1)


def weighed(scores, key_mask, top_score, value_heads):
    weights = jnp.where(key_mask[:, None, None, :], jnp.exp(scores - top_score[..., None]), 0.0)
    weight_sum = jnp.sum(weights, axis=-1)
    accumulated = jnp.einsum(
        "rhqk,rkhe->rhqe",
        weights.astype(jnp.bfloat16),
        value_heads,
        preferred_element_type=jnp.float32,
    )
    return (weight_sum, accumulated)


def body(video, text, patch_lengths, text_len, timestep, w_mod, w_qkv, w_out, stale_cache):
    section_index = lax.axis_index("section")
    seq_count = lax.axis_size("seq")
    requests, patches, per_dev, model_width = video.shape
    text_dev = text.shape[1]
    capacity = per_dev * seq_count
    text_slots = text_dev * seq_count
    column_count = w_out.shape[1]
    head_count = column_count // HEAD
    row_count = per_dev + text_dev
    modulated = lax.all_gather(modulation(timestep, w_mod[0]), "mp", axis=0, tiled=True)
    shift_vec = modulated[:model_width]
    scale_vec = modulated[model_width : 2 * model_width]
    gate_vec = modulated[2 * model_width :]
    weight_qkv = w_qkv[0].reshape(model_width, 3 * column_count)
    weight_out = w_out[0]
    stale_local = stale_cache[0]
    slot_index = jnp.arange(capacity, dtype=jnp.int32)
    video_valid = (slot_index[None, None, :] < patch_lengths[:, :, None]).reshape(requests, -1)
    text_valid = jnp.arange(text_slots, dtype=jnp.int32)[None, :] < text_len[:, None]
    all_valid = jnp.concatenate([video_valid, text_valid], axis=1)
    video_patch = jnp.repeat(jnp.arange(patches, dtype=jnp.int32), capacity)
    all_patch = jnp.concatenate([video_patch, jnp.zeros((text_slots,), jnp.int32)])
    stale_whole = lax.all_gather(stale_local, "seq", axis=2, tiled=True).reshape(
        requests, patches * capacity, 2, column_count
    )
    fresh_video = jnp.zeros((requests, patches, capacity, 2, column_count), jnp.bfloat16)
    fresh_text = jnp.zeros((requests, text_slots, 2, column_count), jnp.bfloat16)
    own_video = jnp.zeros((requests, patches, per_dev, 2, column_count), jnp.bfloat16)
    own_text = jnp.zeros((requests, text_dev, 2, column_count), jnp.bfloat16)
    out_video = jnp.zeros((requests, patches, per_dev, model_width), jnp.bfloat16)
    out_text = jnp.zeros((requests, text_dev, model_width), jnp.bfloat16)
    received = jnp.zeros((requests, row_count, model_width), jnp.bfloat16)
    patch_ids = jnp.arange(patches, dtype=jnp.int32)
    for turn_index in range(patches + 1):
        patch_now = turn_index - section_index
        picked = lax.dynamic_index_in_dim(
            video, jnp.clip(patch_now, 0, patches - 1), 1, keepdims=False
        )
        token_rows = jnp.where(
            section_index == 0, jnp.concatenate([picked, text], axis=1), received
        )
        normed = normalize(token_rows, shift_vec, scale_vec)
        projected = jnp.dot(
            normed.reshape(-1, model_width), weight_qkv, preferred_element_type=jnp.float32
        )
        projected = projected.reshape(requests, row_count, 3, column_count).astype(jnp.bfloat16)
        queries = projected[:, :, 0]
        key_value = projected[:, :, 1:]
        gathered_video, gathered_text = (
            lax.all_gather(key_value[:, :per_dev], "seq", axis=1, tiled=True),
            lax.all_gather(key_value[:, per_dev:], "seq", axis=1, tiled=True),
        )
        current = patch_ids == patch_now
        fresh_video = jnp.where(
            current[None, :, None, None, None], gathered_video[:, None], fresh_video
        )
        fresh_text = jnp.where(patch_now == 0, gathered_text, fresh_text)
        own_video = jnp.where(
            current[None, :, None, None, None], key_value[:, None, :per_dev], own_video
        )
        own_text = jnp.where(patch_now == 0, key_value[:, per_dev:], own_text)
        fresh_all = jnp.concatenate(
            [fresh_video.reshape(requests, patches * capacity, 2, column_count), fresh_text], axis=1
        )
        fresh_mask = all_valid & (all_patch[None, :] <= patch_now)
        query_heads = queries.reshape(requests, row_count, head_count, HEAD)
        scores, value_heads = scores_of(query_heads, fresh_all, head_count)
        fresh_top = masked_max(scores, fresh_mask)
        fresh_sum, fresh_acc = weighed(scores, fresh_mask, fresh_top, value_heads)
        stale_mask = video_valid & (video_patch[None, :] > patch_now)
        scores, value_heads = scores_of(query_heads, stale_whole, head_count)
        stale_top = masked_max(scores, stale_mask)
        stale_sum, stale_acc = weighed(scores, stale_mask, stale_top, value_heads)
        top_score = jnp.maximum(fresh_top, stale_top)
        fresh_weight = jnp.exp(fresh_top - top_score)
        stale_weight = jnp.exp(stale_top - top_score)
        numer = fresh_acc * fresh_weight[..., None] + stale_acc * stale_weight[..., None]
        denom = fresh_sum * fresh_weight + stale_sum * stale_weight
        attended = (numer / denom[..., None]).astype(jnp.bfloat16)
        attended = attended.transpose(0, 2, 1, 3).reshape(requests * row_count, column_count)
        partial_out = jnp.dot(attended, weight_out, preferred_element_type=jnp.float32).reshape(
            requests, row_count, model_width
        )
        summed = lax.psum(partial_out, "mp")
        result = (token_rows.astype(jnp.float32) + gate_vec * summed).astype(jnp.bfloat16)
        out_video = jnp.where(current[None, :, None, None], result[:, None, :per_dev], out_video)
        out_text = jnp.where(patch_now == 0, result[:, per_dev:], out_text)
        if turn_index < patches:
            received = passed_along(result, "section", 1)
    return (out_video[None], out_text[None], own_video[None], own_text[None])


def solution(mesh):
    placed = (
        P(None, None, "seq", None),
        P(None, "seq", None),
        P(),
        P(),
        P(),
        P("section", None, "mp"),
        P("section", None, None, "mp"),
        P("section", "mp", None),
        P("section", None, None, "seq", None, "mp"),
    )
    return jax.shard_map(
        body,
        mesh=mesh,
        in_specs=placed,
        out_specs=(
            P("section", None, None, "seq", None),
            P("section", None, "seq", None),
            P("section", None, None, "seq", None, "mp"),
            P("section", None, "seq", None, "mp"),
        ),
        check_vma=False,
    )
```

profile of v0, /device:TPU:1, one launch (start us, length us, event | category | flops | bytes accessed | tf_op | source)
XLA Modules:
  0.0 715.8 jit_solution(2597853420989053191)
XLA Ops:
  8.0 18.7 %copy.75 = bf16[1,3072,3,768]{1,3,2,0:T(8,128)(2,1)} copy(bf16[1,3072,3,768]{3,1,2,0:T(8,128)(2,1)} %param.15) | data formatting | bytes 28311552 | tf_op args[6]
  27.8 6.4 all-gather.1
  35.4 9.3 %fusion.26 = bf16[2,16,3,768]{3,1,2,0:T(8,128)(2,1)S(1)} fusion(bf16[1,3072,3,768]{1,3,2,0:T(8,128)(2,1)} %copy.75, f32[3072]{0:T(1024)S(1)} %get-tuple-element.76, f32[3072]{0:T(1024)S(1)} %get-tuple-element.77, f32[2,16]{1,0:T(2,128)S(1)} %add_rsqrt_fusion.4, f32[2,16]{1,0:T(2,128)S(1)} %broadcast_multiply_fusion.4, ...), kind=kOutput, calls=%fused_computation.57 | convolution fusion | flops 454139904 | bytes 14524673 | tf_op jit(solution)/shard_map/dot_general | solution.py:106
  44.9 24.0 %all_gather.38 = bf16[2,128,2,768]{3,1,2,0:T(8,128)(2,1)S(1)} all-gather(bf16[2,8,2,768]{3,1,2,0:T(8,128)(2,1)S(1)} %get-tuple-element.73), channel_id=1, replica_groups=mesh['section'=2,'seq'=16,'mp'=4] {'seq'}, dimensions={1}, use_global_device_ids=true | all-gather | bytes 835584 | tf_op jit(solution)/shard_map/all_gather | solution.py:114
  70.1 17.3 %all_gather.37 = bf16[2,128,2,768]{3,1,2,0:T(8,128)(2,1)S(1)} all-gather(bf16[2,8,2,768]{3,1,2,0:T(8,128)(2,1)S(1)} %get-tuple-element.74), channel_id=1, replica_groups=mesh['section'=2,'seq'=16,'mp'=4] {'seq'}, dimensions={1}, use_global_device_ids=true | all-gather | bytes 835584 | tf_op jit(solution)/shard_map/all_gather | solution.py:113
  87.8 2.5 broadcast_in_dim.474
  90.3 5.7 broadcast_in_dim.475
  96.2 2.2 broadcast_select_fusion.4
  98.5 1.5 pad_maximum_fusion.4
  102.5 9.3 %fusion.259 = (bf16[2,512,1,768]{3,2,1,0:T(2,128)(2,1)}, bf16[2,512,1,768]{3,2,1,0:T(2,128)(2,1)}) fusion(bf16[2,512,2,768]{3,2,1,0:T(2,128)(2,1)} %bitcast.353), kind=kLoop, calls=%fused_computation.383 | loop fusion | bytes 6291456 | tf_op jit(solution)/shard_map/slice | solution.py:39
  111.9 6.8 copy.115
  118.7 8.1 %copy.114 = bf16[2,512,1,768]{1,3,0,2:T(8,128)(2,1)} copy(bf16[2,512,1,768]{3,2,1,0:T(2,128)(2,1)} %get-tuple-element.51) | data formatting | bytes 3145728
  126.8 2.0 select_reduce_fusion.9
  130.7 4.0 fusion.18
  134.8 45.5 %all-reduce.7.cloned.1.call-done = f32[2,16,3072]{2,1,0:T(8,128)} async-done(((f32[2,16,3072]{2,1,0:T(8,128)}), f32[2,16,3072]{2,1,0:T(8,128)}) %all-reduce.7.cloned.1.call-update) | async-done | bytes 393232 | tf_op jit(solution)/shard_map/psum | solution.py:147
  181.4 4.3 collective-permute-start
  186.3 3.5 collective-permute-done
  190.2 9.3 %fusion.29 = bf16[2,16,3,768]{3,1,2,0:T(8,128)(2,1)S(1)} fusion(bf16[1,3072,3,768]{1,3,2,0:T(8,128)(2,1)} %copy.75, bf16[2,16,3072]{2,1,0:T(8,128)(2,1)S(1)} %get-tuple-element.37, f32[2,16]{1,0:T(2,128)S(1)} %add_rsqrt_fusion.3, f32[2,16]{1,0:T(2,128)S(1)} %broadcast_multiply_fusion.3, f32[3072]{0:T(1024)S(1)} %get-tuple-element.76, ...), kind=kOutput, calls=%fused_computation.58 | convolution fusion | flops 453648384 | bytes 14524672 | tf_op jit(solution)/shard_map/dot_general | solution.py:106
  201.0 19.7 %all_gather.41 = bf16[2,128,2,768]{3,1,2,0:T(8,128)(2,1)S(1)} all-gather(bf16[2,8,2,768]{3,1,2,0:T(8,128)(2,1)S(1)} %get-tuple-element.71), channel_id=1, replica_groups=mesh['section'=2,'seq'=16,'mp'=4] {'seq'}, dimensions={1}, use_global_device_ids=true | all-gather | bytes 835584 | tf_op jit(solution)/shard_map/all_gather | solution.py:114
  220.8 1.2 copy.84
  222.0 19.2 %all_gather.40 = bf16[2,128,2,768]{3,1,2,0:T(8,128)(2,1)S(1)} all-gather(bf16[2,8,2,768]{3,1,2,0:T(8,128)(2,1)} %get-tuple-element.72), channel_id=1, replica_groups=mesh['section'=2,'seq'=16,'mp'=4] {'seq'}, dimensions={1}, use_global_device_ids=true | all-gather | bytes 835584 | tf_op jit(solution)/shard_map/all_gather | solution.py:113
  242.4 3.6 broadcast_in_dim.487
  246.0 5.8 broadcast_in_dim.488
  251.8 2.0 select_reduce_fusion.8
  254.1 2.4 broadcast_select_fusion.3
  260.6 4.0 fusion.16
  264.7 47.4 %all-reduce.9.cloned.1.call-done = f32[2,16,3072]{2,1,0:T(8,128)} async-done(((f32[2,16,3072]{2,1,0:T(8,128)}), f32[2,16,3072]{2,1,0:T(8,128)}) %all-reduce.9.cloned.1.call-update) | async-done | bytes 393232 | tf_op jit(solution)/shard_map/psum | solution.py:147
  313.2 4.3 collective-permute-start.1
  318.1 3.5 collective-permute-done.1
  322.0 9.3 %fusion.32 = bf16[2,16,3,768]{3,1,2,0:T(8,128)(2,1)S(1)} fusion(bf16[1,3072,3,768]{1,3,2,0:T(8,128)(2,1)} %copy.75, bf16[2,16,3072]{2,1,0:T(8,128)(2,1)S(1)} %get-tuple-element.32, f32[2,16]{1,0:T(2,128)S(1)} %add_rsqrt_fusion.2, f32[2,16]{1,0:T(2,128)S(1)} %broadcast_multiply_fusion.2, f32[3072]{0:T(1024)S(1)} %get-tuple-element.76, ...), kind=kOutput, calls=%fused_computation.59 | convolution fusion | flops 453648384 | bytes 14524672 | tf_op jit(solution)/shard_map/dot_general | solution.py:106
  333.4 19.7 %all_gather.43 = bf16[2,128,2,768]{3,1,2,0:T(8,128)(2,1)S(1)} all-gather(bf16[2,8,2,768]{3,1,2,0:T(8,128)(2,1)S(1)} %get-tuple-element.69), channel_id=1, replica_groups=mesh['section'=2,'seq'=16,'mp'=4] {'seq'}, dimensions={1}, use_global_device_ids=true | all-gather | bytes 835584 | tf_op jit(solution)/shard_map/all_gather | solution.py:114
  353.2 1.2 copy.89
  354.4 19.4 %all_gather.42 = bf16[2,128,2,768]{3,1,2,0:T(8,128)(2,1)S(1)} all-gather(bf16[2,8,2,768]{3,1,2,0:T(8,128)(2,1)} %get-tuple-element.70), channel_id=1, replica_groups=mesh['section'=2,'seq'=16,'mp'=4] {'seq'}, dimensions={1}, use_global_device_ids=true | all-gather | bytes 835584 | tf_op jit(solution)/shard_map/all_gather | solution.py:113
  375.0 3.6 broadcast_in_dim.494
  378.6 5.7 broadcast_in_dim.495
  384.3 2.0 select_reduce_fusion.7
  386.7 2.4 broadcast_select_fusion.2
  393.1 4.0 fusion.14
  397.3 47.4 %all-reduce.11.cloned.1.call-done = f32[2,16,3072]{2,1,0:T(8,128)} async-done(((f32[2,16,3072]{2,1,0:T(8,128)}), f32[2,16,3072]{2,1,0:T(8,128)}) %all-reduce.11.cloned.1.call-update) | async-done | bytes 393232 | tf_op jit(solution)/shard_map/psum | solution.py:147
  445.8 4.3 collective-permute-start.2
  450.7 3.5 collective-permute-done.2
  454.6 9.3 %fusion.35 = bf16[2,16,3,768]{3,1,2,0:T(8,128)(2,1)S(1)} fusion(bf16[1,3072,3,768]{1,3,2,0:T(8,128)(2,1)} %copy.75, bf16[2,16,3072]{2,1,0:T(8,128)(2,1)S(1)} %get-tuple-element.27, f32[2,16]{1,0:T(2,128)S(1)} %add_rsqrt_fusion.1, f32[2,16]{1,0:T(2,128)S(1)} %broadcast_multiply_fusion.1, f32[3072]{0:T(1024)S(1)} %get-tuple-element.76, ...), kind=kOutput, calls=%fused_computation.60 | convolution fusion | flops 453648384 | bytes 14524672 | tf_op jit(solution)/shard_map/dot_general | solution.py:106
  465.4 19.7 %all_gather.45 = bf16[2,128,2,768]{3,1,2,0:T(8,128)(2,1)S(1)} all-gather(bf16[2,8,2,768]{3,1,2,0:T(8,128)(2,1)S(1)} %get-tuple-element.67), channel_id=1, replica_groups=mesh['section'=2,'seq'=16,'mp'=4] {'seq'}, dimensions={1}, use_global_device_ids=true | all-gather | bytes 835584 | tf_op jit(solution)/shard_map/all_gather | solution.py:114
  485.1 1.2 copy.94
  486.4 19.1 %all_gather.44 = bf16[2,128,2,768]{3,1,2,0:T(8,128)(2,1)S(1)} all-gather(bf16[2,8,2,768]{3,1,2,0:T(8,128)(2,1)} %get-tuple-element.68), channel_id=1, replica_groups=mesh['section'=2,'seq'=16,'mp'=4] {'seq'}, dimensions={1}, use_global_device_ids=true | all-gather | bytes 835584 | tf_op jit(solution)/shard_map/all_gather | solution.py:113
  506.7 3.6 broadcast_in_dim.501
  510.3 5.8 broadcast_in_dim.502
  516.1 2.0 select_reduce_fusion.6
  518.4 2.4 broadcast_select_fusion.1
  524.8 4.0 fusion.12
  529.0 47.4 %all-reduce.13.cloned.1.call-done = f32[2,16,3072]{2,1,0:T(8,128)} async-done(((f32[2,16,3072]{2,1,0:T(8,128)}), f32[2,16,3072]{2,1,0:T(8,128)}) %all-reduce.13.cloned.1.call-update) | async-done | bytes 393232 | tf_op jit(solution)/shard_map/psum | solution.py:147
  577.4 4.3 collective-permute-start.3
  582.4 3.5 collective-permute-done.3
  586.3 9.3 %fusion.38 = bf16[2,16,3,768]{3,1,2,0:T(8,128)(2,1)S(1)} fusion(bf16[1,3072,3,768]{1,3,2,0:T(8,128)(2,1)} %copy.75, bf16[2,16,3072]{2,1,0:T(8,128)(2,1)S(1)} %get-tuple-element.22, f32[2,16]{1,0:T(2,128)S(1)} %add_rsqrt_fusion, f32[2,16]{1,0:T(2,128)S(1)} %broadcast_multiply_fusion, f32[3072]{0:T(1024)S(1)} %get-tuple-element.76, ...), kind=kOutput, calls=%fused_computation.61 | convolution fusion | flops 453648384 | bytes 14524672 | tf_op jit(solution)/shard_map/dot_general | solution.py:106
  595.8 1.5 select_bitcast_fusion
  597.3 19.7 %all_gather.47 = bf16[2,128,2,768]{3,1,2,0:T(8,128)(2,1)S(1)} all-gather(bf16[2,8,2,768]{3,1,2,0:T(8,128)(2,1)S(1)} %get-tuple-element.65), channel_id=1, replica_groups=mesh['section'=2,'seq'=16,'mp'=4] {'seq'}, dimensions={1}, use_global_device_ids=true | all-gather | bytes 835584 | tf_op jit(solution)/shard_map/all_gather | solution.py:114
  618.2 19.2 %all_gather.46 = bf16[2,128,2,768]{3,1,2,0:T(8,128)(2,1)S(1)} all-gather(bf16[2,8,2,768]{3,1,2,0:T(8,128)(2,1)} %get-tuple-element.66), channel_id=1, replica_groups=mesh['section'=2,'seq'=16,'mp'=4] {'seq'}, dimensions={1}, use_global_device_ids=true | all-gather | bytes 835584 | tf_op jit(solution)/shard_map/all_gather | solution.py:113
  637.8 2.5 broadcast_in_dim.508
  640.2 5.7 broadcast_in_dim.509
  646.0 2.0 select_reduce_fusion.5
  648.4 2.4 broadcast_select_fusion
  654.2 4.2 fusion.10
  660.3 1.5 copy.108
  662.8 43.2 %all-reduce.15.cloned.1.call-done = f32[2,16,3072]{2,1,0:T(8,128)} async-done(((f32[2,16,3072]{2,1,0:T(8,128)}), f32[2,16,3072]{2,1,0:T(8,128)}) %all-reduce.15.cloned.1.call-update) | async-done | bytes 393232 | tf_op jit(solution)/shard_map/psum | solution.py:147
  (255 shorter events, 50.0 us)
Async XLA Ops:
  7.2 20.3 %copy-start = (bf16[1,512,2304]{2,1,0:T(8,128)(2,1)S(1)}, bf16[1,512,2304]{2,1,0:T(8,128)(2,1)}, u32[]{:S(2)}) copy-start(bf16[1,512,2304]{2,1,0:T(8,128)(2,1)} %param.14) | copy-start | bytes 7077892
  7.2 95.4 %all-gather.4.cloned.1.call-start = ((), (), s32[]{:S(2)}) async-start(), calls=%async_computation.5 | async-start | bytes 3342336 | tf_op jit(solution)/shard_map/all_gather | solution.py:86
  7.9 172.4 %all-reduce.7.cloned.1.call-start = ((), (), s32[]{:S(2)}) async-start(), calls=%async_computation | async-start | bytes 786432 | tf_op jit(solution)/shard_map/psum | solution.py:147
  8.0 26.3 %copy-start.34 = (bf16[2,4,8,3072]{3,2,1,0:T(8,128)(2,1)S(1)}, bf16[2,4,8,3072]{3,2,1,0:T(8,128)(2,1)}, u32[]{:S(2)}) copy-start(bf16[2,4,8,3072]{3,2,1,0:T(8,128)(2,1)} %param.9) | copy-start | bytes 1179652
  26.6 8.4 %copy-start.9 = (bf16[2,8,3072]{2,1,0:T(8,128)(2,1)S(1)}, bf16[2,8,3072]{2,1,0:T(8,128)(2,1)}, u32[]{:S(2)}) copy-start(bf16[2,8,3072]{2,1,0:T(8,128)(2,1)} %param.10) | copy-start | bytes 294916
  44.7 43.1 %copy-start.22 = (bf16[2,16,3,768]{3,1,2,0:T(8,128)(2,1)}, bf16[2,16,3,768]{3,1,2,0:T(8,128)(2,1)S(1)}, u32[]{:S(2)}) copy-start(bf16[2,16,3,768]{3,1,2,0:T(8,128)(2,1)S(1)} %fusion.26) | copy-start | bytes 442372
  44.9 55.8 %copy-start.18 = (bf16[2,16,12,64]{3,2,1,0:T(8,128)(2,1)}, bf16[2,16,12,64]{3,2,1,0:T(8,128)(2,1)S(1)}, u32[]{:S(2)}) copy-start(bf16[2,16,12,64]{3,2,1,0:T(8,128)(2,1)S(1)} %reshape_squeeze.63) | copy-start | bytes 147460
  96.1 2.3 copy-start.44
  96.2 2.2 copy-start.42
  96.2 2.2 copy-start.12
  98.4 1.5 copy-start.55
  98.4 1.6 copy-start.50
  126.8 2.9 copy-start.11
  126.8 2.9 copy-start.17
  130.7 59.2 %copy-start.40 = (bf16[2,8,3072]{2,1,0:T(8,128)(2,1)S(1)}, bf16[2,8,3072]{2,1,0:T(8,128)(2,1)}, u32[]{:S(2)}) copy-start(bf16[2,8,3072]{2,1,0:T(8,128)(2,1)} %get-tuple-element.57) | copy-start | bytes 294916
  134.8 177.4 %all-reduce.9.cloned.1.call-start = ((), (), s32[]{:S(2)}) async-start(), calls=%async_computation.1 | async-start | bytes 786432 | tf_op jit(solution)/shard_map/psum | solution.py:147
  134.8 55.0 %copy-start.46 = (pred[4]{0:T(512)(128)(4,1)}, pred[4]{0:T(512)(128)(4,1)S(1)}, u32[]{:S(2)}) copy-start(pred[4]{0:T(512)(128)(4,1)S(1)} %iota_compare_fusion.3) | copy-start | bytes 16
  181.4 8.8 %copy-start.26 = (bf16[2,16,3072]{2,1,0:T(8,128)(2,1)}, bf16[2,16,3072]{2,1,0:T(8,128)(2,1)S(1)}, u32[]{:S(2)}) copy-start(bf16[2,16,3072]{2,1,0:T(8,128)(2,1)S(1)} %fusion.136) | copy-start | bytes 589828
  181.4 8.4 %collective-permute-start = (bf16[2,16,3072]{2,1,0:T(8,128)(2,1)S(1)}, bf16[2,16,3072]{2,1,0:T(8,128)(2,1)S(1)}, u32[]{:S(2)}, u32[]{:S(2)}) collective-permute-start(bf16[2,16,3072]{2,1,0:T(8,128)(2,1)S(1)} %fusion.136), channel_id=1, source_target_pairs={{0,64},{1,65},{2,66},{3,67},{4,68},{5,69},{6,70},{7,71},{8,72},{9,... | collective-permute-start | bytes 589832 | tf_op jit(solution)/shard_map/ppermute | solution.py:18
  199.5 1.5 copy-start.23
  246.0 5.8 copy-start.19
  251.8 2.4 copy-start.2
  251.8 2.4 copy-start.43
  251.8 2.4 copy-start.52
  254.1 2.4 copy-start.14
  256.5 1.6 copy-start.3
  256.5 1.6 copy-start.41
  260.6 61.1 %copy-start.39 = (bf16[2,8,3072]{2,1,0:T(8,128)(2,1)S(1)}, bf16[2,8,3072]{2,1,0:T(8,128)(2,1)}, u32[]{:S(2)}) copy-start(bf16[2,8,3072]{2,1,0:T(8,128)(2,1)} %get-tuple-element.54) | copy-start | bytes 294916
  264.6 180.1 %all-reduce.11.cloned.1.call-start = ((), (), s32[]{:S(2)}) async-start(), calls=%async_computation.2 | async-start | bytes 786432 | tf_op jit(solution)/shard_map/psum | solution.py:147
  264.7 57.1 %copy-start.48 = (pred[4]{0:T(512)(128)(4,1)}, pred[4]{0:T(512)(128)(4,1)S(1)}, u32[]{:S(2)}) copy-start(pred[4]{0:T(512)(128)(4,1)S(1)} %iota_compare_fusion.2) | copy-start | bytes 16
  313.2 8.8 %copy-start.28 = (bf16[2,16,3072]{2,1,0:T(8,128)(2,1)}, bf16[2,16,3072]{2,1,0:T(8,128)(2,1)S(1)}, u32[]{:S(2)}) copy-start(bf16[2,16,3072]{2,1,0:T(8,128)(2,1)S(1)} %fusion.137) | copy-start | bytes 589828
  313.2 8.4 %collective-permute-start.1 = (bf16[2,16,3072]{2,1,0:T(8,128)(2,1)S(1)}, bf16[2,16,3072]{2,1,0:T(8,128)(2,1)S(1)}, u32[]{:S(2)}, u32[]{:S(2)}) collective-permute-start(bf16[2,16,3072]{2,1,0:T(8,128)(2,1)S(1)} %fusion.137), channel_id=1, source_target_pairs={{0,64},{1,65},{2,66},{3,67},{4,68},{5,69},{6,70},{7,71},{8,72},{9,... | collective-permute-start | bytes 589832 | tf_op jit(solution)/shard_map/ppermute | solution.py:18
  384.3 2.4 copy-start.4
  384.3 2.4 copy-start.54
  386.7 2.4 copy-start.16
  389.1 1.6 copy-start.7
  389.1 1.6 copy-start.21
  393.1 61.1 %copy-start.38 = (bf16[2,8,3072]{2,1,0:T(8,128)(2,1)S(1)}, bf16[2,8,3072]{2,1,0:T(8,128)(2,1)}, u32[]{:S(2)}) copy-start(bf16[2,8,3072]{2,1,0:T(8,128)(2,1)} %get-tuple-element.55) | copy-start | bytes 294916
  397.2 179.2 %all-reduce.13.cloned.1.call-start = ((), (), s32[]{:S(2)}) async-start(), calls=%async_computation.3 | async-start | bytes 786432 | tf_op jit(solution)/shard_map/psum | solution.py:147
  445.8 8.8 %copy-start.30 = (bf16[2,16,3072]{2,1,0:T(8,128)(2,1)}, bf16[2,16,3072]{2,1,0:T(8,128)(2,1)S(1)}, u32[]{:S(2)}) copy-start(bf16[2,16,3072]{2,1,0:T(8,128)(2,1)S(1)} %fusion.138) | copy-start | bytes 589828
  445.8 8.4 %collective-permute-start.2 = (bf16[2,16,3072]{2,1,0:T(8,128)(2,1)S(1)}, bf16[2,16,3072]{2,1,0:T(8,128)(2,1)S(1)}, u32[]{:S(2)}, u32[]{:S(2)}) collective-permute-start(bf16[2,16,3072]{2,1,0:T(8,128)(2,1)S(1)} %fusion.138), channel_id=1, source_target_pairs={{0,64},{1,65},{2,66},{3,67},{4,68},{5,69},{6,70},{7,71},{8,72},{9,... | collective-permute-start | bytes 589832 | tf_op jit(solution)/shard_map/ppermute | solution.py:18
  463.9 1.5 copy-start.25
  510.3 5.8 copy-start.20
  516.1 2.4 copy-start.8
  516.1 2.4 copy-start.53
  518.4 2.4 copy-start.15
  520.8 1.6 copy-start.5
  524.8 61.1 %copy-start.37 = (bf16[2,8,3072]{2,1,0:T(8,128)(2,1)S(1)}, bf16[2,8,3072]{2,1,0:T(8,128)(2,1)}, u32[]{:S(2)}) copy-start(bf16[2,8,3072]{2,1,0:T(8,128)(2,1)} %get-tuple-element.53) | copy-start | bytes 294916
  528.9 177.1 %all-reduce.15.cloned.1.call-start = ((), (), s32[]{:S(2)}) async-start(), calls=%async_computation.4 | async-start | bytes 786432 | tf_op jit(solution)/shard_map/psum | solution.py:147
  577.4 8.6 %copy-start.32 = (bf16[2,16,3072]{2,1,0:T(8,128)(2,1)}, bf16[2,16,3072]{2,1,0:T(8,128)(2,1)S(1)}, u32[]{:S(2)}) copy-start(bf16[2,16,3072]{2,1,0:T(8,128)(2,1)S(1)} %fusion.139) | copy-start | bytes 589828
  577.4 8.4 %collective-permute-start.3 = (bf16[2,16,3072]{2,1,0:T(8,128)(2,1)S(1)}, bf16[2,16,3072]{2,1,0:T(8,128)(2,1)S(1)}, u32[]{:S(2)}, u32[]{:S(2)}) collective-permute-start(bf16[2,16,3072]{2,1,0:T(8,128)(2,1)S(1)} %fusion.139), channel_id=1, source_target_pairs={{0,64},{1,65},{2,66},{3,67},{4,68},{5,69},{6,70},{7,71},{8,72},{9,... | collective-permute-start | bytes 589832 | tf_op jit(solution)/shard_map/ppermute | solution.py:18
  646.0 2.4 copy-start.6
  646.0 2.4 copy-start.51
  648.4 2.4 copy-start.13
  654.2 4.3 copy-start.35
  654.2 4.4 copy-start.36
  654.2 7.6 %copy-start.45 = (pred[4]{0:T(512)(128)(4,1)S(1)}, pred[4]{0:T(512)(128)(4,1)}, u32[]{:S(2)}) copy-start(pred[4]{0:T(512)(128)(4,1)} %copy-done.44) | copy-start | bytes 16
  654.2 7.6 %copy-start.47 = (pred[4]{0:T(512)(128)(4,1)S(1)}, pred[4]{0:T(512)(128)(4,1)}, u32[]{:S(2)}) copy-start(pred[4]{0:T(512)(128)(4,1)} %copy-done.46) | copy-start | bytes 16
  654.2 7.6 %copy-start.49 = (pred[4]{0:T(512)(128)(4,1)S(1)}, pred[4]{0:T(512)(128)(4,1)}, u32[]{:S(2)}) copy-start(pred[4]{0:T(512)(128)(4,1)} %copy-done.48) | copy-start | bytes 16
  654.2 52.8 %copy-start.27 = (bf16[2,16,3072]{2,1,0:T(8,128)(2,1)S(1)}, bf16[2,16,3072]{2,1,0:T(8,128)(2,1)}, u32[]{:S(2)}) copy-start(bf16[2,16,3072]{2,1,0:T(8,128)(2,1)} %copy-done.26) | copy-start | bytes 589828
  654.2 52.8 %copy-start.29 = (bf16[2,16,3072]{2,1,0:T(8,128)(2,1)S(1)}, bf16[2,16,3072]{2,1,0:T(8,128)(2,1)}, u32[]{:S(2)}) copy-start(bf16[2,16,3072]{2,1,0:T(8,128)(2,1)} %copy-done.28) | copy-start | bytes 589828
  654.2 52.8 %copy-start.31 = (bf16[2,16,3072]{2,1,0:T(8,128)(2,1)S(1)}, bf16[2,16,3072]{2,1,0:T(8,128)(2,1)}, u32[]{:S(2)}) copy-start(bf16[2,16,3072]{2,1,0:T(8,128)(2,1)} %copy-done.30) | copy-start | bytes 589828
  654.2 52.8 %copy-start.33 = (bf16[2,16,3072]{2,1,0:T(8,128)(2,1)S(1)}, bf16[2,16,3072]{2,1,0:T(8,128)(2,1)}, u32[]{:S(2)}) copy-start(bf16[2,16,3072]{2,1,0:T(8,128)(2,1)} %copy-done.32) | copy-start | bytes 589828
  654.2 54.4 %copy-start.1 = (bf16[1,512,2304]{2,1,0:T(8,128)(2,1)S(1)}, bf16[1,512,2304]{2,1,0:T(8,128)(2,1)}, u32[]{:S(2)}) copy-start(bf16[1,512,2304]{2,1,0:T(8,128)(2,1)} %param.14) | copy-start | bytes 7077892
  (2 other events, 1.7 us)
Sparse Core Ops, SparseCore 0:
  10.2 52.0 all-gather.3
  134.9 45.3 all-reduce.6
  264.8 47.3 all-reduce.8
  397.3 47.3 all-reduce.10
  529.0 47.3 all-reduce.12
  658.6 47.3 all-reduce.14
where the time goes:
time: 723 us; the launch traced here: 716 us
  waiting for transfers between devices  246 us (34%)
  blocking collectives  203 us (28%)
  local copies, waits for them, and re-layouts  116 us (16%)
  matrix products  86.7 us (12%)
  other arithmetic  30.2 us (4%)
  starting transfers between devices  17.5 us (2%)
  between operations  16 us (2%)
    psum x5, waiting for transfers between devices, body(): summed = lax.psum(partial_out, 'mp')  231 us
    all_gather x5, blocking collectives, body(): lax.all_gather(key_value[:, per_dev:], 'seq', axis=1, tiled=True)  103 us
    all_gather x5, blocking collectives, body(): lax.all_gather(key_value[:, :per_dev], 'seq', axis=1, tiled=True)  94.3 us
    broadcast_in_dim x15, local copies, waits for them, and re-layouts, body(): jnp.where(current[None, :, None, None, None], gathered_video[:, None], fr...  47 us
    dot_general x5, matrix products, body(): jnp.dot(normed.reshape(-1, model_width), weight_qkv, preferred_element_ty...  46.6 us
    unnamed x117, local copies, waits for them, and re-layouts  41 us
    dot_general x5, matrix products, body(): jnp.dot(attended, weight_out, preferred_element_type=jnp.float32)  20.3 us
    ppermute x4, starting transfers between devices, passed_along(): lax.ppermute(value, axis, [(source, source + steps) for source in range(l...  17.3 us
  transfers between devices with their start and end apart: 10, of which 9 were waited for; matrix products, arithmetic and copies ran while one was open for 7% of the time, Pallas kernels for 0%

commit v1 on v0

v1 whole, which is shorter than its diff:
```python
import math

import jax
import jax.numpy as jnp
from jax import lax
from jax.experimental import pallas as pl
from jax.experimental.pallas import tpu as pltpu
from jax.sharding import PartitionSpec as P

HEAD = 64
LANES = 128
EPS = 1e-05
NEG = -1e30
VMEM_LIMIT = 56 * 1024 * 1024


def modulation(timestep, weight):
    half_width = weight.shape[0] // 2
    frequency = jnp.exp(-math.log(10000.0) * jnp.arange(half_width, dtype=jnp.float32) / half_width)
    phases = timestep.astype(jnp.float32)[0] * frequency
    embedding = jnp.concatenate([jnp.cos(phases), jnp.sin(phases)])
    active = jax.nn.silu(embedding).astype(jnp.bfloat16)
    return jnp.dot(active[None, :], weight, preferred_element_type=jnp.float32)


def swap(value, mapping):
    pairs = []
    for section in range(2):
        for part in range(4):
            target = mapping(section, part)
            if target is not None:
                pairs.append((section * 4 + part, target[0] * 4 + target[1]))
    return lax.ppermute(value, ("section", "mp"), pairs)


def swap_core(value):
    return swap(value, lambda section, part: (section, part ^ 1))


def swap_chip(value):
    return swap(value, lambda section, part: (section, part ^ 2))


def next_section(value):
    return swap(value, lambda section, part: (1, part ^ 2) if section == 0 else None)


def qkv_kernel(*refs, rows, units, stale_rows):
    if stale_rows:
        x_ref, mod_ref, w_ref, stale_ref, o_ref, normed_ref, w_buf, sems = refs
    else:
        x_ref, mod_ref, w_ref, o_ref, normed_ref, w_buf, sems = refs
    parts, width, columns = w_ref.shape
    chunks = sems.shape[1]
    depth = width // chunks
    copies = []
    for part in range(parts):
        for chunk in range(chunks):
            span = pl.ds(chunk * depth, depth)
            copy = pltpu.make_async_copy(
                w_ref.at[part, span, :], w_buf.at[part, span, :], sems.at[part, chunk]
            )
            copy.start()
            copies.append(copy)
    total = x_ref.shape[0]
    step = 16
    shift = mod_ref[0:1, :]
    scale = 1.0 + mod_ref[1:2, :]
    for start in range(0, total, step):
        values = x_ref[start : start + step, :].astype(jnp.float32)
        center = values - jnp.mean(values, axis=-1, keepdims=True)
        spread = jnp.mean(center * center, axis=-1, keepdims=True)
        normed = center * lax.rsqrt(spread + EPS) * scale + shift
        normed_ref[start : start + step, :] = normed.astype(jnp.bfloat16)
    blocks = columns // LANES
    if stale_rows:
        for unit in range(units):
            o_ref[unit, 3 * rows : 3 * rows + stale_rows, :] = stale_ref[unit]
    for unit in range(units, o_ref.shape[0]):
        o_ref[unit] = jnp.zeros(o_ref.shape[1:], o_ref.dtype)
    for part in range(parts):
        acc = jnp.zeros((total, columns), jnp.float32)
        for chunk in range(chunks):
            copies[part * chunks + chunk].wait()
            acc += jnp.dot(
                normed_ref[:, chunk * depth : (chunk + 1) * depth],
                w_buf[part, chunk * depth : (chunk + 1) * depth, :],
                preferred_element_type=jnp.float32,
            )
        for request in range(total // rows):
            for block in range(blocks):
                o_ref[request * blocks + block, part * rows : (part + 1) * rows, :] = acc[
                    request * rows : (request + 1) * rows, block * LANES : (block + 1) * LANES
                ].astype(jnp.bfloat16)


def qkv_call(x, mod, weight, stale, rows, devices):
    total, width = x.shape
    parts, _, columns = weight.shape
    units = (total // rows) * (columns // LANES)
    stale_rows = 0 if stale is None else stale.shape[1]
    chunks = 2
    vmem = pl.BlockSpec(memory_space=pltpu.VMEM)
    operands = [x, mod, weight] + ([] if stale is None else [stale])
    return pl.pallas_call(
        lambda *refs: qkv_kernel(*refs, rows=rows, units=units, stale_rows=stale_rows),
        out_shape=jax.ShapeDtypeStruct((devices, 3 * rows + stale_rows, LANES), jnp.bfloat16),
        in_specs=[vmem, vmem, pl.BlockSpec(memory_space=pl.ANY)] + [vmem] * (len(operands) - 3),
        out_specs=vmem,
        scratch_shapes=[
            pltpu.VMEM((total, width), jnp.bfloat16),
            pltpu.VMEM(weight.shape, jnp.bfloat16),
            pltpu.SemaphoreType.DMA((parts, chunks)),
        ],
        compiler_params=pltpu.CompilerParams(vmem_limit_bytes=VMEM_LIMIT),
        name="qkv",
    )(*operands)


def attention_kernel(lens_ref, recv_ref, stale_ref, o_ref, *, rows, per_dev, patches):
    devices = recv_ref.shape[0]
    capacity = devices * per_dev

    def block(ref, base, index):
        start = base + index * per_dev
        return ref[:, start : start + per_dev, :].reshape(capacity, LANES)

    groups = patches + 1
    fresh_k = [block(recv_ref, rows, index) for index in range(groups)]
    fresh_v = [block(recv_ref, 2 * rows, index) for index in range(groups)]
    stale_base = 3 * rows
    stale_k = [None] + [block(stale_ref, stale_base, index) for index in range(patches - 1)]
    stale_base += (patches - 1) * per_dev
    stale_v = [None] + [block(stale_ref, stale_base, index) for index in range(patches - 1)]
    slot = lax.broadcasted_iota(jnp.int32, (1, groups * capacity), 1)
    limit = jnp.zeros((1, groups * capacity), jnp.int32)
    for index in range(groups):
        limit = jnp.where(slot >= index * capacity, lens_ref[index] + index * capacity, limit)
    bias = jnp.where(slot < limit, 0.0, NEG)
    lane = lax.broadcasted_iota(jnp.int32, (1, LANES), 1)
    factor = HEAD ** (-0.5) * math.log2(math.e)
    for patch in range(patches):
        keys = jnp.concatenate(
            [fresh_k[i] if i <= patch else stale_k[i] for i in range(patches)] + [fresh_k[patches]], axis=0
        )
        values = jnp.concatenate(
            [fresh_v[i] if i <= patch else stale_v[i] for i in range(patches)] + [fresh_v[patches]], axis=0
        )
        for group in [patch, patches] if patch == 0 else [patch]:
            queries = block(recv_ref, 0, group)
            outs = []
            for head in range(2):
                mine = (lane < HEAD) if head == 0 else (lane >= HEAD)
                scores = lax.dot_general(
                    jnp.where(mine, queries, jnp.zeros_like(queries)),
                    keys,
                    (((1,), (1,)), ((), ())),
                    preferred_element_type=jnp.float32,
                )
                scores = scores + bias
                top = jnp.max(scores, axis=-1, keepdims=True)
                weights = jnp.exp2((scores - top) * factor)
                weight_sum = jnp.sum(weights, axis=-1, keepdims=True)
                acc = jnp.dot(
                    weights.astype(jnp.bfloat16), values, preferred_element_type=jnp.float32
                )
                outs.append(acc / weight_sum)
            out = jnp.where(lane < HEAD, outs[0], outs[1]).astype(jnp.bfloat16)
            start = group * per_dev
            o_ref[:, start : start + per_dev, :] = out.reshape(devices, per_dev, LANES)


def attention_call(lens, recv, stale, rows, per_dev, patches):
    devices = recv.shape[0]
    vmem = pl.BlockSpec(memory_space=pltpu.VMEM)
    return pl.pallas_call(
        lambda *refs: attention_kernel(*refs, rows=rows, per_dev=per_dev, patches=patches),
        out_shape=jax.ShapeDtypeStruct((devices, rows, LANES), jnp.bfloat16),
        in_specs=[pl.BlockSpec(memory_space=pltpu.SMEM), vmem, vmem],
        out_specs=vmem,
        compiler_params=pltpu.CompilerParams(vmem_limit_bytes=VMEM_LIMIT),
        name="attention",
    )(lens, recv, stale)


def out_kernel(recv_ref, gate_ref, w_ref, o_ref, mixed_ref, w_buf, sems, *, requests):
    depth, width = w_ref.shape
    rows = recv_ref.shape[1]
    blocks = depth // LANES
    chunks = sems.shape[0]
    span = width // chunks
    copies = []
    for chunk in range(chunks):
        at = pl.ds(chunk * span, span)
        copy = pltpu.make_async_copy(w_ref.at[:, at], w_buf.at[:, at], sems.at[chunk])
        copy.start()
        copies.append(copy)
    for request in range(requests):
        for block in range(blocks):
            mixed_ref[request * rows : (request + 1) * rows, block * LANES : (block + 1) * LANES] = recv_ref[
                request * blocks + block
            ]
    per_half = chunks // 2
    for chunk in range(chunks):
        copies[chunk].wait()
        acc = jnp.dot(
            mixed_ref[...],
            w_buf[:, chunk * span : (chunk + 1) * span],
            preferred_element_type=jnp.float32,
        )
        acc = acc * gate_ref[0:1, chunk * span : (chunk + 1) * span]
        at = (chunk % per_half) * span
        o_ref[chunk // per_half, :, at : at + span] = acc.astype(jnp.bfloat16)


def out_call(recv, gate, weight, requests):
    depth, width = weight.shape
    total = requests * recv.shape[1]
    chunks = 4
    vmem = pl.BlockSpec(memory_space=pltpu.VMEM)
    return pl.pallas_call(
        lambda *refs: out_kernel(*refs, requests=requests),
        out_shape=jax.ShapeDtypeStruct((2, total, width // 2), jnp.bfloat16),
        in_specs=[vmem, vmem, pl.BlockSpec(memory_space=pl.ANY)],
        out_specs=vmem,
        scratch_shapes=[
            pltpu.VMEM((total, depth), jnp.bfloat16),
            pltpu.VMEM(weight.shape, jnp.bfloat16),
            pltpu.SemaphoreType.DMA((chunks,)),
        ],
        compiler_params=pltpu.CompilerParams(vmem_limit_bytes=VMEM_LIMIT),
        name="out_projection",
    )(recv, gate, weight)


def body(video, text, patch_lengths, text_len, timestep, w_mod, w_qkv, w_out, stale_cache):
    section = lax.axis_index("section")
    core = lax.axis_index("mp") % 2
    chip = lax.axis_index("mp") // 2
    devices = lax.axis_size("seq")
    requests, patches, per_dev, width = video.shape
    text_dev = text.shape[1]
    columns = w_out.shape[1]
    blocks = columns // LANES
    units = requests * blocks
    rows = patches * per_dev + text_dev
    half = width // 2

    def in_order(mine, other, which):
        return jnp.where(which == 0, jnp.concatenate([mine, other], -1), jnp.concatenate([other, mine], -1))

    own_mod = modulation(timestep, w_mod[0])
    chip_mod = in_order(own_mod, swap_core(own_mod), core)
    modulated = in_order(chip_mod, swap_chip(chip_mod), chip).reshape(3, width)
    gate = modulated[2:3]

    weight_qkv = w_qkv[0].transpose(1, 0, 2)
    weight_out = w_out[0]
    stale = stale_cache[0][:, 1:].reshape(requests, (patches - 1) * per_dev, 2, blocks, LANES)
    stale = stale.transpose(0, 3, 2, 1, 4).reshape(units, 2 * (patches - 1) * per_dev, LANES)
    x = jnp.concatenate([video.reshape(requests, patches * per_dev, width), text], axis=1)
    x = x.reshape(requests * rows, width)

    request = jnp.minimum(lax.axis_index("seq") // blocks, requests - 1)
    lens = jnp.concatenate([patch_lengths, text_len[:, None]], axis=1)
    lens = lax.dynamic_index_in_dim(lens, request, 0, keepdims=False)

    def half_of(value):
        return lax.dynamic_slice_in_dim(value, core * half, half, 1)

    def after_qkv(x_now, sent, stale_recv):
        recv = lax.all_to_all(sent, "seq", 0, 0, tiled=True)
        attended = attention_call(
            lens, recv, recv if stale_recv is None else stale_recv, rows, per_dev, patches
        )
        mixed = lax.all_to_all(attended, "seq", 0, 0, tiled=True)
        partial = out_call(mixed, gate, weight_out, requests)
        mine = lax.dynamic_index_in_dim(partial, core, 0, keepdims=False)
        other = lax.dynamic_index_in_dim(partial, 1 - core, 0, keepdims=False)
        on_chip = (mine.astype(jnp.float32) + swap_core(other).astype(jnp.float32)).astype(jnp.bfloat16)
        summed = on_chip.astype(jnp.float32) + swap_chip(on_chip).astype(jnp.float32)
        result = (half_of(x_now).astype(jnp.float32) + summed).astype(jnp.bfloat16)
        return recv, result

    sent_0 = qkv_call(x, modulated, weight_qkv, stale, rows, devices)
    recv_0, result_0 = after_qkv(x, sent_0, None)
    arrived = next_section(result_0)
    x_1 = in_order(arrived, swap_core(arrived), core)
    sent_1 = qkv_call(x_1, modulated, weight_qkv, None, rows, devices)
    _, result_1 = after_qkv(x_1, sent_1, recv_0)

    result = jnp.where(section == 0, result_0, result_1)
    result = in_order(result, swap_core(result), core).reshape(requests, rows, width)
    key_value = jnp.where(section == 0, sent_0[:units, rows : 3 * rows], sent_1[:units, rows : 3 * rows])
    key_value = key_value.reshape(requests, blocks, 2, rows, LANES).transpose(0, 3, 2, 1, 4)
    key_value = key_value.reshape(requests, rows, 2, columns)
    split_at = patches * per_dev
    return (
        result[:, :split_at].reshape(1, requests, patches, per_dev, width),
        result[:, split_at:][None],
        key_value[:, :split_at].reshape(1, requests, patches, per_dev, 2, columns),
        key_value[:, split_at:][None],
    )


def solution(mesh):
    placed = (
        P(None, None, "seq", None),
        P(None, "seq", None),
        P(),
        P(),
        P(),
        P("section", None, "mp"),
        P("section", None, None, "mp"),
        P("section", "mp", None),
        P("section", None, None, "seq", None, "mp"),
    )
    return jax.shard_map(
        body,
        mesh=mesh,
        in_specs=placed,
        out_specs=(
            P("section", None, None, "seq", None),
            P("section", None, "seq", None),
            P("section", None, None, "seq", None, "mp"),
            P("section", None, "seq", None, "mp"),
        ),
        check_vma=False,
    )
```

time: 723 us -> 150 us (0.21)
  waiting for transfers between devices: 246 us -> 38.2 us
  blocking collectives: 203 us -> 26.2 us
  local copies, waits for them, and re-layouts: 116 us -> 10.6 us
  matrix products: 86.7 us -> 0.42 us
  Pallas kernels: 0 us -> 35.6 us
  other arithmetic: 30.2 us -> 7.84 us
  between operations: 16 us -> 1.7 us
  starting transfers between devices: 17.5 us -> 28.6 us
    psum x5 -> x0, waiting for transfers between devices: 231 us -> none  [body(): summed = lax.psum(partial_out, 'mp')]
    all_gather x11 -> x0, blocking collectives: 203 us -> none  [the longest x5 103 us: body(): lax.all_gather(key_value[:, per_dev:], 'seq', axis=1, tiled=True)]
    dot_general x31 -> x1, matrix products: 86.7 us -> 0.42 us  [modulation(): return jnp.dot(active[None, :], weight, preferred_element_type=jnp.float32)]
    broadcast_in_dim x15 -> x3, local copies, waits for them, and re-layouts: 47 us -> 0.74 us  [the longest x1 0.65 us: body(): result[:, split_at:][None]]
    unnamed x117 -> x26, local copies, waits for them, and re-layouts: 41 us -> 4.55 us
    pallas_call x0 -> x6, Pallas kernels: none -> 35.6 us  [the longest x2 16.2 us: qkv_call(): pl.pallas_call(lambda *refs: qkv_kernel(*refs, rows=rows, units=units, st...]
    all_to_all x0 -> x2, blocking collectives: none -> 26.2 us  [the longest x1 14.9 us: after_qkv(): recv = lax.all_to_all(sent, 'seq', 0, 0, tiled=True)]
    all_to_all x0 -> x2, waiting for transfers between devices: none -> 17.5 us  [the longest x1 11 us: after_qkv(): recv = lax.all_to_all(sent, 'seq', 0, 0, tiled=True)]
  transfers between devices with their start and end apart: 10 -> 11, of which waited for: 9 -> 9; matrix products, arithmetic and copies ran while one was open for 7% -> 4% of each run, Pallas kernels for 0% -> 0%
where the time goes in v1:
time: 150 us; the launch traced here: 149 us
  waiting for transfers between devices  38.2 us (25%)
  Pallas kernels  35.6 us (24%)
  starting transfers between devices  28.6 us (19%)
  blocking collectives  26.2 us (17%)
  local copies, waits for them, and re-layouts  10.6 us (7%)
  other arithmetic  7.84 us (5%)
  between operations  1.7 us (1%)
    ppermute x9, waiting for transfers between devices, swap(): return lax.ppermute(value, ('section', 'mp'), pairs)  20.7 us
    ppermute x9, starting transfers between devices, swap(): return lax.ppermute(value, ('section', 'mp'), pairs)  17.2 us
    pallas_call x2, Pallas kernels, qkv_call(): pl.pallas_call(lambda *refs: qkv_kernel(*refs, rows=rows, units=units, st...  16.2 us
    all_to_all x1, blocking collectives, after_qkv(): recv = lax.all_to_all(sent, 'seq', 0, 0, tiled=True)  14.9 us
    all_to_all x1, blocking collectives, after_qkv(): mixed = lax.all_to_all(attended, 'seq', 0, 0, tiled=True)  11.3 us
    all_to_all x1, waiting for transfers between devices, after_qkv(): recv = lax.all_to_all(sent, 'seq', 0, 0, tiled=True)  11 us
    pallas_call x2, Pallas kernels, attention_call(): pl.pallas_call(lambda *refs: attention_kernel(*refs, rows=rows, per_dev=p...  10.2 us
    pallas_call x2, Pallas kernels, out_call(): pl.pallas_call(lambda *refs: out_kernel(*refs, requests=requests), out_sh...  9.11 us
  transfers between devices with their start and end apart: 11, of which 9 were waited for; matrix products, arithmetic and copies ran while one was open for 4% of the time, Pallas kernels for 0%

profile of v1, /device:TPU:1, one launch (start us, length us, event | category | flops | bytes accessed | tf_op | source)
XLA Modules:
  0.0 149.1 jit_solution(8122490679466001737)
XLA Ops:
  0.6 0.0 copy-start
  1.6 0.8 copy-done
  2.3 0.4 fusion.10
  2.8 1.5 %collective-permute-start = (f32[1,2304]{1,0:T(1,128)S(1)}, f32[1,2304]{1,0:T(1,128)S(1)}, u32[]{:S(2)}, u32[]{:S(2)}) collective-permute-start(f32[1,2304]{1,0:T(1,128)S(1)} %get-tuple-element.9), channel_id=1, source_target_pairs={{0,1},{1,0},{2,3},{3,2},{64,65},{65,64},{66,67},{67,66},{4,5},{5,4... | collective-permute-start | bytes 27656 | tf_op jit(solution)/shard_map/ppermute | solution.py:33
  4.3 0.8 collective-permute-done
  5.1 1.4 collective-permute-start.1
  6.5 0.0 copy-done.7
  6.5 0.8 pad_maximum_fusion
  7.3 0.1 slice.33
  7.4 0.2 reshape.230
  7.6 0.7 copy.18
  8.3 0.0 collective-permute-done.1
  8.3 0.1 fusion.5
  8.4 0.6 select_n.126.refs_1_
  9.1 8.2 %qkv.2 = bf16[16,168,128]{2,1,0:T(8,128)(2,1)} custom-call(bf16[80,3072]{1,0:T(8,128)(2,1)} %bitcast.53, f32[3,3072]{1,0:T(4,128)} %select_n.126.refs_1_, bf16[3,3072,768]{2,1,0:T(8,128)(2,1)} %bitcast.49, bf16[12,48,128]{2,1,0:T(8,128)(2,1)} %bitcast.59), custom_call_target="tpu_custom_call" | custom-call | tf_op jit(solution)/shard_map/qkv/pallas_call | solution.py:105
  17.3 7.8 %all-to-all-start = ((bf16[16,168,128]{2,1,0:T(8,128)(2,1)}), bf16[16,168,128]{2,1,0:T(8,128)(2,1)S(1)}, u32[]{:S(2)}, u32[]{:S(2)}) async-start(bf16[16,168,128]{2,1,0:T(8,128)(2,1)} %qkv.2), calls=%async_computation | async-start | bytes 1376256 | tf_op jit(solution)/shard_map/all_to_all | solution.py:272
  25.1 0.0 copy-done.11
  25.1 0.1 copy.16
  25.2 0.1 pad_add_fusion
  25.3 0.5 fusion.9.refs_0_
  25.9 11.0 %all-to-all-done.refs_1_.refs_2_ = bf16[16,168,128]{2,1,0:T(8,128)(2,1)S(1)} async-done(((bf16[16,168,128]{2,1,0:T(8,128)(2,1)}), bf16[16,168,128]{2,1,0:T(8,128)(2,1)S(1)}, u32[]{:S(2)}, u32[]{:S(2)}) %all-to-all-start) | async-done | bytes 688160 | tf_op jit(solution)/shard_map/all_to_all | solution.py:272
  36.9 0.9 copy-done.1
  37.7 5.2 %attention.2 = bf16[16,40,128]{2,1,0:T(8,128)(2,1)} custom-call(s32[5]{0:T(128)} %fusion.9.refs_0_, bf16[16,168,128]{2,1,0:T(8,128)(2,1)} %copy-done.1, bf16[16,168,128]{2,1,0:T(8,128)(2,1)} %copy-done.1), custom_call_target="tpu_custom_call" | custom-call | tf_op jit(solution)/shard_map/attention/pallas_call | solution.py:176
  42.9 3.6 %all-to-all-start.1 = ((bf16[16,40,128]{2,1,0:T(8,128)(2,1)}), bf16[16,40,128]{2,1,0:T(8,128)(2,1)S(1)}, u32[]{:S(2)}, u32[]{:S(2)}) async-start(bf16[16,40,128]{2,1,0:T(8,128)(2,1)} %attention.2), calls=%async_computation.1 | async-start | bytes 327680 | tf_op jit(solution)/shard_map/all_to_all | solution.py:276
  46.5 0.6 broadcast_select_fusion.2.refs_1_
  47.1 6.5 %all-to-all-done.1.refs_0_ = bf16[16,40,128]{2,1,0:T(8,128)(2,1)S(1)} async-done(((bf16[16,40,128]{2,1,0:T(8,128)(2,1)}), bf16[16,40,128]{2,1,0:T(8,128)(2,1)S(1)}, u32[]{:S(2)}, u32[]{:S(2)}) %all-to-all-start.1) | async-done | bytes 163872 | tf_op jit(solution)/shard_map/all_to_all | solution.py:276
  53.6 0.7 copy-done.6
  54.2 4.5 %out_projection.2 = bf16[2,80,1536]{2,1,0:T(8,128)(2,1)} custom-call(bf16[16,40,128]{2,1,0:T(8,128)(2,1)} %copy-done.6, f32[1,3072]{1,0:T(1,128)} %broadcast_select_fusion.2.refs_1_, bf16[768,3072]{1,0:T(8,128)(2,1)} %bitcast.51), custom_call_target="tpu_custom_call" | custom-call | tf_op jit(solution)/shard_map/out_projection/pallas_call | solution.py:221
  58.8 1.0 dynamic-slice_bitcast_fusion.1
  59.7 3.5 %collective-permute-start.2 = (bf16[80,1536]{1,0:T(8,128)(2,1)S(1)}, bf16[80,1536]{1,0:T(8,128)(2,1)S(1)}, u32[]{:S(2)}, u32[]{:S(2)}) collective-permute-start(bf16[80,1536]{1,0:T(8,128)(2,1)S(1)} %dynamic-slice_bitcast_fusion.1), channel_id=1, source_target_pairs={{0,1},{1,0},{2,3},{3,2},{64,65},{65,64},{66,67},{67,66},{4,5},{5,4... | collective-permute-start | bytes 737288 | tf_op jit(solution)/shard_map/ppermute | solution.py:33
  63.2 1.1 collective-permute-done.2
  64.4 1.0 fusion.3
  65.4 0.9 collective-permute-start.3
  66.2 6.4 %collective-permute-done.3 = bf16[80,1536]{1,0:T(8,128)(2,1)S(1)} collective-permute-done((bf16[80,1536]{1,0:T(8,128)(2,1)S(1)}, bf16[80,1536]{1,0:T(8,128)(2,1)S(1)}, u32[]{:S(2)}, u32[]{:S(2)}) %collective-permute-start.3) | collective-permute-done | bytes 245792 | tf_op jit(solution)/shard_map/ppermute | solution.py:33
  72.6 0.1 add_convert_fusion.1
  72.7 0.0 copy-start.5
  72.7 0.7 copy-done.5
  73.4 4.0 %collective-permute-start.4 = (bf16[80,1536]{1,0:T(8,128)(2,1)S(1)}, bf16[80,1536]{1,0:T(8,128)(2,1)S(1)}, u32[]{:S(2)}, u32[]{:S(2)}) collective-permute-start(bf16[80,1536]{1,0:T(8,128)(2,1)S(1)} %add_convert_fusion.1), channel_id=1, source_target_pairs={{0,66},{1,67},{2,64},{3,65},{4,70},{5,71},{6,68},{7,69},{8,74},{9,... | collective-permute-start | bytes 737288 | tf_op jit(solution)/shard_map/ppermute | solution.py:33
  77.4 4.0 %collective-permute-done.4 = bf16[80,1536]{1,0:T(8,128)(2,1)S(1)} collective-permute-done((bf16[80,1536]{1,0:T(8,128)(2,1)S(1)}, bf16[80,1536]{1,0:T(8,128)(2,1)S(1)}, u32[]{:S(2)}, u32[]{:S(2)}) %collective-permute-start.4) | collective-permute-done | bytes 245792 | tf_op jit(solution)/shard_map/ppermute | solution.py:33
  81.4 2.1 %collective-permute-start.5 = (bf16[80,1536]{1,0:T(8,128)(2,1)S(1)}, bf16[80,1536]{1,0:T(8,128)(2,1)S(1)}, u32[]{:S(2)}, u32[]{:S(2)}) collective-permute-start(bf16[80,1536]{1,0:T(8,128)(2,1)S(1)} %collective-permute-done.4), channel_id=1, source_target_pairs={{0,1},{1,0},{2,3},{3,2},{64,65},{65,64},{66,67},{67,66},{4,5},{5,4... | collective-permute-start | bytes 737288 | tf_op jit(solution)/shard_map/ppermute | solution.py:33
  83.5 1.1 collective-permute-done.5
  84.7 0.9 maximum_select_fusion.refs_0_
  85.5 8.0 %qkv.3 = bf16[16,120,128]{2,1,0:T(8,128)(2,1)} custom-call(bf16[80,3072]{1,0:T(8,128)(2,1)} %maximum_select_fusion.refs_0_, f32[3,3072]{1,0:T(4,128)} %select_n.126.refs_1_, bf16[3,3072,768]{2,1,0:T(8,128)(2,1)} %bitcast.50), custom_call_target="tpu_custom_call" | custom-call | tf_op jit(solution)/shard_map/qkv/pallas_call | solution.py:105
  93.6 14.9 %all_to_all.20.refs_1_ = bf16[16,120,128]{2,1,0:T(8,128)(2,1)} all-to-all(bf16[16,120,128]{2,1,0:T(8,128)(2,1)} %qkv.3), channel_id=1, replica_groups=mesh['section'=2,'seq'=16,'mp'=4] {'seq'}, dimensions={0} | all-to-all | bytes 983040 | tf_op jit(solution)/shard_map/all_to_all | solution.py:272
  108.5 5.1 %attention.3 = bf16[16,40,128]{2,1,0:T(8,128)(2,1)} custom-call(s32[5]{0:T(128)} %fusion.9.refs_0_, bf16[16,120,128]{2,1,0:T(8,128)(2,1)} %all_to_all.20.refs_1_, bf16[16,168,128]{2,1,0:T(8,128)(2,1)} %copy-done.1), custom_call_target="tpu_custom_call" | custom-call | tf_op jit(solution)/shard_map/attention/pallas_call | solution.py:176
  113.5 11.3 %all_to_all.21.refs_0_ = bf16[16,40,128]{2,1,0:T(8,128)(2,1)} all-to-all(bf16[16,40,128]{2,1,0:T(8,128)(2,1)} %attention.3), channel_id=1, replica_groups=mesh['section'=2,'seq'=16,'mp'=4] {'seq'}, dimensions={0} | all-to-all | bytes 327680 | tf_op jit(solution)/shard_map/all_to_all | solution.py:276
  124.8 4.6 %out_projection.3 = bf16[2,80,1536]{2,1,0:T(8,128)(2,1)} custom-call(bf16[16,40,128]{2,1,0:T(8,128)(2,1)} %all_to_all.21.refs_0_, f32[1,3072]{1,0:T(1,128)} %broadcast_select_fusion.2.refs_1_, bf16[768,3072]{1,0:T(8,128)(2,1)} %bitcast.52), custom_call_target="tpu_custom_call" | custom-call | tf_op jit(solution)/shard_map/out_projection/pallas_call | solution.py:221
  129.4 1.0 dynamic-slice_bitcast_fusion
  130.4 2.6 %collective-permute-start.6 = (bf16[80,1536]{1,0:T(8,128)(2,1)S(1)}, bf16[80,1536]{1,0:T(8,128)(2,1)S(1)}, u32[]{:S(2)}, u32[]{:S(2)}) collective-permute-start(bf16[80,1536]{1,0:T(8,128)(2,1)S(1)} %dynamic-slice_bitcast_fusion), channel_id=1, source_target_pairs={{0,1},{1,0},{2,3},{3,2},{64,65},{65,64},{66,67},{67,66},{4,5},{5,4... | collective-permute-start | bytes 737288 | tf_op jit(solution)/shard_map/ppermute | solution.py:33
  133.1 1.1 collective-permute-done.6
  134.2 1.7 %fusion.2 = bf16[80,1536]{1,0:T(8,128)(2,1)} fusion(bf16[80,1536]{1,0:T(8,128)(2,1)S(1)} %collective-permute-done.6, bf16[2,80,1536]{2,1,0:T(8,128)(2,1)} %out_projection.3, s32[]{:T(128)S(6)} %select_n.130), kind=kLoop, calls=%fused_computation.6 | loop fusion | flops 491520 | bytes 737284 | tf_op jit(solution)/shard_map/convert_element_type | solution.py:280
  135.9 0.1 collective-permute-start.7
  136.0 1.0 slice_select_fusion
  137.0 0.1 copy.23
  137.1 0.3 reshape.234
  137.4 6.0 %collective-permute-done.7 = bf16[80,1536]{1,0:T(8,128)(2,1)} collective-permute-done((bf16[80,1536]{1,0:T(8,128)(2,1)}, bf16[80,1536]{1,0:T(8,128)(2,1)}, u32[]{:S(2)}, u32[]{:S(2)}) %collective-permute-start.7) | collective-permute-done | bytes 245792 | tf_op jit(solution)/shard_map/ppermute | solution.py:33
  143.4 1.3 fusion.4
  144.7 1.3 collective-permute-start.8
  146.0 0.9 copy.20
  146.9 0.7 copy.21
  147.6 0.0 collective-permute-done.8
  147.6 0.1 maximum_select_fusion.1
  147.7 0.8 slice_bitcast_fusion
  148.5 0.6 slice_bitcast_fusion.2
  (26 shorter events, 0.2 us)
Async XLA Ops:
  0.6 1.7 %copy-start = (bf16[1,512,2304]{2,1,0:T(8,128)(2,1)S(1)}, bf16[1,512,2304]{2,1,0:T(8,128)(2,1)}, u32[]{:S(2)}) copy-start(bf16[1,512,2304]{2,1,0:T(8,128)(2,1)} %param.14) | copy-start | bytes 7077892
  0.6 5.8 %copy-start.7 = (bf16[2,4,8,3072]{3,2,1,0:T(8,128)(2,1)S(1)}, bf16[2,4,8,3072]{3,2,1,0:T(8,128)(2,1)}, u32[]{:S(2)}) copy-start(bf16[2,4,8,3072]{3,2,1,0:T(8,128)(2,1)} %param.9) | copy-start | bytes 1179652
  0.7 5.8 %copy-start.9 = (bf16[2,8,3072]{2,1,0:T(8,128)(2,1)S(1)}, bf16[2,8,3072]{2,1,0:T(8,128)(2,1)}, u32[]{:S(2)}) copy-start(bf16[2,8,3072]{2,1,0:T(8,128)(2,1)} %param.10) | copy-start | bytes 294916
  0.7 6.6 %copy-start.8 = (bf16[1,2,4,8,2,768]{5,4,3,2,1,0:T(2,128)(2,1)S(1)}, bf16[1,2,4,8,2,768]{5,4,3,2,1,0:T(2,128)(2,1)}, u32[]{:S(2)}) copy-start(bf16[1,2,4,8,2,768]{5,4,3,2,1,0:T(2,128)(2,1)} %param.17) | copy-start | bytes 589828
  2.8 2.3 %collective-permute-start = (f32[1,2304]{1,0:T(1,128)S(1)}, f32[1,2304]{1,0:T(1,128)S(1)}, u32[]{:S(2)}, u32[]{:S(2)}) collective-permute-start(f32[1,2304]{1,0:T(1,128)S(1)} %get-tuple-element.9), channel_id=1, source_target_pairs={{0,1},{1,0},{2,3},{3,2},{64,65},{65,64},{66,67},{67,66},{4,5},{5,4... | collective-permute-start | bytes 27656 | tf_op jit(solution)/shard_map/ppermute | solution.py:33
  5.1 3.2 %collective-permute-start.1 = (f32[1,4608]{1,0:T(1,128)S(1)}, f32[1,4608]{1,0:T(1,128)S(1)}, u32[]{:S(2)}, u32[]{:S(2)}) collective-permute-start(f32[1,4608]{1,0:T(1,128)S(1)} %broadcast_select_fusion.1), channel_id=1, source_target_pairs={{0,2},{1,3},{2,0},{3,1},{64,66},{65,67},{66,64},{67,65},{4,6},{5,7... | collective-permute-start | bytes 55304 | tf_op jit(solution)/shard_map/ppermute | solution.py:33
  9.0 16.0 %copy-start.11 = (s32[2]{0:T(128)S(1)}, s32[2]{0:T(128)}, u32[]{:S(2)}) copy-start(s32[2]{0:T(128)} %param.12) | copy-start | bytes 28
  9.1 16.1 %copy-start.10 = (s32[2,4]{1,0:T(2,128)S(1)}, s32[2,4]{1,0:T(2,128)}, u32[]{:S(2)}) copy-start(s32[2,4]{1,0:T(2,128)} %param.11) | copy-start | bytes 100
  17.3 19.6 %all-to-all-start = ((bf16[16,168,128]{2,1,0:T(8,128)(2,1)}), bf16[16,168,128]{2,1,0:T(8,128)(2,1)S(1)}, u32[]{:S(2)}, u32[]{:S(2)}) async-start(bf16[16,168,128]{2,1,0:T(8,128)(2,1)} %qkv.2), calls=%async_computation | async-start | bytes 1376256 | tf_op jit(solution)/shard_map/all_to_all | solution.py:272
  36.9 0.9 copy-start.1
  42.9 10.7 %all-to-all-start.1 = ((bf16[16,40,128]{2,1,0:T(8,128)(2,1)}), bf16[16,40,128]{2,1,0:T(8,128)(2,1)S(1)}, u32[]{:S(2)}, u32[]{:S(2)}) async-start(bf16[16,40,128]{2,1,0:T(8,128)(2,1)} %attention.2), calls=%async_computation.1 | async-start | bytes 327680 | tf_op jit(solution)/shard_map/all_to_all | solution.py:276
  53.6 0.7 copy-start.6
  54.2 18.4 %copy-start.4 = (bf16[2,40,3072]{2,1,0:T(8,128)(2,1)S(1)}, bf16[2,40,3072]{2,1,0:T(8,128)(2,1)}, u32[]{:S(2)}) copy-start(bf16[2,40,3072]{2,1,0:T(8,128)(2,1)} %pad_maximum_fusion) | copy-start | bytes 1474564
  59.7 4.6 %collective-permute-start.2 = (bf16[80,1536]{1,0:T(8,128)(2,1)S(1)}, bf16[80,1536]{1,0:T(8,128)(2,1)S(1)}, u32[]{:S(2)}, u32[]{:S(2)}) collective-permute-start(bf16[80,1536]{1,0:T(8,128)(2,1)S(1)} %dynamic-slice_bitcast_fusion.1), channel_id=1, source_target_pairs={{0,1},{1,0},{2,3},{3,2},{64,65},{65,64},{66,67},{67,66},{4,5},{5,4... | collective-permute-start | bytes 737288 | tf_op jit(solution)/shard_map/ppermute | solution.py:33
  65.4 7.2 %collective-permute-start.3 = (bf16[80,1536]{1,0:T(8,128)(2,1)S(1)}, bf16[80,1536]{1,0:T(8,128)(2,1)S(1)}, u32[]{:S(2)}, u32[]{:S(2)}) collective-permute-start(bf16[80,1536]{1,0:T(8,128)(2,1)S(1)} %fusion.3), channel_id=1, source_target_pairs={{0,2},{1,3},{2,0},{3,1},{64,66},{65,67},{66,64},{67,65},{4,6},{5,7... | collective-permute-start | bytes 737288 | tf_op jit(solution)/shard_map/ppermute | solution.py:33
  72.7 0.7 copy-start.5
  73.4 8.0 %collective-permute-start.4 = (bf16[80,1536]{1,0:T(8,128)(2,1)S(1)}, bf16[80,1536]{1,0:T(8,128)(2,1)S(1)}, u32[]{:S(2)}, u32[]{:S(2)}) collective-permute-start(bf16[80,1536]{1,0:T(8,128)(2,1)S(1)} %add_convert_fusion.1), channel_id=1, source_target_pairs={{0,66},{1,67},{2,64},{3,65},{4,70},{5,71},{6,68},{7,69},{8,74},{9,... | collective-permute-start | bytes 737288 | tf_op jit(solution)/shard_map/ppermute | solution.py:33
  81.4 3.3 %collective-permute-start.5 = (bf16[80,1536]{1,0:T(8,128)(2,1)S(1)}, bf16[80,1536]{1,0:T(8,128)(2,1)S(1)}, u32[]{:S(2)}, u32[]{:S(2)}) collective-permute-start(bf16[80,1536]{1,0:T(8,128)(2,1)S(1)} %collective-permute-done.4), channel_id=1, source_target_pairs={{0,1},{1,0},{2,3},{3,2},{64,65},{65,64},{66,67},{67,66},{4,5},{5,4... | collective-permute-start | bytes 737288 | tf_op jit(solution)/shard_map/ppermute | solution.py:33
  124.8 11.2 %copy-start.3 = (bf16[16,120,128]{2,1,0:T(8,128)(2,1)S(1)}, bf16[16,120,128]{2,1,0:T(8,128)(2,1)}, u32[]{:S(2)}) copy-start(bf16[16,120,128]{2,1,0:T(8,128)(2,1)} %qkv.3) | copy-start | bytes 1474564
  129.4 14.0 %copy-start.2 = (bf16[80,3072]{1,0:T(8,128)(2,1)S(1)}, bf16[80,3072]{1,0:T(8,128)(2,1)}, u32[]{:S(2)}) copy-start(bf16[80,3072]{1,0:T(8,128)(2,1)} %maximum_select_fusion.refs_0_) | copy-start | bytes 1474564
  130.4 3.8 %collective-permute-start.6 = (bf16[80,1536]{1,0:T(8,128)(2,1)S(1)}, bf16[80,1536]{1,0:T(8,128)(2,1)S(1)}, u32[]{:S(2)}, u32[]{:S(2)}) collective-permute-start(bf16[80,1536]{1,0:T(8,128)(2,1)S(1)} %dynamic-slice_bitcast_fusion), channel_id=1, source_target_pairs={{0,1},{1,0},{2,3},{3,2},{64,65},{65,64},{66,67},{67,66},{4,5},{5,4... | collective-permute-start | bytes 737288 | tf_op jit(solution)/shard_map/ppermute | solution.py:33
  135.9 7.5 %collective-permute-start.7 = (bf16[80,1536]{1,0:T(8,128)(2,1)}, bf16[80,1536]{1,0:T(8,128)(2,1)}, u32[]{:S(2)}, u32[]{:S(2)}) collective-permute-start(bf16[80,1536]{1,0:T(8,128)(2,1)} %fusion.2), channel_id=1, source_target_pairs={{0,2},{1,3},{2,0},{3,1},{64,66},{65,67},{66,64},{67,65},{4,6},{5,7... | collective-permute-start | bytes 737288 | tf_op jit(solution)/shard_map/ppermute | solution.py:33
  144.7 2.8 %collective-permute-start.8 = (bf16[80,1536]{1,0:T(8,128)(2,1)S(1)}, bf16[80,1536]{1,0:T(8,128)(2,1)S(1)}, u32[]{:S(2)}, u32[]{:S(2)}) collective-permute-start(bf16[80,1536]{1,0:T(8,128)(2,1)S(1)} %fusion.4), channel_id=1, source_target_pairs={{0,1},{1,0},{2,3},{3,2},{64,65},{65,64},{66,67},{67,66},{4,5},{5,4... | collective-permute-start | bytes 737288 | tf_op jit(solution)/shard_map/ppermute | solution.py:33

commit v2 on v1

v2 whole, which is shorter than its diff:
```python
import math

import jax
import jax.numpy as jnp
from jax import lax
from jax.experimental import pallas as pl
from jax.experimental.pallas import tpu as pltpu
from jax.sharding import PartitionSpec as P

HEAD = 64
LANES = 128
EPS = 1e-05
NEG = -1e30
VMEM_LIMIT = 12 * 1024 * 1024


def modulation(timestep, weight):
    half_width = weight.shape[0] // 2
    frequency = jnp.exp(-math.log(10000.0) * jnp.arange(half_width, dtype=jnp.float32) / half_width)
    phases = timestep.astype(jnp.float32)[0] * frequency
    embedding = jnp.concatenate([jnp.cos(phases), jnp.sin(phases)])
    active = jax.nn.silu(embedding).astype(jnp.bfloat16)
    return jnp.dot(active[None, :], weight, preferred_element_type=jnp.float32)


def swap(value, mapping):
    pairs = []
    for section in range(2):
        for part in range(4):
            target = mapping(section, part)
            if target is not None:
                pairs.append((section * 4 + part, target[0] * 4 + target[1]))
    return lax.ppermute(value, ("section", "mp"), pairs)


def swap_core(value):
    return swap(value, lambda section, part: (section, part ^ 1))


def swap_chip(value):
    return swap(value, lambda section, part: (section, part ^ 2))


def next_section(value):
    return swap(value, lambda section, part: (1, part ^ 2) if section == 0 else None)

VMEM = pl.BlockSpec(memory_space=pltpu.VMEM)
SMEM = pl.BlockSpec(memory_space=pltpu.SMEM)
ANY = pl.BlockSpec(memory_space=pl.ANY)
PARAMS = pltpu.CompilerParams(vmem_limit_bytes=VMEM_LIMIT)


def centered(values):
    values = values.astype(jnp.float32)
    center = values - jnp.mean(values, axis=-1, keepdims=True)
    spread = jnp.mean(center * center, axis=-1, keepdims=True)
    return center * lax.rsqrt(spread + EPS)


def prepare_kernel(
    video_ref, text_ref, w_ref, stale_ref, half_ref, unit_ref, packed_ref, w_vmem, video_buf, text_buf, stale_buf, x_ref, sems
):
    requests, patches, per_dev, width = video_ref.shape
    first = [
        pltpu.make_async_copy(stale_ref, stale_buf, sems.at[0]),
        pltpu.make_async_copy(video_ref, video_buf, sems.at[1]),
        pltpu.make_async_copy(text_ref, text_buf, sems.at[2]),
    ]
    loads = [
        pltpu.make_async_copy(w_ref.at[part], w_vmem.at[part], sems.at[3 + part]) for part in range(w_ref.shape[0])
    ]
    for copy in first + loads:
        copy.start()
    first[0].wait()
    blocks = w_ref.shape[2] // LANES
    for request in range(requests):
        for patch in range(1, patches):
            both = stale_buf[request, patch]
            for kind in range(2):
                values = both[:, kind, :]
                row = (kind * (patches - 1) + patch - 1) * per_dev
                for block in range(blocks):
                    packed_ref[request * blocks + block, row : row + per_dev, :] = values[
                        :, block * LANES : (block + 1) * LANES
                    ]
    for copy in first[1:]:
        copy.wait()
    row = 0
    for request in range(requests):
        for patch in range(patches + 1):
            values = video_buf[request, patch] if patch < patches else text_buf[request]
            x_ref[row : row + per_dev, :] = values
            unit_ref[row : row + per_dev, :] = centered(values)
            row += per_dev
    half = width // 2
    core = lax.axis_index("mp") % 2
    half_ref[...] = x_ref[:, pl.ds(pl.multiple_of(core * half, LANES), half)]
    for copy in loads:
        copy.wait()


def prepare_call(video, text, weight, stale):
    requests, patches, per_dev, width = video.shape
    total = requests * (patches + 1) * per_dev
    units = requests * (weight.shape[2] // LANES)
    operands = [pltpu.with_memory_space_constraint(value, pltpu.HBM) for value in (video, text, weight, stale)]
    return pl.pallas_call(
        prepare_kernel,
        out_shape=(
            pltpu.VMEM((total, width // 2), jnp.bfloat16),
            pltpu.VMEM((total, width), jnp.float32),
            pltpu.VMEM((units, 2 * (patches - 1) * per_dev, LANES), jnp.bfloat16),
            pltpu.VMEM(weight.shape, jnp.bfloat16),
        ),
        in_specs=[ANY] * 4,
        out_specs=(VMEM,) * 4,
        scratch_shapes=[
            pltpu.VMEM(video.shape, jnp.bfloat16),
            pltpu.VMEM(text.shape, jnp.bfloat16),
            pltpu.VMEM(stale.shape, jnp.bfloat16),
            pltpu.VMEM((total, width), jnp.bfloat16),
            pltpu.SemaphoreType.DMA((3 + weight.shape[0],)),
        ],
        compiler_params=PARAMS,
        name="prepare",
    )(*operands)


def project(normed_ref, w_ref, o_ref, kv_ref, rows):
    parts, _, columns = w_ref.shape
    blocks = columns // LANES
    requests = normed_ref.shape[0] // rows
    for unit in range(requests * blocks, o_ref.shape[0]):
        o_ref[unit] = jnp.zeros(o_ref.shape[1:], o_ref.dtype)
    for part in range(parts):
        acc = jnp.dot(normed_ref[...], w_ref[part], preferred_element_type=jnp.float32)
        if part:
            kv_ref[part - 1] = acc.astype(jnp.bfloat16)
        for request in range(requests):
            for block in range(blocks):
                o_ref[request * blocks + block, part * rows : (part + 1) * rows, :] = acc[
                    request * rows : (request + 1) * rows, block * LANES : (block + 1) * LANES
                ].astype(jnp.bfloat16)


def first_kernel(
    unit_ref, mod_0, mod_1, mod_2, mod_3, w_ref, stale_ref, o_ref, kv_ref, mod_ref, pieces_ref, normed_ref, *, rows
):
    for index, piece in enumerate((mod_0, mod_1, mod_2, mod_3)):
        pieces_ref[lax.axis_index("mp") ^ index, 0:1, :] = piece[...]
    total, width = unit_ref.shape
    piece_width = mod_0.shape[1]
    for line in range(3):
        start = line * width
        while start < (line + 1) * width:
            slot, at = divmod(start, piece_width)
            count = min(piece_width - at, (line + 1) * width - start)
            to = start - line * width
            mod_ref[line : line + 1, to : to + count] = pieces_ref[slot, 0:1, at : at + count]
            start += count
    step = 16
    for start in range(0, total, step):
        normed = unit_ref[start : start + step, :] * (1.0 + mod_ref[1:2, :]) + mod_ref[0:1, :]
        normed_ref[start : start + step, :] = normed.astype(jnp.bfloat16)
    for unit in range(stale_ref.shape[0]):
        o_ref[unit, 3 * rows :, :] = stale_ref[unit]
    project(normed_ref, w_ref, o_ref, kv_ref, rows)


def first_call(unit, mods, weight, stale, rows, devices):
    total, width = unit.shape
    return pl.pallas_call(
        lambda *refs: first_kernel(*refs, rows=rows),
        out_shape=(
            jax.ShapeDtypeStruct((devices, 3 * rows + stale.shape[1], LANES), jnp.bfloat16),
            jax.ShapeDtypeStruct((2, total, weight.shape[2]), jnp.bfloat16),
            pltpu.VMEM((3, width), jnp.float32),
        ),
        in_specs=[VMEM] * 7,
        out_specs=(VMEM,) * 3,
        scratch_shapes=[
            pltpu.VMEM((4, 8, mods[0].shape[1]), jnp.float32),
            pltpu.VMEM((total, width), jnp.bfloat16),
        ],
        compiler_params=PARAMS,
        name="first_qkv",
    )(unit, *mods, weight, stale)


def second_kernel(mine_ref, other_ref, mod_ref, w_ref, o_ref, kv_ref, x_ref, normed_ref, *, rows):
    total, half = mine_ref.shape
    core = lax.axis_index("mp") % 2
    x_ref[:, pl.ds(pl.multiple_of(core * half, LANES), half)] = mine_ref[...]
    x_ref[:, pl.ds(pl.multiple_of((1 - core) * half, LANES), half)] = other_ref[...]
    step = 16
    for start in range(0, total, step):
        normed = centered(x_ref[start : start + step, :]) * (1.0 + mod_ref[1:2, :]) + mod_ref[0:1, :]
        normed_ref[start : start + step, :] = normed.astype(jnp.bfloat16)
    project(normed_ref, w_ref, o_ref, kv_ref, rows)


def second_call(mine, other, mod, weight, rows, devices):
    total, half = mine.shape
    return pl.pallas_call(
        lambda *refs: second_kernel(*refs, rows=rows),
        out_shape=(
            jax.ShapeDtypeStruct((devices, 3 * rows, LANES), jnp.bfloat16),
            jax.ShapeDtypeStruct((2, total, weight.shape[2]), jnp.bfloat16),
        ),
        in_specs=[VMEM] * 4,
        out_specs=(VMEM, VMEM),
        scratch_shapes=[pltpu.VMEM((total, 2 * half), jnp.bfloat16)] * 2,
        compiler_params=PARAMS,
        name="second_qkv",
    )(mine, other, mod, weight)


def attention_kernel(*refs, rows, per_dev, patches, blocks):
    if len(refs) == 8:
        lens_ref, text_ref, recv_ref, stale_ref, w_ref, o_ref, w_vmem, sem = refs
        copy = pltpu.make_async_copy(w_ref, w_vmem, sem)
        copy.start()
    else:
        lens_ref, text_ref, recv_ref, stale_ref, o_ref = refs
        copy = None
    devices = recv_ref.shape[0]
    capacity = devices * per_dev

    def block(ref, base, index):
        start = base + index * per_dev
        return ref[:, start : start + per_dev, :].reshape(capacity, LANES)

    groups = patches + 1
    fresh_k = [block(recv_ref, rows, index) for index in range(groups)]
    fresh_v = [block(recv_ref, 2 * rows, index) for index in range(groups)]
    stale_base = 3 * rows
    stale_k = [None] + [block(stale_ref, stale_base, index) for index in range(patches - 1)]
    stale_base += (patches - 1) * per_dev
    stale_v = [None] + [block(stale_ref, stale_base, index) for index in range(patches - 1)]
    slot = lax.broadcasted_iota(jnp.int32, (1, groups * capacity), 1)
    limit = jnp.zeros((1, groups * capacity), jnp.int32)
    request = jnp.minimum(lax.axis_index("seq") // blocks, lens_ref.shape[0] - 1)
    for index in range(groups):
        length = lens_ref[request, index] if index < patches else text_ref[request]
        limit = jnp.where(slot >= index * capacity, length + index * capacity, limit)
    bias = jnp.where(slot < limit, 0.0, NEG)
    lane = lax.broadcasted_iota(jnp.int32, (1, LANES), 1)
    factor = HEAD ** (-0.5) * math.log2(math.e)
    for patch in range(patches):
        keys = jnp.concatenate(
            [fresh_k[i] if i <= patch else stale_k[i] for i in range(patches)] + [fresh_k[patches]], axis=0
        )
        values = jnp.concatenate(
            [fresh_v[i] if i <= patch else stale_v[i] for i in range(patches)] + [fresh_v[patches]], axis=0
        )
        for group in [patch, patches] if patch == 0 else [patch]:
            queries = block(recv_ref, 0, group)
            outs = []
            for head in range(2):
                mine = (lane < HEAD) if head == 0 else (lane >= HEAD)
                scores = lax.dot_general(
                    jnp.where(mine, queries, jnp.zeros_like(queries)),
                    keys,
                    (((1,), (1,)), ((), ())),
                    preferred_element_type=jnp.float32,
                )
                scores = scores + bias
                top = jnp.max(scores, axis=-1, keepdims=True)
                weights = jnp.exp2((scores - top) * factor)
                weight_sum = jnp.sum(weights, axis=-1, keepdims=True)
                acc = jnp.dot(
                    weights.astype(jnp.bfloat16), values, preferred_element_type=jnp.float32
                )
                outs.append(acc / weight_sum)
            out = jnp.where(lane < HEAD, outs[0], outs[1]).astype(jnp.bfloat16)
            start = group * per_dev
            o_ref[:, start : start + per_dev, :] = out.reshape(devices, per_dev, LANES)
    if copy is not None:
        copy.wait()


def attention_call(lens, text_len, recv, stale, weight, rows, per_dev, blocks):
    devices = recv.shape[0]
    outs = jax.ShapeDtypeStruct((devices, rows, LANES), jnp.bfloat16)
    loads = weight is not None
    return pl.pallas_call(
        lambda *refs: attention_kernel(*refs, rows=rows, per_dev=per_dev, patches=lens.shape[1], blocks=blocks),
        out_shape=(outs, pltpu.VMEM(weight.shape, weight.dtype)) if loads else outs,
        in_specs=[SMEM, SMEM, VMEM, VMEM] + ([ANY] if loads else []),
        out_specs=(VMEM, VMEM) if loads else VMEM,
        scratch_shapes=[pltpu.SemaphoreType.DMA] if loads else [],
        compiler_params=PARAMS,
        name="attention",
    )(lens, text_len, recv, stale, *([pltpu.with_memory_space_constraint(weight, pltpu.HBM)] if loads else []))


def out_kernel(recv_ref, mod_ref, w_ref, other_ref, mine_ref, mixed_ref):
    depth, width = w_ref.shape
    rows = recv_ref.shape[1]
    blocks = depth // LANES
    for request in range(mixed_ref.shape[0] // rows):
        for block in range(blocks):
            mixed_ref[request * rows : (request + 1) * rows, block * LANES : (block + 1) * LANES] = recv_ref[
                request * blocks + block
            ]
    half = width // 2
    core = lax.axis_index("mp") % 2
    for ref, index in ((other_ref, 1 - core), (mine_ref, core)):
        at = pl.ds(pl.multiple_of(index * half, LANES), half)
        acc = jnp.dot(mixed_ref[...], w_ref[:, at], preferred_element_type=jnp.float32)
        ref[...] = (acc * mod_ref[2:3, at]).astype(ref.dtype)


def out_call(recv, mod, weight, requests):
    depth, width = weight.shape
    total = requests * recv.shape[1]
    return pl.pallas_call(
        out_kernel,
        out_shape=(
            pltpu.VMEM((total, width // 2), jnp.bfloat16),
            pltpu.VMEM((total, width // 2), jnp.float32),
        ),
        in_specs=[VMEM, VMEM, VMEM],
        out_specs=(VMEM, VMEM),
        scratch_shapes=[pltpu.VMEM((total, depth), jnp.bfloat16)],
        compiler_params=PARAMS,
        name="out_projection",
    )(recv, mod, weight)


def store_kernel(mine_ref, other_ref, video_ref, text_ref, sems):
    _, requests, patches, per_dev, _ = video_ref.shape
    half = mine_ref.shape[1]
    core = lax.axis_index("mp") % 2
    copies = []
    for side, (source, index) in enumerate(((mine_ref, core), (other_ref, 1 - core))):
        at = pl.ds(pl.multiple_of(index * half, LANES), half)
        row = 0
        for request in range(requests):
            for patch in range(patches + 1):
                target = (
                    video_ref.at[0, request, patch, :, at]
                    if patch < patches
                    else text_ref.at[0, request, :, at]
                )
                copy = pltpu.make_async_copy(
                    source.at[pl.ds(row, per_dev), :], target, sems.at[side, row // per_dev]
                )
                copy.start()
                copies.append(copy)
                row += per_dev
    for copy in copies:
        copy.wait()


def store_call(mine, other, video_shape, text_shape):
    return pl.pallas_call(
        store_kernel,
        out_shape=(
            jax.ShapeDtypeStruct(video_shape, jnp.bfloat16),
            jax.ShapeDtypeStruct(text_shape, jnp.bfloat16),
        ),
        in_specs=[VMEM, VMEM],
        out_specs=(ANY, ANY),
        scratch_shapes=[pltpu.SemaphoreType.DMA((2, mine.shape[0] // video_shape[3]))],
        compiler_params=PARAMS,
        name="store",
    )(mine, other)


def body(video, text, patch_lengths, text_len, timestep, w_mod, w_qkv, w_out, stale_cache):
    devices = lax.axis_size("seq")
    requests, patches, per_dev, _ = video.shape
    columns = w_out.shape[1]
    blocks = columns // LANES
    rows = patches * per_dev + text.shape[1]

    timestep, is_first = lax.optimization_barrier((timestep, lax.axis_index("section") == 0))
    own_mod = modulation(timestep, w_mod[0])
    mods = [own_mod] + [
        swap(own_mod, lambda section, part, flip=flip: (section, part ^ flip)) for flip in (1, 2, 3)
    ]
    x_half, unit, stale, weight_qkv = prepare_call(video, text, w_qkv[0].transpose(1, 0, 2), stale_cache[0])

    def reduced(mixed, weight_out, mod):
        other, mine = out_call(mixed, mod, weight_out, requests)
        return (mine + swap_core(other).astype(jnp.float32)).astype(jnp.bfloat16)

    def added(x_half, on_chip, arrived):
        total = x_half.astype(jnp.float32) + (on_chip.astype(jnp.float32) + arrived.astype(jnp.float32))
        return total.astype(jnp.bfloat16)

    sent_0, kv_0, mod = first_call(unit, mods, weight_qkv, stale, rows, devices)
    recv_0 = lax.all_to_all(sent_0, "seq", 0, 0, tiled=True)
    attended, weight_out = attention_call(
        patch_lengths, text_len, recv_0, recv_0, w_out[0], rows, per_dev, blocks
    )
    on_chip = reduced(lax.all_to_all(attended, "seq", 0, 0, tiled=True), weight_out, mod)
    result_0 = added(x_half, on_chip, swap_chip(on_chip))

    x_half = next_section(result_0)
    sent_1, kv_1 = second_call(x_half, swap_core(x_half), mod, weight_qkv, rows, devices)
    recv_1 = lax.all_to_all(sent_1, "seq", 0, 0, tiled=True)
    attended = attention_call(patch_lengths, text_len, recv_1, recv_0, None, rows, per_dev, blocks)
    on_chip = reduced(lax.all_to_all(attended, "seq", 0, 0, tiled=True), weight_out, mod)
    arrived = swap_chip(on_chip)

    key_value = jnp.where(is_first, kv_0, kv_1).reshape(2, requests, rows, columns).transpose(1, 2, 0, 3)
    split_at = patches * per_dev
    cache_video = key_value[:, :split_at].reshape(1, requests, patches, per_dev, 2, columns)
    cache_text = key_value[:, split_at:][None]
    arrived, cache_video, cache_text = lax.optimization_barrier((arrived, cache_video, cache_text))

    result = jnp.where(is_first, result_0, added(x_half, on_chip, arrived))
    hidden_video, hidden_text = store_call(result, swap_core(result), (1,) + video.shape, (1,) + text.shape)
    return (hidden_video, hidden_text, cache_video, cache_text)


def solution(mesh):
    placed = (
        P(None, None, "seq", None),
        P(None, "seq", None),
        P(),
        P(),
        P(),
        P("section", None, "mp"),
        P("section", None, None, "mp"),
        P("section", "mp", None),
        P("section", None, None, "seq", None, "mp"),
    )
    return jax.shard_map(
        body,
        mesh=mesh,
        in_specs=placed,
        out_specs=(
            P("section", None, None, "seq", None),
            P("section", None, "seq", None),
            P("section", None, None, "seq", None, "mp"),
            P("section", None, "seq", None, "mp"),
        ),
        check_vma=False,
    )
```

time: 150 us -> 121 us (0.81)
  blocking collectives: 26.2 us -> 54.1 us
  waiting for transfers between devices: 38.2 us -> 20.3 us
  Pallas kernels: 35.6 us -> 21.6 us
  starting transfers between devices: 28.6 us -> 17.4 us
  local copies, waits for them, and re-layouts: 10.6 us -> 2.49 us
  other arithmetic: 7.84 us -> 2.29 us
    all_to_all x2 -> x4, blocking collectives: 26.2 us -> 54.1 us  [the longest x1 20.6 us: body(): recv_0 = lax.all_to_all(sent_0, 'seq', 0, 0, tiled=True)]
    all_to_all x2 -> x0, waiting for transfers between devices: 17.5 us -> none  [the longest x1 11 us: after_qkv(): recv = lax.all_to_all(sent, 'seq', 0, 0, tiled=True)]
    all_to_all x2 -> x0, starting transfers between devices: 11.4 us -> none  [the longest x1 7.78 us: after_qkv(): recv = lax.all_to_all(sent, 'seq', 0, 0, tiled=True)]
    pallas_call x4 -> x6, Pallas kernels: 25.3 us -> 14.1 us  [the longest x1 5.39 us: prepare_call(): pl.pallas_call(prepare_kernel, out_shape=(pltpu.VMEM((total, width // 2),...]
    unnamed x26 -> x10, local copies, waits for them, and re-layouts: 4.55 us -> 0.82 us
    select_n x8 -> x2, other arithmetic: 4.05 us -> 1.11 us  [the longest x1 1.07 us: body(): result = jnp.where(is_first, result_0, added(x_half, on_chip, arrived))]
    pallas_call x2, Pallas kernels: 10.2 us -> 7.5 us  [attention_call(): pl.pallas_call(lambda *refs: attention_kernel(*refs, rows=rows, per_dev=p...]
    squeeze x3 -> x0, local copies, waits for them, and re-layouts: 2.52 us -> none  [the longest x2 1.99 us: after_qkv(): other = lax.dynamic_index_in_dim(partial, 1 - core, 0, keepdims=False)]
  transfers between devices with their start and end apart: 11 -> 10, of which waited for: 9 -> 7; matrix products, arithmetic and copies ran while one was open for 4% -> 1% of each run, Pallas kernels for 0% -> 4%
where the time goes in v2:
time: 121 us; the launch traced here: 120 us
  blocking collectives  54.1 us (45%)
  Pallas kernels  21.6 us (18%)
  waiting for transfers between devices  20.3 us (17%)
  starting transfers between devices  17.4 us (14%)
  local copies, waits for them, and re-layouts  2.49 us (2%)
  other arithmetic  2.29 us (2%)
  between operations  1.75 us (1%)
    all_to_all x1, blocking collectives, body(): recv_0 = lax.all_to_all(sent_0, 'seq', 0, 0, tiled=True)  20.6 us
    all_to_all x2, blocking collectives, body(): lax.all_to_all(attended, 'seq', 0, 0, tiled=True)  20.3 us
    ppermute x10, waiting for transfers between devices, swap(): return lax.ppermute(value, ('section', 'mp'), pairs)  20.3 us
    ppermute x10, starting transfers between devices, swap(): return lax.ppermute(value, ('section', 'mp'), pairs)  17.4 us
    all_to_all x1, blocking collectives, body(): recv_1 = lax.all_to_all(sent_1, 'seq', 0, 0, tiled=True)  13.1 us
    pallas_call x2, Pallas kernels, attention_call(): pl.pallas_call(lambda *refs: attention_kernel(*refs, rows=rows, per_dev=p...  7.5 us
    pallas_call x1, Pallas kernels, prepare_call(): pl.pallas_call(prepare_kernel, out_shape=(pltpu.VMEM((total, width // 2),...  5.39 us
    pallas_call x1, Pallas kernels, second_call(): pl.pallas_call(lambda *refs: second_kernel(*refs, rows=rows), out_shape=(...  2.91 us
  transfers between devices with their start and end apart: 10, of which 7 were waited for; matrix products, arithmetic and copies ran while one was open for 1% of the time, Pallas kernels for 4%

profile of v2, /device:TPU:1, one launch (start us, length us, event | category | flops | bytes accessed | tf_op | source)
XLA Modules:
  0.0 120.2 jit_solution(12796101500125188439)
XLA Ops:
  0.6 0.0 copy-start
  1.5 0.8 copy-done
  2.3 0.4 fusion.refs_1_
  2.7 1.4 %collective-permute-start = (f32[1,2304]{1,0:T(1,128)S(1)}, f32[1,2304]{1,0:T(1,128)S(1)}, u32[]{:S(2)}, u32[]{:S(2)}) collective-permute-start(f32[1,2304]{1,0:T(1,128)S(1)} %fusion.refs_1_), channel_id=1, source_target_pairs={{0,1},{1,0},{2,3},{3,2},{64,65},{65,64},{66,67},{67,66},{4,5},{5,4... | collective-permute-start | bytes 27656 | tf_op jit(solution)/shard_map/ppermute | solution.py:33
  4.2 1.3 %collective-permute-start.1 = (f32[1,2304]{1,0:T(1,128)S(1)}, f32[1,2304]{1,0:T(1,128)S(1)}, u32[]{:S(2)}, u32[]{:S(2)}) collective-permute-start(f32[1,2304]{1,0:T(1,128)S(1)} %fusion.refs_1_), channel_id=1, source_target_pairs={{0,2},{1,3},{2,0},{3,1},{64,66},{65,67},{66,64},{67,65},{4,6},{5,7... | collective-permute-start | bytes 27656 | tf_op jit(solution)/shard_map/ppermute | solution.py:33
  5.5 0.4 collective-permute-start.2
  5.9 5.4 %prepare.1 = (bf16[80,1536]{1,0:T(8,128)(2,1)S(1)}, f32[80,3072]{1,0:T(8,128)S(1)}, bf16[12,48,128]{2,1,0:T(8,128)(2,1)S(1)}, bf16[3,3072,768]{2,1,0:T(8,128)(2,1)S(1)}) custom-call(bf16[2,4,8,3072]{3,2,1,0:T(8,128)(2,1)} %video_ref.1, bf16[2,8,3072]{2,1,0:T(8,128)(2,1)} %text_ref.1, bf16[3,3072,768]{2,1,0:T(8,128)(2,1)} %bitcast.17, ...), custom_call_target="tpu_custom_call" | custom-call | tf_op jit(solution)/shard_map/prepare/pallas_call | solution.py:107
  11.3 0.0 collective-permute-done.refs_2_
  11.3 0.0 collective-permute-done.1.refs_3_
  11.3 0.0 collective-permute-done.2.refs_4_
  11.3 0.0 copy-start.2
  11.3 0.0 copy-start.3
  11.3 2.5 %first_qkv.1 = (bf16[16,168,128]{2,1,0:T(8,128)(2,1)S(1)}, bf16[2,80,768]{2,1,0:T(8,128)(2,1)S(1)}, f32[3,3072]{1,0:T(4,128)S(1)}) custom-call(f32[80,3072]{1,0:T(8,128)S(1)} %get-tuple-element.28.refs_0_, f32[1,2304]{1,0:T(1,128)S(1)} %fusion.refs_1_, f32[1,2304]{1,0:T(1,128)S(1)} %collective-permute-done.refs_2_, ...), custom_call_target="tpu_custom_call" | custom-call | tf_op jit(solution)/shard_map/first_qkv/pallas_call | solution.py:172
  13.8 20.6 %all_to_all.20.refs_2_.refs_3_ = bf16[16,168,128]{2,1,0:T(8,128)(2,1)S(1)} all-to-all(bf16[16,168,128]{2,1,0:T(8,128)(2,1)S(1)} %get-tuple-element.32), channel_id=1, replica_groups=mesh['section'=2,'seq'=16,'mp'=4] {'seq'}, dimensions={0} | all-to-all | bytes 1376256 | tf_op jit(solution)/shard_map/all_to_all | solution.py:394
  34.4 0.0 copy-done.2
  34.4 0.0 copy-done.3
  34.4 3.7 %attention.2 = (bf16[16,40,128]{2,1,0:T(8,128)(2,1)S(1)}, bf16[768,3072]{1,0:T(8,128)(2,1)S(1)}) custom-call(s32[2,4]{1,0:T(2,128)S(1)} %copy-done.2, s32[2]{0:T(128)S(1)} %copy-done.3, bf16[16,168,128]{2,1,0:T(8,128)(2,1)S(1)} %all_to_all.20.refs_2_.refs_3_, bf16[16,168,128]{2,1,0:T(8,128)(2,1)S(1)} %all_to_all.20.refs_2_.refs_3_, bf16[768,3072]{1,0:T(8,128)(2,1)} %bitcast.18), custom_call_target="tpu_custom_call" | custom-call | tf_op jit(solution)/shard_map/attention/pallas_call | solution.py:286
  38.2 10.0 %all_to_all.21.recv_ref = bf16[16,40,128]{2,1,0:T(8,128)(2,1)S(1)} all-to-all(bf16[16,40,128]{2,1,0:T(8,128)(2,1)S(1)} %get-tuple-element.33), channel_id=1, replica_groups=mesh['section'=2,'seq'=16,'mp'=4] {'seq'}, dimensions={0} | all-to-all | bytes 327680 | tf_op jit(solution)/shard_map/all_to_all | solution.py:398
  48.2 1.0 out_projection.2
  49.2 2.5 %collective-permute-start.3 = (bf16[80,1536]{1,0:T(8,128)(2,1)S(1)}, bf16[80,1536]{1,0:T(8,128)(2,1)S(1)}, u32[]{:S(2)}, u32[]{:S(2)}) collective-permute-start(bf16[80,1536]{1,0:T(8,128)(2,1)S(1)} %get-tuple-element.37), channel_id=1, source_target_pairs={{0,1},{1,0},{2,3},{3,2},{64,65},{65,64},{66,67},{67,66},{4,5},{5,4... | collective-permute-start | bytes 737288 | tf_op jit(solution)/shard_map/ppermute | solution.py:33
  51.7 1.1 collective-permute-done.3
  52.9 1.3 %collective-permute-start.4 = (bf16[80,1536]{1,0:T(8,128)(2,1)S(1)}, bf16[80,1536]{1,0:T(8,128)(2,1)S(1)}, u32[]{:S(2)}, u32[]{:S(2)}) collective-permute-start(bf16[80,1536]{1,0:T(8,128)(2,1)S(1)} %add_convert_fusion.3), channel_id=1, source_target_pairs={{0,2},{1,3},{2,0},{3,1},{64,66},{65,67},{66,64},{67,65},{4,6},{5,7... | collective-permute-start | bytes 737288 | tf_op jit(solution)/shard_map/ppermute | solution.py:33
  54.2 6.0 %collective-permute-done.4 = bf16[80,1536]{1,0:T(8,128)(2,1)S(1)} collective-permute-done((bf16[80,1536]{1,0:T(8,128)(2,1)S(1)}, bf16[80,1536]{1,0:T(8,128)(2,1)S(1)}, u32[]{:S(2)}, u32[]{:S(2)}) %collective-permute-start.4) | collective-permute-done | bytes 245792 | tf_op jit(solution)/shard_map/ppermute | solution.py:33
  60.2 0.1 add_convert_fusion.2
  60.3 0.0 copy-start.4
  60.3 4.4 %collective-permute-start.5 = (bf16[80,1536]{1,0:T(8,128)(2,1)S(1)}, bf16[80,1536]{1,0:T(8,128)(2,1)S(1)}, u32[]{:S(2)}, u32[]{:S(2)}) collective-permute-start(bf16[80,1536]{1,0:T(8,128)(2,1)S(1)} %add_convert_fusion.2), channel_id=1, source_target_pairs={{0,66},{1,67},{2,64},{3,65},{4,70},{5,71},{6,68},{7,69},{8,74},{9,... | collective-permute-start | bytes 737288 | tf_op jit(solution)/shard_map/ppermute | solution.py:33
  64.7 4.0 %collective-permute-done.5.refs_0_ = bf16[80,1536]{1,0:T(8,128)(2,1)S(1)} collective-permute-done((bf16[80,1536]{1,0:T(8,128)(2,1)S(1)}, bf16[80,1536]{1,0:T(8,128)(2,1)S(1)}, u32[]{:S(2)}, u32[]{:S(2)}) %collective-permute-start.5) | collective-permute-done | bytes 245792 | tf_op jit(solution)/shard_map/ppermute | solution.py:33
  68.7 2.1 %collective-permute-start.6 = (bf16[80,1536]{1,0:T(8,128)(2,1)S(1)}, bf16[80,1536]{1,0:T(8,128)(2,1)S(1)}, u32[]{:S(2)}, u32[]{:S(2)}) collective-permute-start(bf16[80,1536]{1,0:T(8,128)(2,1)S(1)} %collective-permute-done.5.refs_0_), channel_id=1, source_target_pairs={{0,1},{1,0},{2,3},{3,2},{64,65},{65,64},{66,67},{67,66},{4,5},{5,4... | collective-permute-start | bytes 737288 | tf_op jit(solution)/shard_map/ppermute | solution.py:33
  70.8 0.0 copy-done.4
  70.8 1.1 collective-permute-done.6.refs_1_
  72.0 2.9 %second_qkv.1 = (bf16[16,120,128]{2,1,0:T(8,128)(2,1)S(1)}, bf16[2,80,768]{2,1,0:T(8,128)(2,1)S(1)}) custom-call(bf16[80,1536]{1,0:T(8,128)(2,1)S(1)} %collective-permute-done.5.refs_0_, bf16[80,1536]{1,0:T(8,128)(2,1)S(1)} %collective-permute-done.6.refs_1_, f32[3,3072]{1,0:T(4,128)S(1)} %get-tuple-element.34.mod_ref.refs_2_, ...), custom_call_target="tpu_custom_call" | custom-call | tf_op jit(solution)/shard_map/second_qkv/pallas_call | solution.py:204
  74.9 0.0 copy-start.1
  74.9 13.1 %all_to_all.22.refs_2_ = bf16[16,120,128]{2,1,0:T(8,128)(2,1)S(1)} all-to-all(bf16[16,120,128]{2,1,0:T(8,128)(2,1)S(1)} %get-tuple-element.38), channel_id=1, replica_groups=mesh['section'=2,'seq'=16,'mp'=4] {'seq'}, dimensions={0} | all-to-all | bytes 983040 | tf_op jit(solution)/shard_map/all_to_all | solution.py:403
  88.0 3.8 %attention.3 = bf16[16,40,128]{2,1,0:T(8,128)(2,1)S(1)} custom-call(s32[2,4]{1,0:T(2,128)S(1)} %copy-done.2, s32[2]{0:T(128)S(1)} %copy-done.3, bf16[16,120,128]{2,1,0:T(8,128)(2,1)S(1)} %all_to_all.22.refs_2_, bf16[16,168,128]{2,1,0:T(8,128)(2,1)S(1)} %all_to_all.20.refs_2_.refs_3_), custom_call_target="tpu_custom_call" | custom-call | tf_op jit(solution)/shard_map/attention/pallas_call | solution.py:286
  91.8 10.3 %all_to_all.23.recv_ref = bf16[16,40,128]{2,1,0:T(8,128)(2,1)S(1)} all-to-all(bf16[16,40,128]{2,1,0:T(8,128)(2,1)S(1)} %attention.3), channel_id=1, replica_groups=mesh['section'=2,'seq'=16,'mp'=4] {'seq'}, dimensions={0} | all-to-all | bytes 327680 | tf_op jit(solution)/shard_map/all_to_all | solution.py:405
  102.1 1.3 %out_projection.3 = (bf16[80,1536]{1,0:T(8,128)(2,1)}, f32[80,1536]{1,0:T(8,128)S(1)}) custom-call(bf16[16,40,128]{2,1,0:T(8,128)(2,1)S(1)} %all_to_all.23.recv_ref, f32[3,3072]{1,0:T(4,128)S(1)} %get-tuple-element.34.mod_ref.refs_2_, bf16[768,3072]{1,0:T(8,128)(2,1)S(1)} %get-tuple-element.35.w_ref), custom_call_target="tpu_custom_call" | custom-call | tf_op jit(solution)/shard_map/out_projection/pallas_call | solution.py:317
  103.4 0.0 copy-done.1
  103.4 2.5 %collective-permute-start.7 = (bf16[80,1536]{1,0:T(8,128)(2,1)}, bf16[80,1536]{1,0:T(8,128)(2,1)}, u32[]{:S(2)}, u32[]{:S(2)}) collective-permute-start(bf16[80,1536]{1,0:T(8,128)(2,1)} %get-tuple-element.40), channel_id=1, source_target_pairs={{0,1},{1,0},{2,3},{3,2},{64,65},{65,64},{66,67},{67,66},{4,5},{5,4... | collective-permute-start | bytes 737288 | tf_op jit(solution)/shard_map/ppermute | solution.py:33
  105.9 1.5 %collective-permute-done.7 = bf16[80,1536]{1,0:T(8,128)(2,1)} collective-permute-done((bf16[80,1536]{1,0:T(8,128)(2,1)}, bf16[80,1536]{1,0:T(8,128)(2,1)}, u32[]{:S(2)}, u32[]{:S(2)}) %collective-permute-start.7) | collective-permute-done | bytes 245792 | tf_op jit(solution)/shard_map/ppermute | solution.py:33
  107.4 1.0 add_convert_fusion.1
  108.4 0.1 collective-permute-start.8
  108.5 0.2 copy.15
  108.7 0.8 slice.8
  109.5 0.7 slice_bitcast_fusion
  110.2 5.4 %collective-permute-done.8 = bf16[80,1536]{1,0:T(8,128)(2,1)S(1)} collective-permute-done((bf16[80,1536]{1,0:T(8,128)(2,1)S(1)}, bf16[80,1536]{1,0:T(8,128)(2,1)S(1)}, u32[]{:S(2)}, u32[]{:S(2)}) %collective-permute-start.8) | collective-permute-done | bytes 245792 | tf_op jit(solution)/shard_map/ppermute | solution.py:33
  115.6 1.1 fusion.2.mine_ref
  116.7 1.3 %collective-permute-start.9 = (bf16[80,1536]{1,0:T(8,128)(2,1)S(1)}, bf16[80,1536]{1,0:T(8,128)(2,1)S(1)}, u32[]{:S(2)}, u32[]{:S(2)}) collective-permute-start(bf16[80,1536]{1,0:T(8,128)(2,1)S(1)} %fusion.2.mine_ref), channel_id=1, source_target_pairs={{0,1},{1,0},{2,3},{3,2},{64,65},{65,64},{66,67},{67,66},{4,5},{5,4... | collective-permute-start | bytes 737288 | tf_op jit(solution)/shard_map/ppermute | solution.py:33
  118.0 1.1 collective-permute-done.9.other_ref
  119.1 0.9 store.1
  (5 shorter events, 0.2 us)
Async XLA Ops:
  0.6 1.7 %copy-start = (bf16[1,512,2304]{2,1,0:T(8,128)(2,1)S(1)}, bf16[1,512,2304]{2,1,0:T(8,128)(2,1)}, u32[]{:S(2)}) copy-start(bf16[1,512,2304]{2,1,0:T(8,128)(2,1)} %param.14) | copy-start | bytes 7077892
  2.7 8.5 %collective-permute-start = (f32[1,2304]{1,0:T(1,128)S(1)}, f32[1,2304]{1,0:T(1,128)S(1)}, u32[]{:S(2)}, u32[]{:S(2)}) collective-permute-start(f32[1,2304]{1,0:T(1,128)S(1)} %fusion.refs_1_), channel_id=1, source_target_pairs={{0,1},{1,0},{2,3},{3,2},{64,65},{65,64},{66,67},{67,66},{4,5},{5,4... | collective-permute-start | bytes 27656 | tf_op jit(solution)/shard_map/ppermute | solution.py:33
  4.2 7.1 %collective-permute-start.1 = (f32[1,2304]{1,0:T(1,128)S(1)}, f32[1,2304]{1,0:T(1,128)S(1)}, u32[]{:S(2)}, u32[]{:S(2)}) collective-permute-start(f32[1,2304]{1,0:T(1,128)S(1)} %fusion.refs_1_), channel_id=1, source_target_pairs={{0,2},{1,3},{2,0},{3,1},{64,66},{65,67},{66,64},{67,65},{4,6},{5,7... | collective-permute-start | bytes 27656 | tf_op jit(solution)/shard_map/ppermute | solution.py:33
  5.5 5.8 %collective-permute-start.2 = (f32[1,2304]{1,0:T(1,128)S(1)}, f32[1,2304]{1,0:T(1,128)S(1)}, u32[]{:S(2)}, u32[]{:S(2)}) collective-permute-start(f32[1,2304]{1,0:T(1,128)S(1)} %fusion.refs_1_), channel_id=1, source_target_pairs={{0,3},{1,2},{2,1},{3,0},{64,67},{65,66},{66,65},{67,64},{4,7},{5,6... | collective-permute-start | bytes 27656 | tf_op jit(solution)/shard_map/ppermute | solution.py:33
  11.3 23.2 %copy-start.2 = (s32[2,4]{1,0:T(2,128)S(1)}, s32[2,4]{1,0:T(2,128)}, u32[]{:S(2)}) copy-start(s32[2,4]{1,0:T(2,128)} %refs_0_.3) | copy-start | bytes 100
  11.3 23.1 %copy-start.3 = (s32[2]{0:T(128)S(1)}, s32[2]{0:T(128)}, u32[]{:S(2)}) copy-start(s32[2]{0:T(128)} %refs_1_.3) | copy-start | bytes 28
  49.2 3.7 %collective-permute-start.3 = (bf16[80,1536]{1,0:T(8,128)(2,1)S(1)}, bf16[80,1536]{1,0:T(8,128)(2,1)S(1)}, u32[]{:S(2)}, u32[]{:S(2)}) collective-permute-start(bf16[80,1536]{1,0:T(8,128)(2,1)S(1)} %get-tuple-element.37), channel_id=1, source_target_pairs={{0,1},{1,0},{2,3},{3,2},{64,65},{65,64},{66,67},{67,66},{4,5},{5,4... | collective-permute-start | bytes 737288 | tf_op jit(solution)/shard_map/ppermute | solution.py:33
  52.9 7.2 %collective-permute-start.4 = (bf16[80,1536]{1,0:T(8,128)(2,1)S(1)}, bf16[80,1536]{1,0:T(8,128)(2,1)S(1)}, u32[]{:S(2)}, u32[]{:S(2)}) collective-permute-start(bf16[80,1536]{1,0:T(8,128)(2,1)S(1)} %add_convert_fusion.3), channel_id=1, source_target_pairs={{0,2},{1,3},{2,0},{3,1},{64,66},{65,67},{66,64},{67,65},{4,6},{5,7... | collective-permute-start | bytes 737288 | tf_op jit(solution)/shard_map/ppermute | solution.py:33
  60.3 10.6 %copy-start.4 = (bf16[80,1536]{1,0:T(8,128)(2,1)}, bf16[80,1536]{1,0:T(8,128)(2,1)S(1)}, u32[]{:S(2)}) copy-start(bf16[80,1536]{1,0:T(8,128)(2,1)S(1)} %add_convert_fusion.2) | copy-start | bytes 737284
  60.3 8.4 %collective-permute-start.5 = (bf16[80,1536]{1,0:T(8,128)(2,1)S(1)}, bf16[80,1536]{1,0:T(8,128)(2,1)S(1)}, u32[]{:S(2)}, u32[]{:S(2)}) collective-permute-start(bf16[80,1536]{1,0:T(8,128)(2,1)S(1)} %add_convert_fusion.2), channel_id=1, source_target_pairs={{0,66},{1,67},{2,64},{3,65},{4,70},{5,71},{6,68},{7,69},{8,74},{9,... | collective-permute-start | bytes 737288 | tf_op jit(solution)/shard_map/ppermute | solution.py:33
  68.7 3.3 %collective-permute-start.6 = (bf16[80,1536]{1,0:T(8,128)(2,1)S(1)}, bf16[80,1536]{1,0:T(8,128)(2,1)S(1)}, u32[]{:S(2)}, u32[]{:S(2)}) collective-permute-start(bf16[80,1536]{1,0:T(8,128)(2,1)S(1)} %collective-permute-done.5.refs_0_), channel_id=1, source_target_pairs={{0,1},{1,0},{2,3},{3,2},{64,65},{65,64},{66,67},{67,66},{4,5},{5,4... | collective-permute-start | bytes 737288 | tf_op jit(solution)/shard_map/ppermute | solution.py:33
  74.9 28.5 %copy-start.1 = (bf16[2,80,768]{2,1,0:T(8,128)(2,1)}, bf16[2,80,768]{2,1,0:T(8,128)(2,1)S(1)}, u32[]{:S(2)}) copy-start(bf16[2,80,768]{2,1,0:T(8,128)(2,1)S(1)} %get-tuple-element.42) | copy-start | bytes 737284
  103.4 4.0 %collective-permute-start.7 = (bf16[80,1536]{1,0:T(8,128)(2,1)}, bf16[80,1536]{1,0:T(8,128)(2,1)}, u32[]{:S(2)}, u32[]{:S(2)}) collective-permute-start(bf16[80,1536]{1,0:T(8,128)(2,1)} %get-tuple-element.40), channel_id=1, source_target_pairs={{0,1},{1,0},{2,3},{3,2},{64,65},{65,64},{66,67},{67,66},{4,5},{5,4... | collective-permute-start | bytes 737288 | tf_op jit(solution)/shard_map/ppermute | solution.py:33
  108.4 7.2 %collective-permute-start.8 = (bf16[80,1536]{1,0:T(8,128)(2,1)S(1)}, bf16[80,1536]{1,0:T(8,128)(2,1)S(1)}, u32[]{:S(2)}, u32[]{:S(2)}) collective-permute-start(bf16[80,1536]{1,0:T(8,128)(2,1)S(1)} %add_convert_fusion.1), channel_id=1, source_target_pairs={{0,2},{1,3},{2,0},{3,1},{64,66},{65,67},{66,64},{67,65},{4,6},{5,7... | collective-permute-start | bytes 737288 | tf_op jit(solution)/shard_map/ppermute | solution.py:33
  116.7 2.4 %collective-permute-start.9 = (bf16[80,1536]{1,0:T(8,128)(2,1)S(1)}, bf16[80,1536]{1,0:T(8,128)(2,1)S(1)}, u32[]{:S(2)}, u32[]{:S(2)}) collective-permute-start(bf16[80,1536]{1,0:T(8,128)(2,1)S(1)} %fusion.2.mine_ref), channel_id=1, source_target_pairs={{0,1},{1,0},{2,3},{3,2},{64,65},{65,64},{66,67},{67,66},{4,5},{5,4... | collective-permute-start | bytes 737288 | tf_op jit(solution)/shard_map/ppermute | solution.py:33

commit v3 on v2

--- a/solution.py
+++ b/solution.py
@@ -11,6 +11,7 @@
 LANES = 128
 EPS = 1e-05
 NEG = -1e30
+CHUNKS = 2
 VMEM_LIMIT = 12 * 1024 * 1024
 
 
@@ -28,8 +29,7 @@
     for section in range(2):
         for part in range(4):
             target = mapping(section, part)
-            if target is not None:
-                pairs.append((section * 4 + part, target[0] * 4 + target[1]))
+            pairs.append((section * 4 + part, target[0] * 4 + target[1]))
     return lax.ppermute(value, ("section", "mp"), pairs)
 
 
@@ -42,7 +42,7 @@
 
 
 def next_section(value):
-    return swap(value, lambda section, part: (1, part ^ 2) if section == 0 else None)
+    return swap(value, lambda section, part: (1 - section, part ^ 2))
 
 VMEM = pl.BlockSpec(memory_space=pltpu.VMEM)
 SMEM = pl.BlockSpec(memory_space=pltpu.SMEM)
@@ -58,18 +58,17 @@
 
 
 def prepare_kernel(
-    video_ref, text_ref, w_ref, stale_ref, half_ref, unit_ref, packed_ref, w_vmem, video_buf, text_buf, stale_buf, x_ref, sems
+    video_ref, text_ref, w_ref, stale_ref, unit_ref, packed_ref, w_vmem, *refs
 ):
+    *half_refs, video_buf, text_buf, stale_buf, x_ref, sems = refs
     requests, patches, per_dev, width = video_ref.shape
     first = [
         pltpu.make_async_copy(stale_ref, stale_buf, sems.at[0]),
         pltpu.make_async_copy(video_ref, video_buf, sems.at[1]),
         pltpu.make_async_copy(text_ref, text_buf, sems.at[2]),
     ]
-    loads = [
-        pltpu.make_async_copy(w_ref.at[part], w_vmem.at[part], sems.at[3 + part]) for part in range(w_ref.shape[0])
-    ]
-    for copy in first + loads:
+    load = pltpu.make_async_copy(w_ref.at[pl.ds(0, 2)], w_vmem, sems.at[3])
+    for copy in first + [load]:
         copy.start()
     first[0].wait()
     blocks = w_ref.shape[2] // LANES
@@ -94,9 +93,10 @@
             row += per_dev
     half = width // 2
     core = lax.axis_index("mp") % 2
-    half_ref[...] = x_ref[:, pl.ds(pl.multiple_of(core * half, LANES), half)]
-    for copy in loads:
-        copy.wait()
+    span = half // len(half_refs)
+    for chunk, ref in enumerate(half_refs):
+        ref[...] = x_ref[:, pl.ds(pl.multiple_of(core * half + chunk * span, LANES), span)]
+    load.wait()
 
 
 def prepare_call(video, text, weight, stale):
@@ -107,33 +107,36 @@
     return pl.pallas_call(
         prepare_kernel,
         out_shape=(
-            pltpu.VMEM((total, width // 2), jnp.bfloat16),
             pltpu.VMEM((total, width), jnp.float32),
             pltpu.VMEM((units, 2 * (patches - 1) * per_dev, LANES), jnp.bfloat16),
-            pltpu.VMEM(weight.shape, jnp.bfloat16),
-        ),
+            pltpu.VMEM((2,) + weight.shape[1:], jnp.bfloat16),
+        )
+        + (pltpu.VMEM((total, width // 2 // CHUNKS), jnp.bfloat16),) * CHUNKS,
         in_specs=[ANY] * 4,
-        out_specs=(VMEM,) * 4,
+        out_specs=(VMEM,) * (3 + CHUNKS),
         scratch_shapes=[
             pltpu.VMEM(video.shape, jnp.bfloat16),
             pltpu.VMEM(text.shape, jnp.bfloat16),
             pltpu.VMEM(stale.shape, jnp.bfloat16),
             pltpu.VMEM((total, width), jnp.bfloat16),
-            pltpu.SemaphoreType.DMA((3 + weight.shape[0],)),
+            pltpu.SemaphoreType.DMA((4,)),
         ],
         compiler_params=PARAMS,
         name="prepare",
     )(*operands)
 
 
-def project(normed_ref, w_ref, o_ref, kv_ref, rows):
-    parts, _, columns = w_ref.shape
+def project(normed_ref, wqk_ref, wv_ref, o_ref, kv_ref, rows, load=None):
+    columns = wv_ref.shape[1]
     blocks = columns // LANES
     requests = normed_ref.shape[0] // rows
     for unit in range(requests * blocks, o_ref.shape[0]):
         o_ref[unit] = jnp.zeros(o_ref.shape[1:], o_ref.dtype)
-    for part in range(parts):
-        acc = jnp.dot(normed_ref[...], w_ref[part], preferred_element_type=jnp.float32)
+    for part in range(3):
+        if part == 2 and load is not None:
+            load.wait()
+        weight = wqk_ref[part] if part < 2 else wv_ref[...]
+        acc = jnp.dot(normed_ref[...], weight, preferred_element_type=jnp.float32)
         if part:
             kv_ref[part - 1] = acc.astype(jnp.bfloat16)
         for request in range(requests):
@@ -144,8 +147,26 @@
 
 
 def first_kernel(
-    unit_ref, mod_0, mod_1, mod_2, mod_3, w_ref, stale_ref, o_ref, kv_ref, mod_ref, pieces_ref, normed_ref, *, rows
+    unit_ref,
+    mod_0,
+    mod_1,
+    mod_2,
+    mod_3,
+    wqk_ref,
+    w_ref,
+    stale_ref,
+    o_ref,
+    kv_ref,
+    mod_ref,
+    wv_ref,
+    pieces_ref,
+    normed_ref,
+    sem,
+    *,
+    rows,
 ):
+    load = pltpu.make_async_copy(w_ref.at[2], wv_ref, sem)
+    load.start()
     for index, piece in enumerate((mod_0, mod_1, mod_2, mod_3)):
         pieces_ref[lax.axis_index("mp") ^ index, 0:1, :] = piece[...]
     total, width = unit_ref.shape
@@ -164,10 +185,10 @@
         normed_ref[start : start + step, :] = normed.astype(jnp.bfloat16)
     for unit in range(stale_ref.shape[0]):
         o_ref[unit, 3 * rows :, :] = stale_ref[unit]
-    project(normed_ref, w_ref, o_ref, kv_ref, rows)
-
-
-def first_call(unit, mods, weight, stale, rows, devices):
+    project(normed_ref, wqk_ref, wv_ref, o_ref, kv_ref, rows, load)
+
+
+def first_call(unit, mods, weight_qk, weight, stale, rows, devices):
     total, width = unit.shape
     return pl.pallas_call(
         lambda *refs: first_kernel(*refs, rows=rows),
@@ -175,44 +196,65 @@
             jax.ShapeDtypeStruct((devices, 3 * rows + stale.shape[1], LANES), jnp.bfloat16),
             jax.ShapeDtypeStruct((2, total, weight.shape[2]), jnp.bfloat16),
             pltpu.VMEM((3, width), jnp.float32),
+            pltpu.VMEM(weight.shape[1:], jnp.bfloat16),
         ),
-        in_specs=[VMEM] * 7,
-        out_specs=(VMEM,) * 3,
+        in_specs=[VMEM] * 6 + [ANY, VMEM],
+        out_specs=(VMEM,) * 4,
         scratch_shapes=[
             pltpu.VMEM((4, 8, mods[0].shape[1]), jnp.float32),
             pltpu.VMEM((total, width), jnp.bfloat16),
+            pltpu.SemaphoreType.DMA,
         ],
         compiler_params=PARAMS,
         name="first_qkv",
-    )(unit, *mods, weight, stale)
-
-
-def second_kernel(mine_ref, other_ref, mod_ref, w_ref, o_ref, kv_ref, x_ref, normed_ref, *, rows):
-    total, half = mine_ref.shape
+    )(unit, *mods, weight_qk, pltpu.with_memory_space_constraint(weight, pltpu.HBM), stale)
+
+
+def second_kernel(
+    mod_ref, wqk_ref, wv_ref, kv_0_ref, *refs, rows
+):
+    mine_refs, other_refs, before_refs = (refs[i * CHUNKS : (i + 1) * CHUNKS] for i in range(3))
+    o_ref, kv_ref, *base_refs, x_ref, normed_ref = refs[3 * CHUNKS :]
+    total, span = mine_refs[0].shape
+    half = span * CHUNKS
     core = lax.axis_index("mp") % 2
-    x_ref[:, pl.ds(pl.multiple_of(core * half, LANES), half)] = mine_ref[...]
-    x_ref[:, pl.ds(pl.multiple_of((1 - core) * half, LANES), half)] = other_ref[...]
+    for chunk in range(CHUNKS):
+        x_ref[:, pl.ds(pl.multiple_of(core * half + chunk * span, LANES), span)] = mine_refs[chunk][...]
+        x_ref[:, pl.ds(pl.multiple_of((1 - core) * half + chunk * span, LANES), span)] = other_refs[chunk][...]
     step = 16
     for start in range(0, total, step):
         normed = centered(x_ref[start : start + step, :]) * (1.0 + mod_ref[1:2, :]) + mod_ref[0:1, :]
         normed_ref[start : start + step, :] = normed.astype(jnp.bfloat16)
-    project(normed_ref, w_ref, o_ref, kv_ref, rows)
-
-
-def second_call(mine, other, mod, weight, rows, devices):
-    total, half = mine.shape
+    project(normed_ref, wqk_ref, wv_ref, o_ref, kv_ref, rows)
+    is_first = lax.axis_index("section") == 0
+
+    @pl.when(is_first)
+    def _():
+        kv_ref[...] = kv_0_ref[...]
+        for base_ref, before_ref in zip(base_refs, before_refs):
+            base_ref[...] = before_ref[...]
+
+    @pl.when(jnp.logical_not(is_first))
+    def _():
+        for base_ref, mine_ref in zip(base_refs, mine_refs):
+            base_ref[...] = mine_ref[...]
+
+
+def second_call(mine, other, before, kv_0, mod, weight_qk, weight_v, rows, devices):
+    total, span = mine[0].shape
     return pl.pallas_call(
         lambda *refs: second_kernel(*refs, rows=rows),
         out_shape=(
             jax.ShapeDtypeStruct((devices, 3 * rows, LANES), jnp.bfloat16),
-            jax.ShapeDtypeStruct((2, total, weight.shape[2]), jnp.bfloat16),
-        ),
-        in_specs=[VMEM] * 4,
-        out_specs=(VMEM, VMEM),
-        scratch_shapes=[pltpu.VMEM((total, 2 * half), jnp.bfloat16)] * 2,
+            jax.ShapeDtypeStruct(kv_0.shape, jnp.bfloat16),
+        )
+        + (pltpu.VMEM((total, span), jnp.bfloat16),) * CHUNKS,
+        in_specs=[VMEM] * (4 + 3 * CHUNKS),
+        out_specs=(VMEM,) * (2 + CHUNKS),
+        scratch_shapes=[pltpu.VMEM((total, 2 * CHUNKS * span), jnp.bfloat16)] * 2,
         compiler_params=PARAMS,
         name="second_qkv",
-    )(mine, other, mod, weight)
+    )(mod, weight_qk, weight_v, kv_0, *mine, *other, *before)
 
 
 def attention_kernel(*refs, rows, per_dev, patches, blocks):
@@ -245,6 +287,7 @@
         limit = jnp.where(slot >= index * capacity, length + index * capacity, limit)
     bias = jnp.where(slot < limit, 0.0, NEG)
     lane = lax.broadcasted_iota(jnp.int32, (1, LANES), 1)
+    ones = jnp.ones((groups * capacity, LANES), jnp.bfloat16)
     factor = HEAD ** (-0.5) * math.log2(math.e)
     for patch in range(patches):
         keys = jnp.concatenate(
@@ -253,26 +296,26 @@
         values = jnp.concatenate(
             [fresh_v[i] if i <= patch else stale_v[i] for i in range(patches)] + [fresh_v[patches]], axis=0
         )
-        for group in [patch, patches] if patch == 0 else [patch]:
-            queries = block(recv_ref, 0, group)
-            outs = []
-            for head in range(2):
-                mine = (lane < HEAD) if head == 0 else (lane >= HEAD)
-                scores = lax.dot_general(
-                    jnp.where(mine, queries, jnp.zeros_like(queries)),
-                    keys,
-                    (((1,), (1,)), ((), ())),
-                    preferred_element_type=jnp.float32,
-                )
-                scores = scores + bias
-                top = jnp.max(scores, axis=-1, keepdims=True)
-                weights = jnp.exp2((scores - top) * factor)
-                weight_sum = jnp.sum(weights, axis=-1, keepdims=True)
-                acc = jnp.dot(
-                    weights.astype(jnp.bfloat16), values, preferred_element_type=jnp.float32
-                )
-                outs.append(acc / weight_sum)
-            out = jnp.where(lane < HEAD, outs[0], outs[1]).astype(jnp.bfloat16)
+        members = [patch, patches] if patch == 0 else [patch]
+        queries = [block(recv_ref, 0, group) for group in members]
+        queries = [jnp.where(lane < HEAD, q, jnp.zeros_like(q)) for q in queries] + [
+            jnp.where(lane < HEAD, jnp.zeros_like(q), q) for q in queries
+        ]
+        scores = lax.dot_general(
+            jnp.concatenate(queries, axis=0),
+            keys,
+            (((1,), (1,)), ((), ())),
+            preferred_element_type=jnp.float32,
+        )
+        scores = scores + bias
+        top = jnp.max(scores, axis=-1, keepdims=True)
+        weights = jnp.exp2((scores - top) * factor).astype(jnp.bfloat16)
+        acc = jnp.dot(weights, jnp.concatenate([values, ones], axis=1), preferred_element_type=jnp.float32)
+        acc = acc[:, :LANES] / acc[:, LANES:]
+        for index, group in enumerate(members):
+            lower = acc[index * capacity : (index + 1) * capacity]
+            upper = acc[(len(members) + index) * capacity : (len(members) + index + 1) * capacity]
+            out = jnp.where(lane < HEAD, lower, upper).astype(jnp.bfloat16)
             start = group * per_dev
             o_ref[:, start : start + per_dev, :] = out.reshape(devices, per_dev, LANES)
     if copy is not None:
@@ -294,7 +337,9 @@
     )(lens, text_len, recv, stale, *([pltpu.with_memory_space_constraint(weight, pltpu.HBM)] if loads else []))
 
 
-def out_kernel(recv_ref, mod_ref, w_ref, other_ref, mine_ref, mixed_ref):
+def out_kernel(recv_ref, mod_ref, w_ref, *refs, last):
+    *refs, mixed_ref = refs
+    other_refs, mine_refs = refs[: len(refs) // 2], refs[len(refs) // 2 :]
     depth, width = w_ref.shape
     rows = recv_ref.shape[1]
     blocks = depth // LANES
@@ -304,37 +349,46 @@
                 request * blocks + block
             ]
     half = width // 2
+    span = half // len(other_refs)
     core = lax.axis_index("mp") % 2
-    for ref, index in ((other_ref, 1 - core), (mine_ref, core)):
-        at = pl.ds(pl.multiple_of(index * half, LANES), half)
-        acc = jnp.dot(mixed_ref[...], w_ref[:, at], preferred_element_type=jnp.float32)
-        ref[...] = (acc * mod_ref[2:3, at]).astype(ref.dtype)
-
-
-def out_call(recv, mod, weight, requests):
+    for refs, index in ((other_refs, 1 - core), (mine_refs, core)):
+        for chunk, ref in enumerate(refs):
+            at = pl.ds(pl.multiple_of(index * half + chunk * span, LANES), span)
+            acc = jnp.dot(mixed_ref[...], w_ref[:, at], preferred_element_type=jnp.float32)
+            acc = acc * mod_ref[2:3, at]
+            if last:
+                acc = jnp.where(lax.axis_index("section") == 0, jnp.zeros_like(acc), acc)
+            ref[...] = acc.astype(ref.dtype)
+
+
+def out_call(recv, mod, weight, requests, last):
     depth, width = weight.shape
     total = requests * recv.shape[1]
     return pl.pallas_call(
-        out_kernel,
-        out_shape=(
-            pltpu.VMEM((total, width // 2), jnp.bfloat16),
-            pltpu.VMEM((total, width // 2), jnp.float32),
-        ),
+        lambda *refs: out_kernel(*refs, last=last),
+        out_shape=[
+            pltpu.VMEM((total, width // 2 // CHUNKS), dtype)
+            for dtype in (jnp.bfloat16, jnp.float32)
+            for _ in range(CHUNKS)
+        ],
         in_specs=[VMEM, VMEM, VMEM],
-        out_specs=(VMEM, VMEM),
+        out_specs=[VMEM] * (2 * CHUNKS),
         scratch_shapes=[pltpu.VMEM((total, depth), jnp.bfloat16)],
         compiler_params=PARAMS,
         name="out_projection",
     )(recv, mod, weight)
 
 
-def store_kernel(mine_ref, other_ref, video_ref, text_ref, sems):
+def store_kernel(*refs):
+    *pieces, video_ref, text_ref, sems = refs
     _, requests, patches, per_dev, _ = video_ref.shape
-    half = mine_ref.shape[1]
+    span = pieces[0].shape[1]
+    half = span * CHUNKS
     core = lax.axis_index("mp") % 2
     copies = []
-    for side, (source, index) in enumerate(((mine_ref, core), (other_ref, 1 - core))):
-        at = pl.ds(pl.multiple_of(index * half, LANES), half)
+    for side, source in enumerate(pieces):
+        index = core if side < CHUNKS else 1 - core
+        at = pl.ds(pl.multiple_of(index * half + side % CHUNKS * span, LANES), span)
         row = 0
         for request in range(requests):
             for patch in range(patches + 1):
@@ -360,12 +414,12 @@
             jax.ShapeDtypeStruct(video_shape, jnp.bfloat16),
             jax.ShapeDtypeStruct(text_shape, jnp.bfloat16),
         ),
-        in_specs=[VMEM, VMEM],
+        in_specs=[VMEM] * (2 * CHUNKS),
         out_specs=(ANY, ANY),
-        scratch_shapes=[pltpu.SemaphoreType.DMA((2, mine.shape[0] // video_shape[3]))],
+        scratch_shapes=[pltpu.SemaphoreType.DMA((2 * CHUNKS, mine[0].shape[0] // video_shape[3]))],
         compiler_params=PARAMS,
         name="store",
-    )(mine, other)
+    )(*mine, *other)
 
 
 def body(video, text, patch_lengths, text_len, timestep, w_mod, w_qkv, w_out, stale_cache):
@@ -375,44 +429,53 @@
     blocks = columns // LANES
     rows = patches * per_dev + text.shape[1]
 
-    timestep, is_first = lax.optimization_barrier((timestep, lax.axis_index("section") == 0))
     own_mod = modulation(timestep, w_mod[0])
     mods = [own_mod] + [
         swap(own_mod, lambda section, part, flip=flip: (section, part ^ flip)) for flip in (1, 2, 3)
     ]
-    x_half, unit, stale, weight_qkv = prepare_call(video, text, w_qkv[0].transpose(1, 0, 2), stale_cache[0])
-
-    def reduced(mixed, weight_out, mod):
-        other, mine = out_call(mixed, mod, weight_out, requests)
-        return (mine + swap_core(other).astype(jnp.float32)).astype(jnp.bfloat16)
+    weight = w_qkv[0].transpose(1, 0, 2)
+    unit, stale, weight_qk, *x_half = prepare_call(video, text, weight, stale_cache[0])
+
+    def reduced(mixed, weight_out, mod, last):
+        pieces = out_call(mixed, mod, weight_out, requests, last)
+        return [
+            (mine + swap_core(other).astype(jnp.float32)).astype(jnp.bfloat16)
+            for other, mine in zip(pieces[:CHUNKS], pieces[CHUNKS:])
+        ]
 
     def added(x_half, on_chip, arrived):
-        total = x_half.astype(jnp.float32) + (on_chip.astype(jnp.float32) + arrived.astype(jnp.float32))
-        return total.astype(jnp.bfloat16)
-
-    sent_0, kv_0, mod = first_call(unit, mods, weight_qkv, stale, rows, devices)
+        return [
+            (a.astype(jnp.float32) + (b.astype(jnp.float32) + c.astype(jnp.float32))).astype(jnp.bfloat16)
+            for a, b, c in zip(x_half, on_chip, arrived)
+        ]
+
+    def each(function, values):
+        return [function(value) for value in values]
+
+    sent_0, kv_0, mod, weight_v = first_call(unit, mods, weight_qk, weight, stale, rows, devices)
     recv_0 = lax.all_to_all(sent_0, "seq", 0, 0, tiled=True)
-    attended, weight_out = attention_call(
-        patch_lengths, text_len, recv_0, recv_0, w_out[0], rows, per_dev, blocks
+    weight_out = w_out[0]
+    attended = attention_call(patch_lengths, text_len, recv_0, recv_0, None, rows, per_dev, blocks)
+    on_chip = reduced(lax.all_to_all(attended, "seq", 0, 0, tiled=True), weight_out, mod, False)
+    result_0 = added(x_half, on_chip, each(swap_chip, on_chip))
+
+    x_half = each(next_section, result_0)
+    sent_1, key_value, *base = second_call(
+        x_half, each(swap_core, x_half), result_0, kv_0, mod, weight_qk, weight_v, rows, devices
     )
-    on_chip = reduced(lax.all_to_all(attended, "seq", 0, 0, tiled=True), weight_out, mod)
-    result_0 = added(x_half, on_chip, swap_chip(on_chip))
-
-    x_half = next_section(result_0)
-    sent_1, kv_1 = second_call(x_half, swap_core(x_half), mod, weight_qkv, rows, devices)
     recv_1 = lax.all_to_all(sent_1, "seq", 0, 0, tiled=True)
     attended = attention_call(patch_lengths, text_len, recv_1, recv_0, None, rows, per_dev, blocks)
-    on_chip = reduced(lax.all_to_all(attended, "seq", 0, 0, tiled=True), weight_out, mod)
-    arrived = swap_chip(on_chip)
-
-    key_value = jnp.where(is_first, kv_0, kv_1).reshape(2, requests, rows, columns).transpose(1, 2, 0, 3)
+    on_chip = reduced(lax.all_to_all(attended, "seq", 0, 0, tiled=True), weight_out, mod, True)
+    arrived = each(swap_chip, on_chip)
+
+    key_value = key_value.reshape(2, requests, rows, columns).transpose(1, 2, 0, 3)
     split_at = patches * per_dev
     cache_video = key_value[:, :split_at].reshape(1, requests, patches, per_dev, 2, columns)
     cache_text = key_value[:, split_at:][None]
     arrived, cache_video, cache_text = lax.optimization_barrier((arrived, cache_video, cache_text))
 
-    result = jnp.where(is_first, result_0, added(x_half, on_chip, arrived))
-    hidden_video, hidden_text = store_call(result, swap_core(result), (1,) + video.shape, (1,) + text.shape)
+    result = added(base, on_chip, arrived)
+    hidden_video, hidden_text = store_call(result, each(swap_core, result), (1,) + video.shape, (1,) + text.shape)
     return (hidden_video, hidden_text, cache_video, cache_text)
 
 

time: 121 us -> 113 us (0.934)
  waiting for transfers between devices: 20.3 us -> 12.3 us
  starting transfers between devices: 17.4 us -> 22.7 us
  Pallas kernels: 21.6 us -> 18.3 us
  other arithmetic: 2.29 us -> 0.37 us
    ppermute x10 -> x17, waiting for transfers between devices: 20.3 us -> 12.3 us  [swap(): return lax.ppermute(value, ('section', 'mp'), pairs)]
    ppermute x10 -> x17, starting transfers between devices: 17.4 us -> 22.7 us  [swap(): return lax.ppermute(value, ('section', 'mp'), pairs)]
    pallas_call x2, Pallas kernels: 7.5 us -> 4.79 us  [attention_call(): pl.pallas_call(lambda *refs: attention_kernel(*refs, rows=rows, per_dev=p...]
    pallas_call x3, Pallas kernels: 7.68 us -> 5.95 us  [the longest x1 3.98 us: prepare_call(): pl.pallas_call(prepare_kernel, out_shape=(pltpu.VMEM((total, width), jnp....]
  transfers between devices with their start and end apart: 10 -> 17, of which waited for: 7 -> 9; matrix products, arithmetic and copies ran while one was open for 1% -> 2% of each run, Pallas kernels for 4% -> 4%
where the time goes in v3:
time: 113 us; the launch traced here: 112 us
  blocking collectives  54 us (48%)
  starting transfers between devices  22.7 us (20%)
  Pallas kernels  18.3 us (16%)
  waiting for transfers between devices  12.3 us (11%)
  local copies, waits for them, and re-layouts  2.49 us (2%)
  between operations  1.76 us (2%)
    ppermute x17, starting transfers between devices, swap(): return lax.ppermute(value, ('section', 'mp'), pairs)  22.7 us
    all_to_all x2, blocking collectives, body(): lax.all_to_all(attended, 'seq', 0, 0, tiled=True)  20.5 us
    all_to_all x1, blocking collectives, body(): recv_0 = lax.all_to_all(sent_0, 'seq', 0, 0, tiled=True)  20.4 us
    all_to_all x1, blocking collectives, body(): recv_1 = lax.all_to_all(sent_1, 'seq', 0, 0, tiled=True)  13.1 us
    ppermute x17, waiting for transfers between devices, swap(): return lax.ppermute(value, ('section', 'mp'), pairs)  12.3 us
    pallas_call x2, Pallas kernels, attention_call(): pl.pallas_call(lambda *refs: attention_kernel(*refs, rows=rows, per_dev=p...  4.79 us
    pallas_call x1, Pallas kernels, prepare_call(): pl.pallas_call(prepare_kernel, out_shape=(pltpu.VMEM((total, width), jnp....  3.98 us
    pallas_call x1, Pallas kernels, first_call(): pl.pallas_call(lambda *refs: first_kernel(*refs, rows=rows), out_shape=(j...  3.57 us
  transfers between devices with their start and end apart: 17, of which 9 were waited for; matrix products, arithmetic and copies ran while one was open for 2% of the time, Pallas kernels for 4%

profile of v3, /device:TPU:1, one launch (start us, length us, event | category | flops | bytes accessed | tf_op | source)
XLA Modules:
  0.0 112.3 jit_solution(10422953275836950543)
XLA Ops:
  0.6 0.0 copy-start
  1.5 0.8 copy-done
  2.3 0.4 fusion.refs_1_
  2.7 2.6 %collective-permute-start.2 = (f32[1,2304]{1,0:T(1,128)S(1)}, f32[1,2304]{1,0:T(1,128)S(1)}, u32[]{:S(2)}, u32[]{:S(2)}) collective-permute-start(f32[1,2304]{1,0:T(1,128)S(1)} %fusion.refs_1_), channel_id=1, source_target_pairs={{0,3},{1,2},{2,1},{3,0},{64,67},{65,66},{66,65},{67,64},{4,7},{5,6... | collective-permute-start | bytes 27656 | tf_op jit(solution)/shard_map/ppermute | solution.py:33
  5.3 0.2 collective-permute-start.1
  5.5 0.3 collective-permute-start
  5.8 4.0 %prepare.1 = (f32[80,3072]{1,0:T(8,128)S(1)}, bf16[12,48,128]{2,1,0:T(8,128)(2,1)S(1)}, bf16[2,3072,768]{2,1,0:T(8,128)(2,1)S(1)}, bf16[80,768]{1,0:T(8,128)(2,1)S(1)}, bf16[80,768]{1,0:T(8,128)(2,1)S(1)}) custom-call(bf16[2,4,8,3072]{3,2,1,0:T(8,128)(2,1)} %video_ref.1, bf16[2,8,3072]{2,1,0:T(8,128)(2,1)} %text_ref.1, bf16[3,3072,768]{2,1,0:T(8,128)(2,1)} %bitcast.22, ...), custom_call_target="tpu_custom_call" | custom-call | tf_op jit(solution)/shard_map/prepare/pallas_call | solution.py:107
  9.8 0.0 collective-permute-done.2.refs_4_
  9.8 0.0 collective-permute-done.1.refs_3_
  9.8 0.0 collective-permute-done.refs_2_
  9.8 0.0 slice-start
  9.8 0.0 copy-start.1
  9.8 0.0 copy-start.2
  9.9 0.0 slice-start.1
  9.9 3.6 %first_qkv.1 = (bf16[16,168,128]{2,1,0:T(8,128)(2,1)S(1)}, bf16[2,80,768]{2,1,0:T(8,128)(2,1)S(1)}, f32[3,3072]{1,0:T(4,128)S(1)}, bf16[3072,768]{1,0:T(8,128)(2,1)S(1)}) custom-call(f32[80,3072]{1,0:T(8,128)S(1)} %get-tuple-element.31.refs_0_, f32[1,2304]{1,0:T(1,128)S(1)} %fusion.refs_1_, f32[1,2304]{1,0:T(1,128)S(1)} %collective-permute-done.refs_2_, ...), custom_call_target="tpu_custom_call" | custom-call | tf_op jit(solution)/shard_map/first_qkv/pallas_call | solution.py:193
  13.4 20.4 %all_to_all.20.refs_2_.refs_3_ = bf16[16,168,128]{2,1,0:T(8,128)(2,1)S(1)} all-to-all(bf16[16,168,128]{2,1,0:T(8,128)(2,1)S(1)} %get-tuple-element.38), channel_id=1, replica_groups=mesh['section'=2,'seq'=16,'mp'=4] {'seq'}, dimensions={0} | all-to-all | bytes 1376256 | tf_op jit(solution)/shard_map/all_to_all | solution.py:456
  33.9 0.0 copy-done.1
  33.9 0.0 copy-done.2
  33.9 2.4 %attention.2 = bf16[16,40,128]{2,1,0:T(8,128)(2,1)S(1)} custom-call(s32[2,4]{1,0:T(2,128)S(1)} %copy-done.1, s32[2]{0:T(128)S(1)} %copy-done.2, bf16[16,168,128]{2,1,0:T(8,128)(2,1)S(1)} %all_to_all.20.refs_2_.refs_3_, bf16[16,168,128]{2,1,0:T(8,128)(2,1)S(1)} %all_to_all.20.refs_2_.refs_3_), custom_call_target="tpu_custom_call" | custom-call | tf_op jit(solution)/shard_map/attention/pallas_call | solution.py:329
  36.3 10.1 %all_to_all.21.refs_0_ = bf16[16,40,128]{2,1,0:T(8,128)(2,1)S(1)} all-to-all(bf16[16,40,128]{2,1,0:T(8,128)(2,1)S(1)} %attention.2), channel_id=1, replica_groups=mesh['section'=2,'seq'=16,'mp'=4] {'seq'}, dimensions={0} | all-to-all | bytes 327680 | tf_op jit(solution)/shard_map/all_to_all | solution.py:459
  46.4 0.0 slice-done
  46.4 0.0 slice-done.1
  46.4 1.0 out_projection.2
  47.4 2.5 %collective-permute-start.3 = (bf16[80,768]{1,0:T(8,128)(2,1)S(1)}, bf16[80,768]{1,0:T(8,128)(2,1)S(1)}, u32[]{:S(2)}, u32[]{:S(2)}) collective-permute-start(bf16[80,768]{1,0:T(8,128)(2,1)S(1)} %get-tuple-element.40), channel_id=1, source_target_pairs={{0,1},{1,0},{2,3},{3,2},{64,65},{65,64},{66,67},{67,66},{4,5},{5,4... | collective-permute-start | bytes 368648 | tf_op jit(solution)/shard_map/ppermute | solution.py:33
  49.9 0.1 collective-permute-start.6
  50.0 0.9 collective-permute-done.3
  50.9 1.2 %collective-permute-start.4 = (bf16[80,768]{1,0:T(8,128)(2,1)S(1)}, bf16[80,768]{1,0:T(8,128)(2,1)S(1)}, u32[]{:S(2)}, u32[]{:S(2)}) collective-permute-start(bf16[80,768]{1,0:T(8,128)(2,1)S(1)} %add_convert_fusion.7), channel_id=1, source_target_pairs={{0,2},{1,3},{2,0},{3,1},{64,66},{65,67},{66,64},{67,65},{4,6},{5,7... | collective-permute-start | bytes 368648 | tf_op jit(solution)/shard_map/ppermute | solution.py:33
  52.1 0.0 collective-permute-done.6
  52.2 0.4 collective-permute-start.7
  52.6 3.0 %collective-permute-done.4 = bf16[80,768]{1,0:T(8,128)(2,1)S(1)} collective-permute-done((bf16[80,768]{1,0:T(8,128)(2,1)S(1)}, bf16[80,768]{1,0:T(8,128)(2,1)S(1)}, u32[]{:S(2)}, u32[]{:S(2)}) %collective-permute-start.4) | collective-permute-done | bytes 122912 | tf_op jit(solution)/shard_map/ppermute | solution.py:33
  55.6 2.5 %collective-permute-start.5 = (bf16[80,768]{1,0:T(8,128)(2,1)S(1)}, bf16[80,768]{1,0:T(8,128)(2,1)S(1)}, u32[]{:S(2)}, u32[]{:S(2)}) collective-permute-start(bf16[80,768]{1,0:T(8,128)(2,1)S(1)} %add_convert_fusion.6.refs_8_), channel_id=1, source_target_pairs={{0,66},{1,67},{2,64},{3,65},{64,2},{65,3},{66,0},{67,1},{4,70},{5,... | collective-permute-start | bytes 368648 | tf_op jit(solution)/shard_map/ppermute | solution.py:33
  58.1 0.1 collective-permute-done.7
  58.2 2.5 %collective-permute-start.8 = (bf16[80,768]{1,0:T(8,128)(2,1)S(1)}, bf16[80,768]{1,0:T(8,128)(2,1)S(1)}, u32[]{:S(2)}, u32[]{:S(2)}) collective-permute-start(bf16[80,768]{1,0:T(8,128)(2,1)S(1)} %add_convert_fusion.4.refs_9_), channel_id=1, source_target_pairs={{0,66},{1,67},{2,64},{3,65},{64,2},{65,3},{66,0},{67,1},{4,70},{5,... | collective-permute-start | bytes 368648 | tf_op jit(solution)/shard_map/ppermute | solution.py:33
  60.7 0.0 collective-permute-done.5.refs_4_
  60.7 4.2 %collective-permute-start.9 = (bf16[80,768]{1,0:T(8,128)(2,1)S(1)}, bf16[80,768]{1,0:T(8,128)(2,1)S(1)}, u32[]{:S(2)}, u32[]{:S(2)}) collective-permute-start(bf16[80,768]{1,0:T(8,128)(2,1)S(1)} %collective-permute-done.5.refs_4_), channel_id=1, source_target_pairs={{0,1},{1,0},{2,3},{3,2},{64,65},{65,64},{66,67},{67,66},{4,5},{5,4... | collective-permute-start | bytes 368648 | tf_op jit(solution)/shard_map/ppermute | solution.py:33
  64.9 0.0 collective-permute-done.8.refs_5_
  64.9 1.7 %collective-permute-start.10 = (bf16[80,768]{1,0:T(8,128)(2,1)S(1)}, bf16[80,768]{1,0:T(8,128)(2,1)S(1)}, u32[]{:S(2)}, u32[]{:S(2)}) collective-permute-start(bf16[80,768]{1,0:T(8,128)(2,1)S(1)} %collective-permute-done.8.refs_5_), channel_id=1, source_target_pairs={{0,1},{1,0},{2,3},{3,2},{64,65},{65,64},{66,67},{67,66},{4,5},{5,4... | collective-permute-start | bytes 368648 | tf_op jit(solution)/shard_map/ppermute | solution.py:33
  66.6 0.0 collective-permute-done.9.refs_6_
  66.6 1.0 collective-permute-done.10.refs_7_
  67.5 2.9 %second_qkv.1 = (bf16[16,120,128]{2,1,0:T(8,128)(2,1)S(1)}, bf16[2,80,768]{2,1,0:T(8,128)(2,1)S(1)}, bf16[80,768]{1,0:T(8,128)(2,1)S(1)}, bf16[80,768]{1,0:T(8,128)(2,1)S(1)}) custom-call(f32[3,3072]{1,0:T(4,128)S(1)} %get-tuple-element.34.refs_1_.refs_0_, bf16[2,3072,768]{2,1,0:T(8,128)(2,1)S(1)} %get-tuple-element.32.refs_5_.refs_1_, ...), custom_call_target="tpu_custom_call" | custom-call | tf_op jit(solution)/shard_map/second_qkv/pallas_call | solution.py:245
  70.5 13.1 %all_to_all.22.refs_2_ = bf16[16,120,128]{2,1,0:T(8,128)(2,1)S(1)} all-to-all(bf16[16,120,128]{2,1,0:T(8,128)(2,1)S(1)} %get-tuple-element.45), channel_id=1, replica_groups=mesh['section'=2,'seq'=16,'mp'=4] {'seq'}, dimensions={0} | all-to-all | bytes 983040 | tf_op jit(solution)/shard_map/all_to_all | solution.py:466
  83.6 2.4 %attention.3 = bf16[16,40,128]{2,1,0:T(8,128)(2,1)S(1)} custom-call(s32[2,4]{1,0:T(2,128)S(1)} %copy-done.1, s32[2]{0:T(128)S(1)} %copy-done.2, bf16[16,120,128]{2,1,0:T(8,128)(2,1)S(1)} %all_to_all.22.refs_2_, bf16[16,168,128]{2,1,0:T(8,128)(2,1)S(1)} %all_to_all.20.refs_2_.refs_3_), custom_call_target="tpu_custom_call" | custom-call | tf_op jit(solution)/shard_map/attention/pallas_call | solution.py:329
  86.0 10.3 %all_to_all.23.refs_0_ = bf16[16,40,128]{2,1,0:T(8,128)(2,1)S(1)} all-to-all(bf16[16,40,128]{2,1,0:T(8,128)(2,1)S(1)} %attention.3), channel_id=1, replica_groups=mesh['section'=2,'seq'=16,'mp'=4] {'seq'}, dimensions={0} | all-to-all | bytes 327680 | tf_op jit(solution)/shard_map/all_to_all | solution.py:468
  96.3 1.0 out_projection.3
  97.3 2.6 %collective-permute-start.11 = (bf16[80,768]{1,0:T(8,128)(2,1)S(1)}, bf16[80,768]{1,0:T(8,128)(2,1)S(1)}, u32[]{:S(2)}, u32[]{:S(2)}) collective-permute-start(bf16[80,768]{1,0:T(8,128)(2,1)S(1)} %get-tuple-element.47), channel_id=1, source_target_pairs={{0,1},{1,0},{2,3},{3,2},{64,65},{65,64},{66,67},{67,66},{4,5},{5,4... | collective-permute-start | bytes 368648 | tf_op jit(solution)/shard_map/ppermute | solution.py:33
  99.9 0.2 copy.15
  100.1 0.8 slice.8
  100.9 0.0 collective-permute-start.13
  100.9 0.0 collective-permute-done.11
  101.0 0.1 collective-permute-start.12
  101.1 1.2 %collective-permute-done.13 = bf16[80,768]{1,0:T(8,128)(2,1)S(1)} collective-permute-done((bf16[80,768]{1,0:T(8,128)(2,1)S(1)}, bf16[80,768]{1,0:T(8,128)(2,1)S(1)}, u32[]{:S(2)}, u32[]{:S(2)}) %collective-permute-start.13) | collective-permute-done | bytes 122912 | tf_op jit(solution)/shard_map/ppermute | solution.py:33
  102.3 0.3 collective-permute-start.14
  102.6 0.7 slice_bitcast_fusion
  103.3 2.2 %collective-permute-done.12 = bf16[80,768]{1,0:T(8,128)(2,1)S(1)} collective-permute-done((bf16[80,768]{1,0:T(8,128)(2,1)S(1)}, bf16[80,768]{1,0:T(8,128)(2,1)S(1)}, u32[]{:S(2)}, u32[]{:S(2)}) %collective-permute-start.12) | collective-permute-done | bytes 122912 | tf_op jit(solution)/shard_map/ppermute | solution.py:33
  105.4 2.6 %collective-permute-done.14 = bf16[80,768]{1,0:T(8,128)(2,1)S(1)} collective-permute-done((bf16[80,768]{1,0:T(8,128)(2,1)S(1)}, bf16[80,768]{1,0:T(8,128)(2,1)S(1)}, u32[]{:S(2)}, u32[]{:S(2)}) %collective-permute-start.14) | collective-permute-done | bytes 122912 | tf_op jit(solution)/shard_map/ppermute | solution.py:33
  108.1 1.4 %collective-permute-start.15 = (bf16[80,768]{1,0:T(8,128)(2,1)S(1)}, bf16[80,768]{1,0:T(8,128)(2,1)S(1)}, u32[]{:S(2)}, u32[]{:S(2)}) collective-permute-start(bf16[80,768]{1,0:T(8,128)(2,1)S(1)} %add_convert_fusion.1.refs_0_), channel_id=1, source_target_pairs={{0,1},{1,0},{2,3},{3,2},{64,65},{65,64},{66,67},{67,66},{4,5},{5,4... | collective-permute-start | bytes 368648 | tf_op jit(solution)/shard_map/ppermute | solution.py:33
  109.6 0.1 add_convert_fusion.refs_1_
  109.6 0.1 collective-permute-start.16
  109.7 0.8 collective-permute-done.15.refs_2_
  110.5 0.5 collective-permute-done.16.refs_3_
  111.0 1.1 store.1
  (11 shorter events, 0.3 us)
Async XLA Ops:
  0.6 1.7 %copy-start = (bf16[1,512,2304]{2,1,0:T(8,128)(2,1)S(1)}, bf16[1,512,2304]{2,1,0:T(8,128)(2,1)}, u32[]{:S(2)}) copy-start(bf16[1,512,2304]{2,1,0:T(8,128)(2,1)} %param.14) | copy-start | bytes 7077892
  2.7 7.1 %collective-permute-start.2 = (f32[1,2304]{1,0:T(1,128)S(1)}, f32[1,2304]{1,0:T(1,128)S(1)}, u32[]{:S(2)}, u32[]{:S(2)}) collective-permute-start(f32[1,2304]{1,0:T(1,128)S(1)} %fusion.refs_1_), channel_id=1, source_target_pairs={{0,3},{1,2},{2,1},{3,0},{64,67},{65,66},{66,65},{67,64},{4,7},{5,6... | collective-permute-start | bytes 27656 | tf_op jit(solution)/shard_map/ppermute | solution.py:33
  5.3 4.5 %collective-permute-start.1 = (f32[1,2304]{1,0:T(1,128)S(1)}, f32[1,2304]{1,0:T(1,128)S(1)}, u32[]{:S(2)}, u32[]{:S(2)}) collective-permute-start(f32[1,2304]{1,0:T(1,128)S(1)} %fusion.refs_1_), channel_id=1, source_target_pairs={{0,2},{1,3},{2,0},{3,1},{64,66},{65,67},{66,64},{67,65},{4,6},{5,7... | collective-permute-start | bytes 27656 | tf_op jit(solution)/shard_map/ppermute | solution.py:33
  5.5 4.3 %collective-permute-start = (f32[1,2304]{1,0:T(1,128)S(1)}, f32[1,2304]{1,0:T(1,128)S(1)}, u32[]{:S(2)}, u32[]{:S(2)}) collective-permute-start(f32[1,2304]{1,0:T(1,128)S(1)} %fusion.refs_1_), channel_id=1, source_target_pairs={{0,1},{1,0},{2,3},{3,2},{64,65},{65,64},{66,67},{67,66},{4,5},{5,4... | collective-permute-start | bytes 27656 | tf_op jit(solution)/shard_map/ppermute | solution.py:33
  9.8 36.6 %slice-start = ((s8[4718592]{0:T(1024)(128)(4,1)}), s8[4194304]{0:T(1024)(128)(4,1)S(1)}, s32[]{:S(2)}) async-start(s8[4718592]{0:T(1024)(128)(4,1)} %bitcast.17), calls=%async_computation.4 | async-start | bytes 8388608
  9.8 24.0 %copy-start.1 = (s32[2,4]{1,0:T(2,128)S(1)}, s32[2,4]{1,0:T(2,128)}, u32[]{:S(2)}) copy-start(s32[2,4]{1,0:T(2,128)} %refs_0_.3) | copy-start | bytes 100
  9.8 24.0 %copy-start.2 = (s32[2]{0:T(128)S(1)}, s32[2]{0:T(128)}, u32[]{:S(2)}) copy-start(s32[2]{0:T(128)} %refs_1_.3) | copy-start | bytes 28
  9.9 36.5 %slice-start.1 = ((s8[4718592]{0:T(1024)(128)(4,1)}), s8[524288]{0:T(1024)(128)(4,1)S(1)}, s32[]{:S(2)}) async-start(s8[4718592]{0:T(1024)(128)(4,1)} %bitcast.17), calls=%async_computation.5 | async-start | bytes 1048576
  47.4 3.5 %collective-permute-start.3 = (bf16[80,768]{1,0:T(8,128)(2,1)S(1)}, bf16[80,768]{1,0:T(8,128)(2,1)S(1)}, u32[]{:S(2)}, u32[]{:S(2)}) collective-permute-start(bf16[80,768]{1,0:T(8,128)(2,1)S(1)} %get-tuple-element.40), channel_id=1, source_target_pairs={{0,1},{1,0},{2,3},{3,2},{64,65},{65,64},{66,67},{67,66},{4,5},{5,4... | collective-permute-start | bytes 368648 | tf_op jit(solution)/shard_map/ppermute | solution.py:33
  49.9 2.2 %collective-permute-start.6 = (bf16[80,768]{1,0:T(8,128)(2,1)S(1)}, bf16[80,768]{1,0:T(8,128)(2,1)S(1)}, u32[]{:S(2)}, u32[]{:S(2)}) collective-permute-start(bf16[80,768]{1,0:T(8,128)(2,1)S(1)} %get-tuple-element.43), channel_id=1, source_target_pairs={{0,1},{1,0},{2,3},{3,2},{64,65},{65,64},{66,67},{67,66},{4,5},{5,4... | collective-permute-start | bytes 368648 | tf_op jit(solution)/shard_map/ppermute | solution.py:33
  50.9 4.6 %collective-permute-start.4 = (bf16[80,768]{1,0:T(8,128)(2,1)S(1)}, bf16[80,768]{1,0:T(8,128)(2,1)S(1)}, u32[]{:S(2)}, u32[]{:S(2)}) collective-permute-start(bf16[80,768]{1,0:T(8,128)(2,1)S(1)} %add_convert_fusion.7), channel_id=1, source_target_pairs={{0,2},{1,3},{2,0},{3,1},{64,66},{65,67},{66,64},{67,65},{4,6},{5,7... | collective-permute-start | bytes 368648 | tf_op jit(solution)/shard_map/ppermute | solution.py:33
  52.2 6.0 %collective-permute-start.7 = (bf16[80,768]{1,0:T(8,128)(2,1)S(1)}, bf16[80,768]{1,0:T(8,128)(2,1)S(1)}, u32[]{:S(2)}, u32[]{:S(2)}) collective-permute-start(bf16[80,768]{1,0:T(8,128)(2,1)S(1)} %add_convert_fusion.5), channel_id=1, source_target_pairs={{0,2},{1,3},{2,0},{3,1},{64,66},{65,67},{66,64},{67,65},{4,6},{5,7... | collective-permute-start | bytes 368648 | tf_op jit(solution)/shard_map/ppermute | solution.py:33
  55.6 5.1 %collective-permute-start.5 = (bf16[80,768]{1,0:T(8,128)(2,1)S(1)}, bf16[80,768]{1,0:T(8,128)(2,1)S(1)}, u32[]{:S(2)}, u32[]{:S(2)}) collective-permute-start(bf16[80,768]{1,0:T(8,128)(2,1)S(1)} %add_convert_fusion.6.refs_8_), channel_id=1, source_target_pairs={{0,66},{1,67},{2,64},{3,65},{64,2},{65,3},{66,0},{67,1},{4,70},{5,... | collective-permute-start | bytes 368648 | tf_op jit(solution)/shard_map/ppermute | solution.py:33
  58.2 6.6 %collective-permute-start.8 = (bf16[80,768]{1,0:T(8,128)(2,1)S(1)}, bf16[80,768]{1,0:T(8,128)(2,1)S(1)}, u32[]{:S(2)}, u32[]{:S(2)}) collective-permute-start(bf16[80,768]{1,0:T(8,128)(2,1)S(1)} %add_convert_fusion.4.refs_9_), channel_id=1, source_target_pairs={{0,66},{1,67},{2,64},{3,65},{64,2},{65,3},{66,0},{67,1},{4,70},{5,... | collective-permute-start | bytes 368648 | tf_op jit(solution)/shard_map/ppermute | solution.py:33
  60.7 5.9 %collective-permute-start.9 = (bf16[80,768]{1,0:T(8,128)(2,1)S(1)}, bf16[80,768]{1,0:T(8,128)(2,1)S(1)}, u32[]{:S(2)}, u32[]{:S(2)}) collective-permute-start(bf16[80,768]{1,0:T(8,128)(2,1)S(1)} %collective-permute-done.5.refs_4_), channel_id=1, source_target_pairs={{0,1},{1,0},{2,3},{3,2},{64,65},{65,64},{66,67},{67,66},{4,5},{5,4... | collective-permute-start | bytes 368648 | tf_op jit(solution)/shard_map/ppermute | solution.py:33
  64.9 2.7 %collective-permute-start.10 = (bf16[80,768]{1,0:T(8,128)(2,1)S(1)}, bf16[80,768]{1,0:T(8,128)(2,1)S(1)}, u32[]{:S(2)}, u32[]{:S(2)}) collective-permute-start(bf16[80,768]{1,0:T(8,128)(2,1)S(1)} %collective-permute-done.8.refs_5_), channel_id=1, source_target_pairs={{0,1},{1,0},{2,3},{3,2},{64,65},{65,64},{66,67},{67,66},{4,5},{5,4... | collective-permute-start | bytes 368648 | tf_op jit(solution)/shard_map/ppermute | solution.py:33
  97.3 3.6 %collective-permute-start.11 = (bf16[80,768]{1,0:T(8,128)(2,1)S(1)}, bf16[80,768]{1,0:T(8,128)(2,1)S(1)}, u32[]{:S(2)}, u32[]{:S(2)}) collective-permute-start(bf16[80,768]{1,0:T(8,128)(2,1)S(1)} %get-tuple-element.47), channel_id=1, source_target_pairs={{0,1},{1,0},{2,3},{3,2},{64,65},{65,64},{66,67},{67,66},{4,5},{5,4... | collective-permute-start | bytes 368648 | tf_op jit(solution)/shard_map/ppermute | solution.py:33
  100.9 1.3 %collective-permute-start.13 = (bf16[80,768]{1,0:T(8,128)(2,1)S(1)}, bf16[80,768]{1,0:T(8,128)(2,1)S(1)}, u32[]{:S(2)}, u32[]{:S(2)}) collective-permute-start(bf16[80,768]{1,0:T(8,128)(2,1)S(1)} %get-tuple-element.49), channel_id=1, source_target_pairs={{0,1},{1,0},{2,3},{3,2},{64,65},{65,64},{66,67},{67,66},{4,5},{5,4... | collective-permute-start | bytes 368648 | tf_op jit(solution)/shard_map/ppermute | solution.py:33
  101.0 4.5 %collective-permute-start.12 = (bf16[80,768]{1,0:T(8,128)(2,1)S(1)}, bf16[80,768]{1,0:T(8,128)(2,1)S(1)}, u32[]{:S(2)}, u32[]{:S(2)}) collective-permute-start(bf16[80,768]{1,0:T(8,128)(2,1)S(1)} %add_convert_fusion.3), channel_id=1, source_target_pairs={{0,2},{1,3},{2,0},{3,1},{64,66},{65,67},{66,64},{67,65},{4,6},{5,7... | collective-permute-start | bytes 368648 | tf_op jit(solution)/shard_map/ppermute | solution.py:33
  102.3 5.8 %collective-permute-start.14 = (bf16[80,768]{1,0:T(8,128)(2,1)S(1)}, bf16[80,768]{1,0:T(8,128)(2,1)S(1)}, u32[]{:S(2)}, u32[]{:S(2)}) collective-permute-start(bf16[80,768]{1,0:T(8,128)(2,1)S(1)} %add_convert_fusion.2), channel_id=1, source_target_pairs={{0,2},{1,3},{2,0},{3,1},{64,66},{65,67},{66,64},{67,65},{4,6},{5,7... | collective-permute-start | bytes 368648 | tf_op jit(solution)/shard_map/ppermute | solution.py:33
  108.1 2.4 %collective-permute-start.15 = (bf16[80,768]{1,0:T(8,128)(2,1)S(1)}, bf16[80,768]{1,0:T(8,128)(2,1)S(1)}, u32[]{:S(2)}, u32[]{:S(2)}) collective-permute-start(bf16[80,768]{1,0:T(8,128)(2,1)S(1)} %add_convert_fusion.1.refs_0_), channel_id=1, source_target_pairs={{0,1},{1,0},{2,3},{3,2},{64,65},{65,64},{66,67},{67,66},{4,5},{5,4... | collective-permute-start | bytes 368648 | tf_op jit(solution)/shard_map/ppermute | solution.py:33
  109.6 1.4 %collective-permute-start.16 = (bf16[80,768]{1,0:T(8,128)(2,1)S(1)}, bf16[80,768]{1,0:T(8,128)(2,1)S(1)}, u32[]{:S(2)}, u32[]{:S(2)}) collective-permute-start(bf16[80,768]{1,0:T(8,128)(2,1)S(1)} %add_convert_fusion.refs_1_), channel_id=1, source_target_pairs={{0,1},{1,0},{2,3},{3,2},{64,65},{65,64},{66,67},{67,66},{4,5},{5,4... | collective-permute-start | bytes 368648 | tf_op jit(solution)/shard_map/ppermute | solution.py:33

commit v4 on v3

--- a/solution.py
+++ b/solution.py
@@ -307,9 +307,9 @@
             (((1,), (1,)), ((), ())),
             preferred_element_type=jnp.float32,
         )
-        scores = scores + bias
+        scores = scores * factor + bias
         top = jnp.max(scores, axis=-1, keepdims=True)
-        weights = jnp.exp2((scores - top) * factor).astype(jnp.bfloat16)
+        weights = jnp.exp2(scores - top).astype(jnp.bfloat16)
         acc = jnp.dot(weights, jnp.concatenate([values, ones], axis=1), preferred_element_type=jnp.float32)
         acc = acc[:, :LANES] / acc[:, LANES:]
         for index, group in enumerate(members):
@@ -379,35 +379,81 @@
     )(recv, mod, weight)
 
 
+def pick_kernel(arrived_ref, own_ref, o_ref):
+    @pl.when(lax.axis_index("section") == 0)
+    def _():
+        o_ref[...] = own_ref[...]
+
+    @pl.when(lax.axis_index("section") != 0)
+    def _():
+        o_ref[...] = arrived_ref[...]
+
+
+def pick_call(arrived, own):
+    return pl.pallas_call(
+        pick_kernel,
+        out_shape=pltpu.VMEM(own.shape, own.dtype),
+        in_specs=[VMEM, VMEM],
+        out_specs=VMEM,
+        compiler_params=PARAMS,
+        name="pick",
+    )(arrived, own)
+
+
+def cache_kernel(kv_ref, video_ref, text_ref):
+    _, requests, patches, per_dev, _, _ = video_ref.shape
+    row = 0
+    for request in range(requests):
+        for patch in range(patches + 1):
+            for kind in range(2):
+                values = kv_ref[kind, row : row + per_dev, :]
+                if patch < patches:
+                    video_ref[0, request, patch, :, kind, :] = values
+                else:
+                    text_ref[0, request, :, kind, :] = values
+            row += per_dev
+
+
+def cache_call(kv, video_shape, requests):
+    per_dev, columns = video_shape[3], video_shape[5]
+    return pl.pallas_call(
+        cache_kernel,
+        out_shape=(
+            jax.ShapeDtypeStruct(video_shape, jnp.bfloat16),
+            jax.ShapeDtypeStruct((1, requests, per_dev, 2, columns), jnp.bfloat16),
+        ),
+        in_specs=[VMEM],
+        out_specs=(VMEM, VMEM),
+        compiler_params=PARAMS,
+        name="cache",
+    )(kv)
+
+
 def store_kernel(*refs):
     *pieces, video_ref, text_ref, sems = refs
-    _, requests, patches, per_dev, _ = video_ref.shape
-    span = pieces[0].shape[1]
+    patches = video_ref.shape[2]
+    span = pieces[0].shape[-1]
     half = span * CHUNKS
     core = lax.axis_index("mp") % 2
     copies = []
     for side, source in enumerate(pieces):
         index = core if side < CHUNKS else 1 - core
         at = pl.ds(pl.multiple_of(index * half + side % CHUNKS * span, LANES), span)
-        row = 0
-        for request in range(requests):
-            for patch in range(patches + 1):
-                target = (
-                    video_ref.at[0, request, patch, :, at]
-                    if patch < patches
-                    else text_ref.at[0, request, :, at]
-                )
-                copy = pltpu.make_async_copy(
-                    source.at[pl.ds(row, per_dev), :], target, sems.at[side, row // per_dev]
-                )
-                copy.start()
-                copies.append(copy)
-                row += per_dev
+        copies.append(
+            pltpu.make_async_copy(
+                source.at[:, pl.ds(0, patches)], video_ref.at[0, :, :, :, at], sems.at[side, 0]
+            )
+        )
+        copies.append(pltpu.make_async_copy(source.at[:, patches], text_ref.at[0, :, :, at], sems.at[side, 1]))
+    for copy in copies:
+        copy.start()
     for copy in copies:
         copy.wait()
 
 
 def store_call(mine, other, video_shape, text_shape):
+    _, requests, patches, per_dev, _ = video_shape
+    pieces = [piece.reshape(requests, patches + 1, per_dev, -1) for piece in mine + other]
     return pl.pallas_call(
         store_kernel,
         out_shape=(
@@ -416,17 +462,16 @@
         ),
         in_specs=[VMEM] * (2 * CHUNKS),
         out_specs=(ANY, ANY),
-        scratch_shapes=[pltpu.SemaphoreType.DMA((2 * CHUNKS, mine[0].shape[0] // video_shape[3]))],
+        scratch_shapes=[pltpu.SemaphoreType.DMA((2 * CHUNKS, 2))],
         compiler_params=PARAMS,
         name="store",
-    )(*mine, *other)
+    )(*pieces)
 
 
 def body(video, text, patch_lengths, text_len, timestep, w_mod, w_qkv, w_out, stale_cache):
     devices = lax.axis_size("seq")
     requests, patches, per_dev, _ = video.shape
-    columns = w_out.shape[1]
-    blocks = columns // LANES
+    blocks = w_out.shape[1] // LANES
     rows = patches * per_dev + text.shape[1]
 
     own_mod = modulation(timestep, w_mod[0])
@@ -457,9 +502,10 @@
     weight_out = w_out[0]
     attended = attention_call(patch_lengths, text_len, recv_0, recv_0, None, rows, per_dev, blocks)
     on_chip = reduced(lax.all_to_all(attended, "seq", 0, 0, tiled=True), weight_out, mod, False)
-    result_0 = added(x_half, on_chip, each(swap_chip, on_chip))
-
-    x_half = each(next_section, result_0)
+    crossed = pick_call(next_section(on_chip[1]), on_chip[1])
+    result_0 = added(x_half, [on_chip[0], crossed], [swap_chip(on_chip[0]), swap_chip(crossed)])
+
+    x_half = [next_section(result_0[0]), result_0[1]]
     sent_1, key_value, *base = second_call(
         x_half, each(swap_core, x_half), result_0, kv_0, mod, weight_qk, weight_v, rows, devices
     )
@@ -467,13 +513,9 @@
     attended = attention_call(patch_lengths, text_len, recv_1, recv_0, None, rows, per_dev, blocks)
     on_chip = reduced(lax.all_to_all(attended, "seq", 0, 0, tiled=True), weight_out, mod, True)
     arrived = each(swap_chip, on_chip)
-
-    key_value = key_value.reshape(2, requests, rows, columns).transpose(1, 2, 0, 3)
-    split_at = patches * per_dev
-    cache_video = key_value[:, :split_at].reshape(1, requests, patches, per_dev, 2, columns)
-    cache_text = key_value[:, split_at:][None]
-    arrived, cache_video, cache_text = lax.optimization_barrier((arrived, cache_video, cache_text))
-
+    arrived[0], key_value = lax.optimization_barrier((arrived[0], key_value))
+
+    cache_video, cache_text = cache_call(key_value, (1,) + stale_cache.shape[1:], requests)
     result = added(base, on_chip, arrived)
     hidden_video, hidden_text = store_call(result, each(swap_core, result), (1,) + video.shape, (1,) + text.shape)
     return (hidden_video, hidden_text, cache_video, cache_text)

time: 113 us -> 110 us (0.973)
  waiting for transfers between devices: 12.3 us -> 10.6 us
  local copies, waits for them, and re-layouts: 2.49 us -> 0.83 us
    ppermute x17, waiting for transfers between devices: 12.3 us -> 10.6 us  [swap(): return lax.ppermute(value, ('section', 'mp'), pairs)]
  transfers between devices with their start and end apart: 17 -> 17, of which waited for: 9 -> 9; matrix products, arithmetic and copies ran while one was open for 2% -> 0% of each run, Pallas kernels for 4% -> 4%
where the time goes in v4:
time: 110 us
  blocking collectives  54 us (49%)
  starting transfers between devices  22.7 us (21%)
  Pallas kernels  18.8 us (17%)
  waiting for transfers between devices  10.6 us (10%)
  between operations  1.78 us (2%)
    ppermute x17, starting transfers between devices, swap(): return lax.ppermute(value, ('section', 'mp'), pairs)  22.7 us
    all_to_all x2, blocking collectives, body(): lax.all_to_all(attended, 'seq', 0, 0, tiled=True)  20.5 us
    all_to_all x1, blocking collectives, body(): recv_0 = lax.all_to_all(sent_0, 'seq', 0, 0, tiled=True)  20.4 us
    all_to_all x1, blocking collectives, body(): recv_1 = lax.all_to_all(sent_1, 'seq', 0, 0, tiled=True)  13.1 us
    ppermute x17, waiting for transfers between devices, swap(): return lax.ppermute(value, ('section', 'mp'), pairs)  10.6 us
    pallas_call x2, Pallas kernels, attention_call(): pl.pallas_call(lambda *refs: attention_kernel(*refs, rows=rows, per_dev=p...  4.77 us
    pallas_call x1, Pallas kernels, prepare_call(): pl.pallas_call(prepare_kernel, out_shape=(pltpu.VMEM((total, width), jnp....  3.98 us
    pallas_call x1, Pallas kernels, first_call(): pl.pallas_call(lambda *refs: first_kernel(*refs, rows=rows), out_shape=(j...  3.56 us
  transfers between devices with their start and end apart: 17, of which 9 were waited for; matrix products, arithmetic and copies ran while one was open for 0% of the time, Pallas kernels for 4%

profile of v4, /device:TPU:1, one launch (start us, length us, event | category | flops | bytes accessed | tf_op | source)
XLA Modules:
  0.0 109.5 jit_solution(13231291961671862203)
XLA Ops:
  0.6 0.0 copy-start
  1.5 0.8 copy-done
  2.3 0.4 fusion.refs_1_
  2.7 2.6 %collective-permute-start.2 = (f32[1,2304]{1,0:T(1,128)S(1)}, f32[1,2304]{1,0:T(1,128)S(1)}, u32[]{:S(2)}, u32[]{:S(2)}) collective-permute-start(f32[1,2304]{1,0:T(1,128)S(1)} %fusion.refs_1_), channel_id=1, source_target_pairs={{0,3},{1,2},{2,1},{3,0},{64,67},{65,66},{66,65},{67,64},{4,7},{5,6... | collective-permute-start | bytes 27656 | tf_op jit(solution)/shard_map/ppermute | solution.py:33
  5.3 0.2 collective-permute-start.1
  5.5 0.3 collective-permute-start
  5.8 4.0 %prepare.1 = (f32[80,3072]{1,0:T(8,128)S(1)}, bf16[12,48,128]{2,1,0:T(8,128)(2,1)S(1)}, bf16[2,3072,768]{2,1,0:T(8,128)(2,1)S(1)}, bf16[80,768]{1,0:T(8,128)(2,1)S(1)}, bf16[80,768]{1,0:T(8,128)(2,1)S(1)}) custom-call(bf16[2,4,8,3072]{3,2,1,0:T(8,128)(2,1)} %video_ref.1, bf16[2,8,3072]{2,1,0:T(8,128)(2,1)} %text_ref.1, bf16[3,3072,768]{2,1,0:T(8,128)(2,1)} %bitcast.22, ...), custom_call_target="tpu_custom_call" | custom-call | tf_op jit(solution)/shard_map/prepare/pallas_call | solution.py:107
  9.8 0.0 collective-permute-done.2.refs_4_
  9.8 0.0 collective-permute-done.1.refs_3_
  9.8 0.0 collective-permute-done.refs_2_
  9.8 0.0 slice-start
  9.8 0.0 copy-start.1
  9.8 0.0 copy-start.2
  9.9 0.0 slice-start.1
  9.9 3.6 %first_qkv.1 = (bf16[16,168,128]{2,1,0:T(8,128)(2,1)S(1)}, bf16[2,80,768]{2,1,0:T(8,128)(2,1)S(1)}, f32[3,3072]{1,0:T(4,128)S(1)}, bf16[3072,768]{1,0:T(8,128)(2,1)S(1)}) custom-call(f32[80,3072]{1,0:T(8,128)S(1)} %get-tuple-element.31.refs_0_, f32[1,2304]{1,0:T(1,128)S(1)} %fusion.refs_1_, f32[1,2304]{1,0:T(1,128)S(1)} %collective-permute-done.refs_2_, ...), custom_call_target="tpu_custom_call" | custom-call | tf_op jit(solution)/shard_map/first_qkv/pallas_call | solution.py:193
  13.4 20.4 %all_to_all.20.refs_2_.refs_3_ = bf16[16,168,128]{2,1,0:T(8,128)(2,1)S(1)} all-to-all(bf16[16,168,128]{2,1,0:T(8,128)(2,1)S(1)} %get-tuple-element.38), channel_id=1, replica_groups=mesh['section'=2,'seq'=16,'mp'=4] {'seq'}, dimensions={0} | all-to-all | bytes 1376256 | tf_op jit(solution)/shard_map/all_to_all | solution.py:501
  33.9 0.0 copy-done.1
  33.9 0.0 copy-done.2
  33.9 2.4 %attention.2 = bf16[16,40,128]{2,1,0:T(8,128)(2,1)S(1)} custom-call(s32[2,4]{1,0:T(2,128)S(1)} %copy-done.1, s32[2]{0:T(128)S(1)} %copy-done.2, bf16[16,168,128]{2,1,0:T(8,128)(2,1)S(1)} %all_to_all.20.refs_2_.refs_3_, bf16[16,168,128]{2,1,0:T(8,128)(2,1)S(1)} %all_to_all.20.refs_2_.refs_3_), custom_call_target="tpu_custom_call" | custom-call | tf_op jit(solution)/shard_map/attention/pallas_call | solution.py:329
  36.2 10.1 %all_to_all.21.refs_0_ = bf16[16,40,128]{2,1,0:T(8,128)(2,1)S(1)} all-to-all(bf16[16,40,128]{2,1,0:T(8,128)(2,1)S(1)} %attention.2), channel_id=1, replica_groups=mesh['section'=2,'seq'=16,'mp'=4] {'seq'}, dimensions={0} | all-to-all | bytes 327680 | tf_op jit(solution)/shard_map/all_to_all | solution.py:504
  46.4 0.0 slice-done
  46.4 0.0 slice-done.1
  46.4 1.0 out_projection.2
  47.4 2.5 %collective-permute-start.3 = (bf16[80,768]{1,0:T(8,128)(2,1)S(1)}, bf16[80,768]{1,0:T(8,128)(2,1)S(1)}, u32[]{:S(2)}, u32[]{:S(2)}) collective-permute-start(bf16[80,768]{1,0:T(8,128)(2,1)S(1)} %get-tuple-element.40), channel_id=1, source_target_pairs={{0,1},{1,0},{2,3},{3,2},{64,65},{65,64},{66,67},{67,66},{4,5},{5,4... | collective-permute-start | bytes 368648 | tf_op jit(solution)/shard_map/ppermute | solution.py:33
  49.9 0.1 collective-permute-start.6
  50.0 0.9 collective-permute-done.3
  50.9 1.2 %collective-permute-start.4 = (bf16[80,768]{1,0:T(8,128)(2,1)S(1)}, bf16[80,768]{1,0:T(8,128)(2,1)S(1)}, u32[]{:S(2)}, u32[]{:S(2)}) collective-permute-start(bf16[80,768]{1,0:T(8,128)(2,1)S(1)} %add_convert_fusion.7), channel_id=1, source_target_pairs={{0,2},{1,3},{2,0},{3,1},{64,66},{65,67},{66,64},{67,65},{4,6},{5,7... | collective-permute-start | bytes 368648 | tf_op jit(solution)/shard_map/ppermute | solution.py:33
  52.1 0.0 collective-permute-done.6
  52.2 1.9 %collective-permute-start.7 = (bf16[80,768]{1,0:T(8,128)(2,1)S(1)}, bf16[80,768]{1,0:T(8,128)(2,1)S(1)}, u32[]{:S(2)}, u32[]{:S(2)}) collective-permute-start(bf16[80,768]{1,0:T(8,128)(2,1)S(1)} %add_convert_fusion.5.own_ref), channel_id=1, source_target_pairs={{0,66},{1,67},{2,64},{3,65},{64,2},{65,3},{66,0},{67,1},{4,70},{5,... | collective-permute-start | bytes 368648 | tf_op jit(solution)/shard_map/ppermute | solution.py:33
  54.1 1.5 %collective-permute-done.4 = bf16[80,768]{1,0:T(8,128)(2,1)S(1)} collective-permute-done((bf16[80,768]{1,0:T(8,128)(2,1)S(1)}, bf16[80,768]{1,0:T(8,128)(2,1)S(1)}, u32[]{:S(2)}, u32[]{:S(2)}) %collective-permute-start.4) | collective-permute-done | bytes 122912 | tf_op jit(solution)/shard_map/ppermute | solution.py:33
  55.5 0.1 add_convert_fusion.6.refs_8_
  55.6 2.5 %collective-permute-start.5 = (bf16[80,768]{1,0:T(8,128)(2,1)S(1)}, bf16[80,768]{1,0:T(8,128)(2,1)S(1)}, u32[]{:S(2)}, u32[]{:S(2)}) collective-permute-start(bf16[80,768]{1,0:T(8,128)(2,1)S(1)} %add_convert_fusion.6.refs_8_), channel_id=1, source_target_pairs={{0,66},{1,67},{2,64},{3,65},{64,2},{65,3},{66,0},{67,1},{4,70},{5,... | collective-permute-start | bytes 368648 | tf_op jit(solution)/shard_map/ppermute | solution.py:33
  58.1 0.0 collective-permute-done.7.arrived_ref
  58.1 0.1 collective-permute-start.8
  58.2 2.4 %collective-permute-done.5.refs_4_ = bf16[80,768]{1,0:T(8,128)(2,1)S(1)} collective-permute-done((bf16[80,768]{1,0:T(8,128)(2,1)S(1)}, bf16[80,768]{1,0:T(8,128)(2,1)S(1)}, u32[]{:S(2)}, u32[]{:S(2)}) %collective-permute-start.5) | collective-permute-done | bytes 122912 | tf_op jit(solution)/shard_map/ppermute | solution.py:33
  60.6 2.3 %collective-permute-start.9 = (bf16[80,768]{1,0:T(8,128)(2,1)S(1)}, bf16[80,768]{1,0:T(8,128)(2,1)S(1)}, u32[]{:S(2)}, u32[]{:S(2)}) collective-permute-start(bf16[80,768]{1,0:T(8,128)(2,1)S(1)} %collective-permute-done.5.refs_4_), channel_id=1, source_target_pairs={{0,1},{1,0},{2,3},{3,2},{64,65},{65,64},{66,67},{67,66},{4,5},{5,4... | collective-permute-start | bytes 368648 | tf_op jit(solution)/shard_map/ppermute | solution.py:33
  63.0 0.0 collective-permute-done.8
  63.0 0.1 add_convert_fusion.4.refs_5_.refs_9_
  63.0 1.6 %collective-permute-start.10 = (bf16[80,768]{1,0:T(8,128)(2,1)S(1)}, bf16[80,768]{1,0:T(8,128)(2,1)S(1)}, u32[]{:S(2)}, u32[]{:S(2)}) collective-permute-start(bf16[80,768]{1,0:T(8,128)(2,1)S(1)} %add_convert_fusion.4.refs_5_.refs_9_), channel_id=1, source_target_pairs={{0,1},{1,0},{2,3},{3,2},{64,65},{65,64},{66,67},{67,66},{4,5},{5,4... | collective-permute-start | bytes 368648 | tf_op jit(solution)/shard_map/ppermute | solution.py:33
  64.7 0.0 collective-permute-done.9.refs_6_
  64.7 1.0 collective-permute-done.10.refs_7_
  65.6 2.9 %second_qkv.1 = (bf16[16,120,128]{2,1,0:T(8,128)(2,1)S(1)}, bf16[2,80,768]{2,1,0:T(8,128)(2,1)S(1)}, bf16[80,768]{1,0:T(8,128)(2,1)S(1)}, bf16[80,768]{1,0:T(8,128)(2,1)S(1)}) custom-call(f32[3,3072]{1,0:T(4,128)S(1)} %get-tuple-element.34.refs_1_.refs_0_, bf16[2,3072,768]{2,1,0:T(8,128)(2,1)S(1)} %get-tuple-element.32.refs_5_.refs_1_, ...), custom_call_target="tpu_custom_call" | custom-call | tf_op jit(solution)/shard_map/second_qkv/pallas_call | solution.py:245
  68.6 13.1 %all_to_all.22.refs_2_ = bf16[16,120,128]{2,1,0:T(8,128)(2,1)S(1)} all-to-all(bf16[16,120,128]{2,1,0:T(8,128)(2,1)S(1)} %get-tuple-element.45), channel_id=1, replica_groups=mesh['section'=2,'seq'=16,'mp'=4] {'seq'}, dimensions={0} | all-to-all | bytes 983040 | tf_op jit(solution)/shard_map/all_to_all | solution.py:512
  81.7 2.4 %attention.3 = bf16[16,40,128]{2,1,0:T(8,128)(2,1)S(1)} custom-call(s32[2,4]{1,0:T(2,128)S(1)} %copy-done.1, s32[2]{0:T(128)S(1)} %copy-done.2, bf16[16,120,128]{2,1,0:T(8,128)(2,1)S(1)} %all_to_all.22.refs_2_, bf16[16,168,128]{2,1,0:T(8,128)(2,1)S(1)} %all_to_all.20.refs_2_.refs_3_), custom_call_target="tpu_custom_call" | custom-call | tf_op jit(solution)/shard_map/attention/pallas_call | solution.py:329
  84.1 10.3 %all_to_all.23.refs_0_ = bf16[16,40,128]{2,1,0:T(8,128)(2,1)S(1)} all-to-all(bf16[16,40,128]{2,1,0:T(8,128)(2,1)S(1)} %attention.3), channel_id=1, replica_groups=mesh['section'=2,'seq'=16,'mp'=4] {'seq'}, dimensions={0} | all-to-all | bytes 327680 | tf_op jit(solution)/shard_map/all_to_all | solution.py:514
  94.4 1.0 out_projection.3
  95.4 2.6 %collective-permute-start.11 = (bf16[80,768]{1,0:T(8,128)(2,1)S(1)}, bf16[80,768]{1,0:T(8,128)(2,1)S(1)}, u32[]{:S(2)}, u32[]{:S(2)}) collective-permute-start(bf16[80,768]{1,0:T(8,128)(2,1)S(1)} %get-tuple-element.47), channel_id=1, source_target_pairs={{0,1},{1,0},{2,3},{3,2},{64,65},{65,64},{66,67},{67,66},{4,5},{5,4... | collective-permute-start | bytes 368648 | tf_op jit(solution)/shard_map/ppermute | solution.py:33
  98.0 0.1 collective-permute-start.13
  98.1 0.9 collective-permute-done.11
  99.0 0.1 collective-permute-start.12
  99.1 0.2 collective-permute-done.13
  99.4 1.3 %collective-permute-start.14 = (bf16[80,768]{1,0:T(8,128)(2,1)S(1)}, bf16[80,768]{1,0:T(8,128)(2,1)S(1)}, u32[]{:S(2)}, u32[]{:S(2)}) collective-permute-start(bf16[80,768]{1,0:T(8,128)(2,1)S(1)} %add_convert_fusion.1), channel_id=1, source_target_pairs={{0,2},{1,3},{2,0},{3,1},{64,66},{65,67},{66,64},{67,65},{4,6},{5,7... | collective-permute-start | bytes 368648 | tf_op jit(solution)/shard_map/ppermute | solution.py:33
  100.7 3.0 %collective-permute-done.12 = bf16[80,768]{1,0:T(8,128)(2,1)S(1)} collective-permute-done((bf16[80,768]{1,0:T(8,128)(2,1)S(1)}, bf16[80,768]{1,0:T(8,128)(2,1)S(1)}, u32[]{:S(2)}, u32[]{:S(2)}) %collective-permute-start.12) | collective-permute-done | bytes 122912 | tf_op jit(solution)/shard_map/ppermute | solution.py:33
  103.7 2.1 %collective-permute-start.15 = (bf16[80,768]{1,0:T(8,128)(2,1)S(1)}, bf16[80,768]{1,0:T(8,128)(2,1)S(1)}, u32[]{:S(2)}, u32[]{:S(2)}) collective-permute-start(bf16[80,768]{1,0:T(8,128)(2,1)S(1)} %add_convert_fusion.2), channel_id=1, source_target_pairs={{0,1},{1,0},{2,3},{3,2},{64,65},{65,64},{66,67},{67,66},{4,5},{5,4... | collective-permute-start | bytes 368648 | tf_op jit(solution)/shard_map/ppermute | solution.py:33
  105.7 0.5 collective-permute-done.14
  106.3 0.1 add_convert_fusion
  106.3 1.3 %collective-permute-start.16 = (bf16[80,768]{1,0:T(8,128)(2,1)S(1)}, bf16[80,768]{1,0:T(8,128)(2,1)S(1)}, u32[]{:S(2)}, u32[]{:S(2)}) collective-permute-start(bf16[80,768]{1,0:T(8,128)(2,1)S(1)} %add_convert_fusion), channel_id=1, source_target_pairs={{0,1},{1,0},{2,3},{3,2},{64,65},{65,64},{66,67},{67,66},{4,5},{5,4... | collective-permute-start | bytes 368648 | tf_op jit(solution)/shard_map/ppermute | solution.py:33
  107.6 0.8 cache.1
  108.4 0.0 collective-permute-done.15
  108.4 0.2 collective-permute-done.16
  108.6 0.8 store.1
  (10 shorter events, 0.2 us)
Async XLA Ops:
  0.6 1.7 %copy-start = (bf16[1,512,2304]{2,1,0:T(8,128)(2,1)S(1)}, bf16[1,512,2304]{2,1,0:T(8,128)(2,1)}, u32[]{:S(2)}) copy-start(bf16[1,512,2304]{2,1,0:T(8,128)(2,1)} %param.14) | copy-start | bytes 7077892
  2.7 7.1 %collective-permute-start.2 = (f32[1,2304]{1,0:T(1,128)S(1)}, f32[1,2304]{1,0:T(1,128)S(1)}, u32[]{:S(2)}, u32[]{:S(2)}) collective-permute-start(f32[1,2304]{1,0:T(1,128)S(1)} %fusion.refs_1_), channel_id=1, source_target_pairs={{0,3},{1,2},{2,1},{3,0},{64,67},{65,66},{66,65},{67,64},{4,7},{5,6... | collective-permute-start | bytes 27656 | tf_op jit(solution)/shard_map/ppermute | solution.py:33
  5.3 4.5 %collective-permute-start.1 = (f32[1,2304]{1,0:T(1,128)S(1)}, f32[1,2304]{1,0:T(1,128)S(1)}, u32[]{:S(2)}, u32[]{:S(2)}) collective-permute-start(f32[1,2304]{1,0:T(1,128)S(1)} %fusion.refs_1_), channel_id=1, source_target_pairs={{0,2},{1,3},{2,0},{3,1},{64,66},{65,67},{66,64},{67,65},{4,6},{5,7... | collective-permute-start | bytes 27656 | tf_op jit(solution)/shard_map/ppermute | solution.py:33
  5.5 4.3 %collective-permute-start = (f32[1,2304]{1,0:T(1,128)S(1)}, f32[1,2304]{1,0:T(1,128)S(1)}, u32[]{:S(2)}, u32[]{:S(2)}) collective-permute-start(f32[1,2304]{1,0:T(1,128)S(1)} %fusion.refs_1_), channel_id=1, source_target_pairs={{0,1},{1,0},{2,3},{3,2},{64,65},{65,64},{66,67},{67,66},{4,5},{5,4... | collective-permute-start | bytes 27656 | tf_op jit(solution)/shard_map/ppermute | solution.py:33
  9.8 36.6 %slice-start = ((s8[4718592]{0:T(1024)(128)(4,1)}), s8[4194304]{0:T(1024)(128)(4,1)S(1)}, s32[]{:S(2)}) async-start(s8[4718592]{0:T(1024)(128)(4,1)} %bitcast.14), calls=%async_computation.4 | async-start | bytes 8388608
  9.8 24.0 %copy-start.1 = (s32[2,4]{1,0:T(2,128)S(1)}, s32[2,4]{1,0:T(2,128)}, u32[]{:S(2)}) copy-start(s32[2,4]{1,0:T(2,128)} %refs_0_.3) | copy-start | bytes 100
  9.8 24.0 %copy-start.2 = (s32[2]{0:T(128)S(1)}, s32[2]{0:T(128)}, u32[]{:S(2)}) copy-start(s32[2]{0:T(128)} %refs_1_.3) | copy-start | bytes 28
  9.9 36.5 %slice-start.1 = ((s8[4718592]{0:T(1024)(128)(4,1)}), s8[524288]{0:T(1024)(128)(4,1)S(1)}, s32[]{:S(2)}) async-start(s8[4718592]{0:T(1024)(128)(4,1)} %bitcast.14), calls=%async_computation.5 | async-start | bytes 1048576
  47.4 3.5 %collective-permute-start.3 = (bf16[80,768]{1,0:T(8,128)(2,1)S(1)}, bf16[80,768]{1,0:T(8,128)(2,1)S(1)}, u32[]{:S(2)}, u32[]{:S(2)}) collective-permute-start(bf16[80,768]{1,0:T(8,128)(2,1)S(1)} %get-tuple-element.40), channel_id=1, source_target_pairs={{0,1},{1,0},{2,3},{3,2},{64,65},{65,64},{66,67},{67,66},{4,5},{5,4... | collective-permute-start | bytes 368648 | tf_op jit(solution)/shard_map/ppermute | solution.py:33
  49.9 2.2 %collective-permute-start.6 = (bf16[80,768]{1,0:T(8,128)(2,1)S(1)}, bf16[80,768]{1,0:T(8,128)(2,1)S(1)}, u32[]{:S(2)}, u32[]{:S(2)}) collective-permute-start(bf16[80,768]{1,0:T(8,128)(2,1)S(1)} %get-tuple-element.43), channel_id=1, source_target_pairs={{0,1},{1,0},{2,3},{3,2},{64,65},{65,64},{66,67},{67,66},{4,5},{5,4... | collective-permute-start | bytes 368648 | tf_op jit(solution)/shard_map/ppermute | solution.py:33
  50.9 4.6 %collective-permute-start.4 = (bf16[80,768]{1,0:T(8,128)(2,1)S(1)}, bf16[80,768]{1,0:T(8,128)(2,1)S(1)}, u32[]{:S(2)}, u32[]{:S(2)}) collective-permute-start(bf16[80,768]{1,0:T(8,128)(2,1)S(1)} %add_convert_fusion.7), channel_id=1, source_target_pairs={{0,2},{1,3},{2,0},{3,1},{64,66},{65,67},{66,64},{67,65},{4,6},{5,7... | collective-permute-start | bytes 368648 | tf_op jit(solution)/shard_map/ppermute | solution.py:33
  52.2 5.9 %collective-permute-start.7 = (bf16[80,768]{1,0:T(8,128)(2,1)S(1)}, bf16[80,768]{1,0:T(8,128)(2,1)S(1)}, u32[]{:S(2)}, u32[]{:S(2)}) collective-permute-start(bf16[80,768]{1,0:T(8,128)(2,1)S(1)} %add_convert_fusion.5.own_ref), channel_id=1, source_target_pairs={{0,66},{1,67},{2,64},{3,65},{64,2},{65,3},{66,0},{67,1},{4,70},{5,... | collective-permute-start | bytes 368648 | tf_op jit(solution)/shard_map/ppermute | solution.py:33
  55.6 5.0 %collective-permute-start.5 = (bf16[80,768]{1,0:T(8,128)(2,1)S(1)}, bf16[80,768]{1,0:T(8,128)(2,1)S(1)}, u32[]{:S(2)}, u32[]{:S(2)}) collective-permute-start(bf16[80,768]{1,0:T(8,128)(2,1)S(1)} %add_convert_fusion.6.refs_8_), channel_id=1, source_target_pairs={{0,66},{1,67},{2,64},{3,65},{64,2},{65,3},{66,0},{67,1},{4,70},{5,... | collective-permute-start | bytes 368648 | tf_op jit(solution)/shard_map/ppermute | solution.py:33
  58.1 4.9 %collective-permute-start.8 = (bf16[80,768]{1,0:T(8,128)(2,1)S(1)}, bf16[80,768]{1,0:T(8,128)(2,1)S(1)}, u32[]{:S(2)}, u32[]{:S(2)}) collective-permute-start(bf16[80,768]{1,0:T(8,128)(2,1)S(1)} %pick.1), channel_id=1, source_target_pairs={{0,2},{1,3},{2,0},{3,1},{64,66},{65,67},{66,64},{67,65},{4,6},{5,7... | collective-permute-start | bytes 368648 | tf_op jit(solution)/shard_map/ppermute | solution.py:33
  60.6 4.0 %collective-permute-start.9 = (bf16[80,768]{1,0:T(8,128)(2,1)S(1)}, bf16[80,768]{1,0:T(8,128)(2,1)S(1)}, u32[]{:S(2)}, u32[]{:S(2)}) collective-permute-start(bf16[80,768]{1,0:T(8,128)(2,1)S(1)} %collective-permute-done.5.refs_4_), channel_id=1, source_target_pairs={{0,1},{1,0},{2,3},{3,2},{64,65},{65,64},{66,67},{67,66},{4,5},{5,4... | collective-permute-start | bytes 368648 | tf_op jit(solution)/shard_map/ppermute | solution.py:33
  63.0 2.6 %collective-permute-start.10 = (bf16[80,768]{1,0:T(8,128)(2,1)S(1)}, bf16[80,768]{1,0:T(8,128)(2,1)S(1)}, u32[]{:S(2)}, u32[]{:S(2)}) collective-permute-start(bf16[80,768]{1,0:T(8,128)(2,1)S(1)} %add_convert_fusion.4.refs_5_.refs_9_), channel_id=1, source_target_pairs={{0,1},{1,0},{2,3},{3,2},{64,65},{65,64},{66,67},{67,66},{4,5},{5,4... | collective-permute-start | bytes 368648 | tf_op jit(solution)/shard_map/ppermute | solution.py:33
  95.4 3.6 %collective-permute-start.11 = (bf16[80,768]{1,0:T(8,128)(2,1)S(1)}, bf16[80,768]{1,0:T(8,128)(2,1)S(1)}, u32[]{:S(2)}, u32[]{:S(2)}) collective-permute-start(bf16[80,768]{1,0:T(8,128)(2,1)S(1)} %get-tuple-element.47), channel_id=1, source_target_pairs={{0,1},{1,0},{2,3},{3,2},{64,65},{65,64},{66,67},{67,66},{4,5},{5,4... | collective-permute-start | bytes 368648 | tf_op jit(solution)/shard_map/ppermute | solution.py:33
  98.0 1.3 %collective-permute-start.13 = (bf16[80,768]{1,0:T(8,128)(2,1)S(1)}, bf16[80,768]{1,0:T(8,128)(2,1)S(1)}, u32[]{:S(2)}, u32[]{:S(2)}) collective-permute-start(bf16[80,768]{1,0:T(8,128)(2,1)S(1)} %get-tuple-element.52), channel_id=1, source_target_pairs={{0,1},{1,0},{2,3},{3,2},{64,65},{65,64},{66,67},{67,66},{4,5},{5,4... | collective-permute-start | bytes 368648 | tf_op jit(solution)/shard_map/ppermute | solution.py:33
  99.0 4.6 %collective-permute-start.12 = (bf16[80,768]{1,0:T(8,128)(2,1)S(1)}, bf16[80,768]{1,0:T(8,128)(2,1)S(1)}, u32[]{:S(2)}, u32[]{:S(2)}) collective-permute-start(bf16[80,768]{1,0:T(8,128)(2,1)S(1)} %add_convert_fusion.3), channel_id=1, source_target_pairs={{0,2},{1,3},{2,0},{3,1},{64,66},{65,67},{66,64},{67,65},{4,6},{5,7... | collective-permute-start | bytes 368648 | tf_op jit(solution)/shard_map/ppermute | solution.py:33
  99.4 6.9 %collective-permute-start.14 = (bf16[80,768]{1,0:T(8,128)(2,1)S(1)}, bf16[80,768]{1,0:T(8,128)(2,1)S(1)}, u32[]{:S(2)}, u32[]{:S(2)}) collective-permute-start(bf16[80,768]{1,0:T(8,128)(2,1)S(1)} %add_convert_fusion.1), channel_id=1, source_target_pairs={{0,2},{1,3},{2,0},{3,1},{64,66},{65,67},{66,64},{67,65},{4,6},{5,7... | collective-permute-start | bytes 368648 | tf_op jit(solution)/shard_map/ppermute | solution.py:33
  103.7 4.7 %collective-permute-start.15 = (bf16[80,768]{1,0:T(8,128)(2,1)S(1)}, bf16[80,768]{1,0:T(8,128)(2,1)S(1)}, u32[]{:S(2)}, u32[]{:S(2)}) collective-permute-start(bf16[80,768]{1,0:T(8,128)(2,1)S(1)} %add_convert_fusion.2), channel_id=1, source_target_pairs={{0,1},{1,0},{2,3},{3,2},{64,65},{65,64},{66,67},{67,66},{4,5},{5,4... | collective-permute-start | bytes 368648 | tf_op jit(solution)/shard_map/ppermute | solution.py:33
  106.3 2.2 %collective-permute-start.16 = (bf16[80,768]{1,0:T(8,128)(2,1)S(1)}, bf16[80,768]{1,0:T(8,128)(2,1)S(1)}, u32[]{:S(2)}, u32[]{:S(2)}) collective-permute-start(bf16[80,768]{1,0:T(8,128)(2,1)S(1)} %add_convert_fusion), channel_id=1, source_target_pairs={{0,1},{1,0},{2,3},{3,2},{64,65},{65,64},{66,67},{67,66},{4,5},{5,4... | collective-permute-start | bytes 368648 | tf_op jit(solution)/shard_map/ppermute | solution.py:33

commit v5 on v4

--- a/solution.py
+++ b/solution.py
@@ -337,9 +337,8 @@
     )(lens, text_len, recv, stale, *([pltpu.with_memory_space_constraint(weight, pltpu.HBM)] if loads else []))
 
 
-def out_kernel(recv_ref, mod_ref, w_ref, *refs, last):
+def out_kernel(recv_ref, mod_ref, w_ref, *refs, mine, last):
     *refs, mixed_ref = refs
-    other_refs, mine_refs = refs[: len(refs) // 2], refs[len(refs) // 2 :]
     depth, width = w_ref.shape
     rows = recv_ref.shape[1]
     blocks = depth // LANES
@@ -349,30 +348,29 @@
                 request * blocks + block
             ]
     half = width // 2
-    span = half // len(other_refs)
+    span = half // len(refs)
     core = lax.axis_index("mp") % 2
-    for refs, index in ((other_refs, 1 - core), (mine_refs, core)):
-        for chunk, ref in enumerate(refs):
-            at = pl.ds(pl.multiple_of(index * half + chunk * span, LANES), span)
-            acc = jnp.dot(mixed_ref[...], w_ref[:, at], preferred_element_type=jnp.float32)
-            acc = acc * mod_ref[2:3, at]
-            if last:
-                acc = jnp.where(lax.axis_index("section") == 0, jnp.zeros_like(acc), acc)
-            ref[...] = acc.astype(ref.dtype)
-
-
-def out_call(recv, mod, weight, requests, last):
+    index = core if mine else 1 - core
+    for chunk, ref in enumerate(refs):
+        at = pl.ds(pl.multiple_of(index * half + chunk * span, LANES), span)
+        acc = jnp.dot(mixed_ref[...], w_ref[:, at], preferred_element_type=jnp.float32)
+        acc = acc * mod_ref[2:3, at]
+        if last:
+            acc = jnp.where(lax.axis_index("section") == 0, jnp.zeros_like(acc), acc)
+        ref[...] = acc.astype(ref.dtype)
+
+
+def out_call(recv, mod, weight, requests, mine, last):
     depth, width = weight.shape
     total = requests * recv.shape[1]
     return pl.pallas_call(
-        lambda *refs: out_kernel(*refs, last=last),
+        lambda *refs: out_kernel(*refs, mine=mine, last=last),
         out_shape=[
-            pltpu.VMEM((total, width // 2 // CHUNKS), dtype)
-            for dtype in (jnp.bfloat16, jnp.float32)
+            pltpu.VMEM((total, width // 2 // CHUNKS), jnp.float32 if mine else jnp.bfloat16)
             for _ in range(CHUNKS)
         ],
         in_specs=[VMEM, VMEM, VMEM],
-        out_specs=[VMEM] * (2 * CHUNKS),
+        out_specs=[VMEM] * CHUNKS,
         scratch_shapes=[pltpu.VMEM((total, depth), jnp.bfloat16)],
         compiler_params=PARAMS,
         name="out_projection",
@@ -482,11 +480,9 @@
     unit, stale, weight_qk, *x_half = prepare_call(video, text, weight, stale_cache[0])
 
     def reduced(mixed, weight_out, mod, last):
-        pieces = out_call(mixed, mod, weight_out, requests, last)
-        return [
-            (mine + swap_core(other).astype(jnp.float32)).astype(jnp.bfloat16)
-            for other, mine in zip(pieces[:CHUNKS], pieces[CHUNKS:])
-        ]
+        others = each(swap_core, out_call(mixed, mod, weight_out, requests, False, last))
+        mines = out_call(mixed, mod, weight_out, requests, True, last)
+        return [(a + b.astype(jnp.float32)).astype(jnp.bfloat16) for a, b in zip(mines, others)]
 
     def added(x_half, on_chip, arrived):
         return [
@@ -502,10 +498,10 @@
     weight_out = w_out[0]
     attended = attention_call(patch_lengths, text_len, recv_0, recv_0, None, rows, per_dev, blocks)
     on_chip = reduced(lax.all_to_all(attended, "seq", 0, 0, tiled=True), weight_out, mod, False)
-    crossed = pick_call(next_section(on_chip[1]), on_chip[1])
-    result_0 = added(x_half, [on_chip[0], crossed], [swap_chip(on_chip[0]), swap_chip(crossed)])
-
-    x_half = [next_section(result_0[0]), result_0[1]]
+    crossed = pick_call(next_section(on_chip[0]), on_chip[0])
+    result_0 = added(x_half, [crossed, on_chip[1]], [swap_chip(crossed), swap_chip(on_chip[1])])
+
+    x_half = [result_0[0], next_section(result_0[1])]
     sent_1, key_value, *base = second_call(
         x_half, each(swap_core, x_half), result_0, kv_0, mod, weight_qk, weight_v, rows, devices
     )

time: 110 us -> 109 us (level)
  waiting for transfers between devices: 10.6 us -> 9.47 us
    ppermute x17, waiting for transfers between devices: 10.6 us -> 9.47 us  [swap(): return lax.ppermute(value, ('section', 'mp'), pairs)]
    pallas_call x2 -> x4, Pallas kernels: 1.97 us -> 2.25 us  [out_call(): pl.pallas_call(lambda *refs: out_kernel(*refs, mine=mine, last=last), out...]
  transfers between devices with their start and end apart: 17 -> 17, of which waited for: 9 -> 9; matrix products, arithmetic and copies ran while one was open for 0% -> 0% of each run, Pallas kernels for 4% -> 5%
where the time goes in v5:
time: 109 us
  blocking collectives  54 us (50%)
  starting transfers between devices  22.7 us (21%)
  Pallas kernels  19.1 us (18%)
  waiting for transfers between devices  9.47 us (9%)
  between operations  1.78 us (2%)
    ppermute x17, starting transfers between devices, swap(): return lax.ppermute(value, ('section', 'mp'), pairs)  22.7 us
    all_to_all x2, blocking collectives, body(): lax.all_to_all(attended, 'seq', 0, 0, tiled=True)  20.5 us
    all_to_all x1, blocking collectives, body(): recv_0 = lax.all_to_all(sent_0, 'seq', 0, 0, tiled=True)  20.4 us
    all_to_all x1, blocking collectives, body(): recv_1 = lax.all_to_all(sent_1, 'seq', 0, 0, tiled=True)  13.1 us
    ppermute x17, waiting for transfers between devices, swap(): return lax.ppermute(value, ('section', 'mp'), pairs)  9.47 us
    pallas_call x2, Pallas kernels, attention_call(): pl.pallas_call(lambda *refs: attention_kernel(*refs, rows=rows, per_dev=p...  4.77 us
    pallas_call x1, Pallas kernels, prepare_call(): pl.pallas_call(prepare_kernel, out_shape=(pltpu.VMEM((total, width), jnp....  3.98 us
    pallas_call x1, Pallas kernels, first_call(): pl.pallas_call(lambda *refs: first_kernel(*refs, rows=rows), out_shape=(j...  3.57 us
  transfers between devices with their start and end apart: 17, of which 9 were waited for; matrix products, arithmetic and copies ran while one was open for 0% of the time, Pallas kernels for 5%

profile of v5, /device:TPU:1, one launch (start us, length us, event | category | flops | bytes accessed | tf_op | source)
XLA Modules:
  0.0 108.7 jit_solution(9281234485902382091)
XLA Ops:
  0.6 0.0 copy-start
  1.5 0.8 copy-done
  2.3 0.4 fusion.refs_1_
  2.7 2.6 %collective-permute-start.2 = (f32[1,2304]{1,0:T(1,128)S(1)}, f32[1,2304]{1,0:T(1,128)S(1)}, u32[]{:S(2)}, u32[]{:S(2)}) collective-permute-start(f32[1,2304]{1,0:T(1,128)S(1)} %fusion.refs_1_), channel_id=1, source_target_pairs={{0,3},{1,2},{2,1},{3,0},{64,67},{65,66},{66,65},{67,64},{4,7},{5,6... | collective-permute-start | bytes 27656 | tf_op jit(solution)/shard_map/ppermute | solution.py:33
  5.3 0.2 collective-permute-start.1
  5.5 0.3 collective-permute-start
  5.8 4.0 %prepare.1 = (f32[80,3072]{1,0:T(8,128)S(1)}, bf16[12,48,128]{2,1,0:T(8,128)(2,1)S(1)}, bf16[2,3072,768]{2,1,0:T(8,128)(2,1)S(1)}, bf16[80,768]{1,0:T(8,128)(2,1)S(1)}, bf16[80,768]{1,0:T(8,128)(2,1)S(1)}) custom-call(bf16[2,4,8,3072]{3,2,1,0:T(8,128)(2,1)} %video_ref.1, bf16[2,8,3072]{2,1,0:T(8,128)(2,1)} %text_ref.1, bf16[3,3072,768]{2,1,0:T(8,128)(2,1)} %bitcast.24, ...), custom_call_target="tpu_custom_call" | custom-call | tf_op jit(solution)/shard_map/prepare/pallas_call | solution.py:107
  9.8 0.0 collective-permute-done.2.refs_4_
  9.8 0.0 collective-permute-done.1.refs_3_
  9.8 0.0 collective-permute-done.refs_2_
  9.8 0.0 slice-start
  9.8 0.0 copy-start.1
  9.8 0.0 copy-start.2
  9.9 0.0 slice-start.1
  9.9 3.6 %first_qkv.1 = (bf16[16,168,128]{2,1,0:T(8,128)(2,1)S(1)}, bf16[2,80,768]{2,1,0:T(8,128)(2,1)S(1)}, f32[3,3072]{1,0:T(4,128)S(1)}, bf16[3072,768]{1,0:T(8,128)(2,1)S(1)}) custom-call(f32[80,3072]{1,0:T(8,128)S(1)} %get-tuple-element.31.refs_0_, f32[1,2304]{1,0:T(1,128)S(1)} %fusion.refs_1_, f32[1,2304]{1,0:T(1,128)S(1)} %collective-permute-done.refs_2_, ...), custom_call_target="tpu_custom_call" | custom-call | tf_op jit(solution)/shard_map/first_qkv/pallas_call | solution.py:193
  13.4 20.4 %all_to_all.20.refs_2_.refs_3_ = bf16[16,168,128]{2,1,0:T(8,128)(2,1)S(1)} all-to-all(bf16[16,168,128]{2,1,0:T(8,128)(2,1)S(1)} %get-tuple-element.38), channel_id=1, replica_groups=mesh['section'=2,'seq'=16,'mp'=4] {'seq'}, dimensions={0} | all-to-all | bytes 1376256 | tf_op jit(solution)/shard_map/all_to_all | solution.py:497
  33.9 0.0 copy-done.1
  33.9 0.0 copy-done.2
  33.9 2.4 %attention.2 = bf16[16,40,128]{2,1,0:T(8,128)(2,1)S(1)} custom-call(s32[2,4]{1,0:T(2,128)S(1)} %copy-done.1, s32[2]{0:T(128)S(1)} %copy-done.2, bf16[16,168,128]{2,1,0:T(8,128)(2,1)S(1)} %all_to_all.20.refs_2_.refs_3_, bf16[16,168,128]{2,1,0:T(8,128)(2,1)S(1)} %all_to_all.20.refs_2_.refs_3_), custom_call_target="tpu_custom_call" | custom-call | tf_op jit(solution)/shard_map/attention/pallas_call | solution.py:329
  36.2 10.1 %all_to_all.21.refs_0_ = bf16[16,40,128]{2,1,0:T(8,128)(2,1)S(1)} all-to-all(bf16[16,40,128]{2,1,0:T(8,128)(2,1)S(1)} %attention.2), channel_id=1, replica_groups=mesh['section'=2,'seq'=16,'mp'=4] {'seq'}, dimensions={0} | all-to-all | bytes 327680 | tf_op jit(solution)/shard_map/all_to_all | solution.py:500
  46.4 0.0 slice-done
  46.4 0.0 slice-done.1
  46.4 0.6 out_projection.5
  46.9 2.5 %collective-permute-start.6 = (bf16[80,768]{1,0:T(8,128)(2,1)S(1)}, bf16[80,768]{1,0:T(8,128)(2,1)S(1)}, u32[]{:S(2)}, u32[]{:S(2)}) collective-permute-start(bf16[80,768]{1,0:T(8,128)(2,1)S(1)} %get-tuple-element.43), channel_id=1, source_target_pairs={{0,1},{1,0},{2,3},{3,2},{64,65},{65,64},{66,67},{67,66},{4,5},{5,4... | collective-permute-start | bytes 368648 | tf_op jit(solution)/shard_map/ppermute | solution.py:33
  49.5 0.1 collective-permute-start.3
  49.6 0.6 out_projection.4
  50.2 0.3 collective-permute-done.6
  50.5 1.2 %collective-permute-start.7 = (bf16[80,768]{1,0:T(8,128)(2,1)S(1)}, bf16[80,768]{1,0:T(8,128)(2,1)S(1)}, u32[]{:S(2)}, u32[]{:S(2)}) collective-permute-start(bf16[80,768]{1,0:T(8,128)(2,1)S(1)} %add_convert_fusion.5), channel_id=1, source_target_pairs={{0,2},{1,3},{2,0},{3,1},{64,66},{65,67},{66,64},{67,65},{4,6},{5,7... | collective-permute-start | bytes 368648 | tf_op jit(solution)/shard_map/ppermute | solution.py:33
  51.7 0.0 collective-permute-done.3
  51.7 1.9 %collective-permute-start.4 = (bf16[80,768]{1,0:T(8,128)(2,1)S(1)}, bf16[80,768]{1,0:T(8,128)(2,1)S(1)}, u32[]{:S(2)}, u32[]{:S(2)}) collective-permute-start(bf16[80,768]{1,0:T(8,128)(2,1)S(1)} %add_convert_fusion.7.own_ref), channel_id=1, source_target_pairs={{0,66},{1,67},{2,64},{3,65},{64,2},{65,3},{66,0},{67,1},{4,70},{5,... | collective-permute-start | bytes 368648 | tf_op jit(solution)/shard_map/ppermute | solution.py:33
  53.6 1.5 %collective-permute-done.7 = bf16[80,768]{1,0:T(8,128)(2,1)S(1)} collective-permute-done((bf16[80,768]{1,0:T(8,128)(2,1)S(1)}, bf16[80,768]{1,0:T(8,128)(2,1)S(1)}, u32[]{:S(2)}, u32[]{:S(2)}) %collective-permute-start.7) | collective-permute-done | bytes 122912 | tf_op jit(solution)/shard_map/ppermute | solution.py:33
  55.1 0.1 add_convert_fusion.4.refs_9_
  55.2 2.5 %collective-permute-start.8 = (bf16[80,768]{1,0:T(8,128)(2,1)S(1)}, bf16[80,768]{1,0:T(8,128)(2,1)S(1)}, u32[]{:S(2)}, u32[]{:S(2)}) collective-permute-start(bf16[80,768]{1,0:T(8,128)(2,1)S(1)} %add_convert_fusion.4.refs_9_), channel_id=1, source_target_pairs={{0,66},{1,67},{2,64},{3,65},{64,2},{65,3},{66,0},{67,1},{4,70},{5,... | collective-permute-start | bytes 368648 | tf_op jit(solution)/shard_map/ppermute | solution.py:33
  57.6 0.0 collective-permute-done.4.arrived_ref
  57.7 0.1 collective-permute-start.5
  57.8 2.4 %collective-permute-done.8.refs_5_ = bf16[80,768]{1,0:T(8,128)(2,1)S(1)} collective-permute-done((bf16[80,768]{1,0:T(8,128)(2,1)S(1)}, bf16[80,768]{1,0:T(8,128)(2,1)S(1)}, u32[]{:S(2)}, u32[]{:S(2)}) %collective-permute-start.8) | collective-permute-done | bytes 122912 | tf_op jit(solution)/shard_map/ppermute | solution.py:33
  60.2 2.3 %collective-permute-start.10 = (bf16[80,768]{1,0:T(8,128)(2,1)S(1)}, bf16[80,768]{1,0:T(8,128)(2,1)S(1)}, u32[]{:S(2)}, u32[]{:S(2)}) collective-permute-start(bf16[80,768]{1,0:T(8,128)(2,1)S(1)} %collective-permute-done.8.refs_5_), channel_id=1, source_target_pairs={{0,1},{1,0},{2,3},{3,2},{64,65},{65,64},{66,67},{67,66},{4,5},{5,4... | collective-permute-start | bytes 368648 | tf_op jit(solution)/shard_map/ppermute | solution.py:33
  62.5 0.0 collective-permute-done.5
  62.5 0.1 add_convert_fusion.6.refs_4_.refs_8_
  62.6 1.6 %collective-permute-start.9 = (bf16[80,768]{1,0:T(8,128)(2,1)S(1)}, bf16[80,768]{1,0:T(8,128)(2,1)S(1)}, u32[]{:S(2)}, u32[]{:S(2)}) collective-permute-start(bf16[80,768]{1,0:T(8,128)(2,1)S(1)} %add_convert_fusion.6.refs_4_.refs_8_), channel_id=1, source_target_pairs={{0,1},{1,0},{2,3},{3,2},{64,65},{65,64},{66,67},{67,66},{4,5},{5,4... | collective-permute-start | bytes 368648 | tf_op jit(solution)/shard_map/ppermute | solution.py:33
  64.2 0.0 collective-permute-done.10.refs_7_
  64.2 1.0 collective-permute-done.9.refs_6_
  65.2 2.9 %second_qkv.1 = (bf16[16,120,128]{2,1,0:T(8,128)(2,1)S(1)}, bf16[2,80,768]{2,1,0:T(8,128)(2,1)S(1)}, bf16[80,768]{1,0:T(8,128)(2,1)S(1)}, bf16[80,768]{1,0:T(8,128)(2,1)S(1)}) custom-call(f32[3,3072]{1,0:T(4,128)S(1)} %get-tuple-element.34.refs_1_.refs_0_, bf16[2,3072,768]{2,1,0:T(8,128)(2,1)S(1)} %get-tuple-element.32.refs_5_.refs_1_, ...), custom_call_target="tpu_custom_call" | custom-call | tf_op jit(solution)/shard_map/second_qkv/pallas_call | solution.py:245
  68.1 13.1 %all_to_all.22.refs_2_ = bf16[16,120,128]{2,1,0:T(8,128)(2,1)S(1)} all-to-all(bf16[16,120,128]{2,1,0:T(8,128)(2,1)S(1)} %get-tuple-element.45), channel_id=1, replica_groups=mesh['section'=2,'seq'=16,'mp'=4] {'seq'}, dimensions={0} | all-to-all | bytes 983040 | tf_op jit(solution)/shard_map/all_to_all | solution.py:508
  81.3 2.4 %attention.3 = bf16[16,40,128]{2,1,0:T(8,128)(2,1)S(1)} custom-call(s32[2,4]{1,0:T(2,128)S(1)} %copy-done.1, s32[2]{0:T(128)S(1)} %copy-done.2, bf16[16,120,128]{2,1,0:T(8,128)(2,1)S(1)} %all_to_all.22.refs_2_, bf16[16,168,128]{2,1,0:T(8,128)(2,1)S(1)} %all_to_all.20.refs_2_.refs_3_), custom_call_target="tpu_custom_call" | custom-call | tf_op jit(solution)/shard_map/attention/pallas_call | solution.py:329
  83.7 10.3 %all_to_all.23.refs_0_ = bf16[16,40,128]{2,1,0:T(8,128)(2,1)S(1)} all-to-all(bf16[16,40,128]{2,1,0:T(8,128)(2,1)S(1)} %attention.3), channel_id=1, replica_groups=mesh['section'=2,'seq'=16,'mp'=4] {'seq'}, dimensions={0} | all-to-all | bytes 327680 | tf_op jit(solution)/shard_map/all_to_all | solution.py:510
  94.0 0.6 out_projection.7
  94.5 2.6 %collective-permute-start.13 = (bf16[80,768]{1,0:T(8,128)(2,1)S(1)}, bf16[80,768]{1,0:T(8,128)(2,1)S(1)}, u32[]{:S(2)}, u32[]{:S(2)}) collective-permute-start(bf16[80,768]{1,0:T(8,128)(2,1)S(1)} %get-tuple-element.52), channel_id=1, source_target_pairs={{0,1},{1,0},{2,3},{3,2},{64,65},{65,64},{66,67},{67,66},{4,5},{5,4... | collective-permute-start | bytes 368648 | tf_op jit(solution)/shard_map/ppermute | solution.py:33
  97.2 0.1 collective-permute-start.11
  97.3 0.6 out_projection.6
  97.8 0.3 collective-permute-done.13
  98.2 0.1 collective-permute-start.14
  98.3 0.2 collective-permute-done.11
  98.5 1.3 %collective-permute-start.12 = (bf16[80,768]{1,0:T(8,128)(2,1)S(1)}, bf16[80,768]{1,0:T(8,128)(2,1)S(1)}, u32[]{:S(2)}, u32[]{:S(2)}) collective-permute-start(bf16[80,768]{1,0:T(8,128)(2,1)S(1)} %add_convert_fusion.3), channel_id=1, source_target_pairs={{0,2},{1,3},{2,0},{3,1},{64,66},{65,67},{66,64},{67,65},{4,6},{5,7... | collective-permute-start | bytes 368648 | tf_op jit(solution)/shard_map/ppermute | solution.py:33
  99.8 3.0 %collective-permute-done.14 = bf16[80,768]{1,0:T(8,128)(2,1)S(1)} collective-permute-done((bf16[80,768]{1,0:T(8,128)(2,1)S(1)}, bf16[80,768]{1,0:T(8,128)(2,1)S(1)}, u32[]{:S(2)}, u32[]{:S(2)}) %collective-permute-start.14) | collective-permute-done | bytes 122912 | tf_op jit(solution)/shard_map/ppermute | solution.py:33
  102.8 2.1 %collective-permute-start.16 = (bf16[80,768]{1,0:T(8,128)(2,1)S(1)}, bf16[80,768]{1,0:T(8,128)(2,1)S(1)}, u32[]{:S(2)}, u32[]{:S(2)}) collective-permute-start(bf16[80,768]{1,0:T(8,128)(2,1)S(1)} %add_convert_fusion), channel_id=1, source_target_pairs={{0,1},{1,0},{2,3},{3,2},{64,65},{65,64},{66,67},{67,66},{4,5},{5,4... | collective-permute-start | bytes 368648 | tf_op jit(solution)/shard_map/ppermute | solution.py:33
  104.9 0.5 collective-permute-done.12
  105.5 1.3 %collective-permute-start.15 = (bf16[80,768]{1,0:T(8,128)(2,1)S(1)}, bf16[80,768]{1,0:T(8,128)(2,1)S(1)}, u32[]{:S(2)}, u32[]{:S(2)}) collective-permute-start(bf16[80,768]{1,0:T(8,128)(2,1)S(1)} %add_convert_fusion.2), channel_id=1, source_target_pairs={{0,1},{1,0},{2,3},{3,2},{64,65},{65,64},{66,67},{67,66},{4,5},{5,4... | collective-permute-start | bytes 368648 | tf_op jit(solution)/shard_map/ppermute | solution.py:33
  106.7 0.8 cache.1
  107.5 0.0 collective-permute-done.16
  107.5 0.2 collective-permute-done.15
  107.7 0.8 store.1
  (11 shorter events, 0.3 us)
Async XLA Ops:
  0.6 1.7 %copy-start = (bf16[1,512,2304]{2,1,0:T(8,128)(2,1)S(1)}, bf16[1,512,2304]{2,1,0:T(8,128)(2,1)}, u32[]{:S(2)}) copy-start(bf16[1,512,2304]{2,1,0:T(8,128)(2,1)} %param.14) | copy-start | bytes 7077892
  2.7 7.1 %collective-permute-start.2 = (f32[1,2304]{1,0:T(1,128)S(1)}, f32[1,2304]{1,0:T(1,128)S(1)}, u32[]{:S(2)}, u32[]{:S(2)}) collective-permute-start(f32[1,2304]{1,0:T(1,128)S(1)} %fusion.refs_1_), channel_id=1, source_target_pairs={{0,3},{1,2},{2,1},{3,0},{64,67},{65,66},{66,65},{67,64},{4,7},{5,6... | collective-permute-start | bytes 27656 | tf_op jit(solution)/shard_map/ppermute | solution.py:33
  5.3 4.5 %collective-permute-start.1 = (f32[1,2304]{1,0:T(1,128)S(1)}, f32[1,2304]{1,0:T(1,128)S(1)}, u32[]{:S(2)}, u32[]{:S(2)}) collective-permute-start(f32[1,2304]{1,0:T(1,128)S(1)} %fusion.refs_1_), channel_id=1, source_target_pairs={{0,2},{1,3},{2,0},{3,1},{64,66},{65,67},{66,64},{67,65},{4,6},{5,7... | collective-permute-start | bytes 27656 | tf_op jit(solution)/shard_map/ppermute | solution.py:33
  5.5 4.3 %collective-permute-start = (f32[1,2304]{1,0:T(1,128)S(1)}, f32[1,2304]{1,0:T(1,128)S(1)}, u32[]{:S(2)}, u32[]{:S(2)}) collective-permute-start(f32[1,2304]{1,0:T(1,128)S(1)} %fusion.refs_1_), channel_id=1, source_target_pairs={{0,1},{1,0},{2,3},{3,2},{64,65},{65,64},{66,67},{67,66},{4,5},{5,4... | collective-permute-start | bytes 27656 | tf_op jit(solution)/shard_map/ppermute | solution.py:33
  9.8 36.6 %slice-start = ((s8[4718592]{0:T(1024)(128)(4,1)}), s8[4194304]{0:T(1024)(128)(4,1)S(1)}, s32[]{:S(2)}) async-start(s8[4718592]{0:T(1024)(128)(4,1)} %bitcast.14), calls=%async_computation.4 | async-start | bytes 8388608
  9.8 24.0 %copy-start.1 = (s32[2,4]{1,0:T(2,128)S(1)}, s32[2,4]{1,0:T(2,128)}, u32[]{:S(2)}) copy-start(s32[2,4]{1,0:T(2,128)} %refs_0_.3) | copy-start | bytes 100
  9.8 24.0 %copy-start.2 = (s32[2]{0:T(128)S(1)}, s32[2]{0:T(128)}, u32[]{:S(2)}) copy-start(s32[2]{0:T(128)} %refs_1_.3) | copy-start | bytes 28
  9.9 36.5 %slice-start.1 = ((s8[4718592]{0:T(1024)(128)(4,1)}), s8[524288]{0:T(1024)(128)(4,1)S(1)}, s32[]{:S(2)}) async-start(s8[4718592]{0:T(1024)(128)(4,1)} %bitcast.14), calls=%async_computation.5 | async-start | bytes 1048576
  46.9 3.5 %collective-permute-start.6 = (bf16[80,768]{1,0:T(8,128)(2,1)S(1)}, bf16[80,768]{1,0:T(8,128)(2,1)S(1)}, u32[]{:S(2)}, u32[]{:S(2)}) collective-permute-start(bf16[80,768]{1,0:T(8,128)(2,1)S(1)} %get-tuple-element.43), channel_id=1, source_target_pairs={{0,1},{1,0},{2,3},{3,2},{64,65},{65,64},{66,67},{67,66},{4,5},{5,4... | collective-permute-start | bytes 368648 | tf_op jit(solution)/shard_map/ppermute | solution.py:33
  49.5 2.2 %collective-permute-start.3 = (bf16[80,768]{1,0:T(8,128)(2,1)S(1)}, bf16[80,768]{1,0:T(8,128)(2,1)S(1)}, u32[]{:S(2)}, u32[]{:S(2)}) collective-permute-start(bf16[80,768]{1,0:T(8,128)(2,1)S(1)} %get-tuple-element.40), channel_id=1, source_target_pairs={{0,1},{1,0},{2,3},{3,2},{64,65},{65,64},{66,67},{67,66},{4,5},{5,4... | collective-permute-start | bytes 368648 | tf_op jit(solution)/shard_map/ppermute | solution.py:33
  50.5 4.6 %collective-permute-start.7 = (bf16[80,768]{1,0:T(8,128)(2,1)S(1)}, bf16[80,768]{1,0:T(8,128)(2,1)S(1)}, u32[]{:S(2)}, u32[]{:S(2)}) collective-permute-start(bf16[80,768]{1,0:T(8,128)(2,1)S(1)} %add_convert_fusion.5), channel_id=1, source_target_pairs={{0,2},{1,3},{2,0},{3,1},{64,66},{65,67},{66,64},{67,65},{4,6},{5,7... | collective-permute-start | bytes 368648 | tf_op jit(solution)/shard_map/ppermute | solution.py:33
  51.7 5.9 %collective-permute-start.4 = (bf16[80,768]{1,0:T(8,128)(2,1)S(1)}, bf16[80,768]{1,0:T(8,128)(2,1)S(1)}, u32[]{:S(2)}, u32[]{:S(2)}) collective-permute-start(bf16[80,768]{1,0:T(8,128)(2,1)S(1)} %add_convert_fusion.7.own_ref), channel_id=1, source_target_pairs={{0,66},{1,67},{2,64},{3,65},{64,2},{65,3},{66,0},{67,1},{4,70},{5,... | collective-permute-start | bytes 368648 | tf_op jit(solution)/shard_map/ppermute | solution.py:33
  55.2 5.0 %collective-permute-start.8 = (bf16[80,768]{1,0:T(8,128)(2,1)S(1)}, bf16[80,768]{1,0:T(8,128)(2,1)S(1)}, u32[]{:S(2)}, u32[]{:S(2)}) collective-permute-start(bf16[80,768]{1,0:T(8,128)(2,1)S(1)} %add_convert_fusion.4.refs_9_), channel_id=1, source_target_pairs={{0,66},{1,67},{2,64},{3,65},{64,2},{65,3},{66,0},{67,1},{4,70},{5,... | collective-permute-start | bytes 368648 | tf_op jit(solution)/shard_map/ppermute | solution.py:33
  57.7 4.9 %collective-permute-start.5 = (bf16[80,768]{1,0:T(8,128)(2,1)S(1)}, bf16[80,768]{1,0:T(8,128)(2,1)S(1)}, u32[]{:S(2)}, u32[]{:S(2)}) collective-permute-start(bf16[80,768]{1,0:T(8,128)(2,1)S(1)} %pick.1), channel_id=1, source_target_pairs={{0,2},{1,3},{2,0},{3,1},{64,66},{65,67},{66,64},{67,65},{4,6},{5,7... | collective-permute-start | bytes 368648 | tf_op jit(solution)/shard_map/ppermute | solution.py:33
  60.2 4.0 %collective-permute-start.10 = (bf16[80,768]{1,0:T(8,128)(2,1)S(1)}, bf16[80,768]{1,0:T(8,128)(2,1)S(1)}, u32[]{:S(2)}, u32[]{:S(2)}) collective-permute-start(bf16[80,768]{1,0:T(8,128)(2,1)S(1)} %collective-permute-done.8.refs_5_), channel_id=1, source_target_pairs={{0,1},{1,0},{2,3},{3,2},{64,65},{65,64},{66,67},{67,66},{4,5},{5,4... | collective-permute-start | bytes 368648 | tf_op jit(solution)/shard_map/ppermute | solution.py:33
  62.6 2.6 %collective-permute-start.9 = (bf16[80,768]{1,0:T(8,128)(2,1)S(1)}, bf16[80,768]{1,0:T(8,128)(2,1)S(1)}, u32[]{:S(2)}, u32[]{:S(2)}) collective-permute-start(bf16[80,768]{1,0:T(8,128)(2,1)S(1)} %add_convert_fusion.6.refs_4_.refs_8_), channel_id=1, source_target_pairs={{0,1},{1,0},{2,3},{3,2},{64,65},{65,64},{66,67},{67,66},{4,5},{5,4... | collective-permute-start | bytes 368648 | tf_op jit(solution)/shard_map/ppermute | solution.py:33
  94.5 3.6 %collective-permute-start.13 = (bf16[80,768]{1,0:T(8,128)(2,1)S(1)}, bf16[80,768]{1,0:T(8,128)(2,1)S(1)}, u32[]{:S(2)}, u32[]{:S(2)}) collective-permute-start(bf16[80,768]{1,0:T(8,128)(2,1)S(1)} %get-tuple-element.52), channel_id=1, source_target_pairs={{0,1},{1,0},{2,3},{3,2},{64,65},{65,64},{66,67},{67,66},{4,5},{5,4... | collective-permute-start | bytes 368648 | tf_op jit(solution)/shard_map/ppermute | solution.py:33
  97.2 1.3 %collective-permute-start.11 = (bf16[80,768]{1,0:T(8,128)(2,1)S(1)}, bf16[80,768]{1,0:T(8,128)(2,1)S(1)}, u32[]{:S(2)}, u32[]{:S(2)}) collective-permute-start(bf16[80,768]{1,0:T(8,128)(2,1)S(1)} %get-tuple-element.47), channel_id=1, source_target_pairs={{0,1},{1,0},{2,3},{3,2},{64,65},{65,64},{66,67},{67,66},{4,5},{5,4... | collective-permute-start | bytes 368648 | tf_op jit(solution)/shard_map/ppermute | solution.py:33
  98.2 4.6 %collective-permute-start.14 = (bf16[80,768]{1,0:T(8,128)(2,1)S(1)}, bf16[80,768]{1,0:T(8,128)(2,1)S(1)}, u32[]{:S(2)}, u32[]{:S(2)}) collective-permute-start(bf16[80,768]{1,0:T(8,128)(2,1)S(1)} %add_convert_fusion.1), channel_id=1, source_target_pairs={{0,2},{1,3},{2,0},{3,1},{64,66},{65,67},{66,64},{67,65},{4,6},{5,7... | collective-permute-start | bytes 368648 | tf_op jit(solution)/shard_map/ppermute | solution.py:33
  98.5 6.9 %collective-permute-start.12 = (bf16[80,768]{1,0:T(8,128)(2,1)S(1)}, bf16[80,768]{1,0:T(8,128)(2,1)S(1)}, u32[]{:S(2)}, u32[]{:S(2)}) collective-permute-start(bf16[80,768]{1,0:T(8,128)(2,1)S(1)} %add_convert_fusion.3), channel_id=1, source_target_pairs={{0,2},{1,3},{2,0},{3,1},{64,66},{65,67},{66,64},{67,65},{4,6},{5,7... | collective-permute-start | bytes 368648 | tf_op jit(solution)/shard_map/ppermute | solution.py:33
  102.8 4.7 %collective-permute-start.16 = (bf16[80,768]{1,0:T(8,128)(2,1)S(1)}, bf16[80,768]{1,0:T(8,128)(2,1)S(1)}, u32[]{:S(2)}, u32[]{:S(2)}) collective-permute-start(bf16[80,768]{1,0:T(8,128)(2,1)S(1)} %add_convert_fusion), channel_id=1, source_target_pairs={{0,1},{1,0},{2,3},{3,2},{64,65},{65,64},{66,67},{67,66},{4,5},{5,4... | collective-permute-start | bytes 368648 | tf_op jit(solution)/shard_map/ppermute | solution.py:33
  105.5 2.2 %collective-permute-start.15 = (bf16[80,768]{1,0:T(8,128)(2,1)S(1)}, bf16[80,768]{1,0:T(8,128)(2,1)S(1)}, u32[]{:S(2)}, u32[]{:S(2)}) collective-permute-start(bf16[80,768]{1,0:T(8,128)(2,1)S(1)} %add_convert_fusion.2), channel_id=1, source_target_pairs={{0,1},{1,0},{2,3},{3,2},{64,65},{65,64},{66,67},{67,66},{4,5},{5,4... | collective-permute-start | bytes 368648 | tf_op jit(solution)/shard_map/ppermute | solution.py:33

commit v6 on v5

--- a/solution.py
+++ b/solution.py
@@ -12,6 +12,7 @@
 EPS = 1e-05
 NEG = -1e30
 CHUNKS = 2
+WIDE = 256
 VMEM_LIMIT = 12 * 1024 * 1024
 
 
@@ -135,15 +136,18 @@
     for part in range(3):
         if part == 2 and load is not None:
             load.wait()
-        weight = wqk_ref[part] if part < 2 else wv_ref[...]
-        acc = jnp.dot(normed_ref[...], weight, preferred_element_type=jnp.float32)
-        if part:
-            kv_ref[part - 1] = acc.astype(jnp.bfloat16)
-        for request in range(requests):
-            for block in range(blocks):
-                o_ref[request * blocks + block, part * rows : (part + 1) * rows, :] = acc[
-                    request * rows : (request + 1) * rows, block * LANES : (block + 1) * LANES
-                ].astype(jnp.bfloat16)
+        for wide in range(0, columns, WIDE):
+            at = slice(wide, wide + WIDE)
+            weight = wqk_ref[part, :, at] if part < 2 else wv_ref[:, at]
+            acc = jnp.dot(normed_ref[...], weight, preferred_element_type=jnp.float32).astype(jnp.bfloat16)
+            if part:
+                kv_ref[part - 1, :, at] = acc
+            for request in range(requests):
+                for block in range(WIDE // LANES):
+                    unit = request * blocks + wide // LANES + block
+                    o_ref[unit, part * rows : (part + 1) * rows, :] = acc[
+                        request * rows : (request + 1) * rows, block * LANES : (block + 1) * LANES
+                    ]
 
 
 def first_kernel(
@@ -214,17 +218,26 @@
     mod_ref, wqk_ref, wv_ref, kv_0_ref, *refs, rows
 ):
     mine_refs, other_refs, before_refs = (refs[i * CHUNKS : (i + 1) * CHUNKS] for i in range(3))
-    o_ref, kv_ref, *base_refs, x_ref, normed_ref = refs[3 * CHUNKS :]
+    o_ref, kv_ref, *base_refs, normed_ref = refs[3 * CHUNKS :]
     total, span = mine_refs[0].shape
     half = span * CHUNKS
     core = lax.axis_index("mp") % 2
-    for chunk in range(CHUNKS):
-        x_ref[:, pl.ds(pl.multiple_of(core * half + chunk * span, LANES), span)] = mine_refs[chunk][...]
-        x_ref[:, pl.ds(pl.multiple_of((1 - core) * half + chunk * span, LANES), span)] = other_refs[chunk][...]
+    pieces = [
+        (ref, pl.ds(pl.multiple_of(index * half + chunk * span, LANES), span))
+        for refs, index in ((mine_refs, core), (other_refs, 1 - core))
+        for chunk, ref in enumerate(refs)
+    ]
     step = 16
     for start in range(0, total, step):
-        normed = centered(x_ref[start : start + step, :]) * (1.0 + mod_ref[1:2, :]) + mod_ref[0:1, :]
-        normed_ref[start : start + step, :] = normed.astype(jnp.bfloat16)
+        line = slice(start, start + step)
+        values = [ref[line, :].astype(jnp.float32) for ref, _ in pieces]
+        mean = sum(jnp.sum(value, axis=-1, keepdims=True) for value in values) / (2 * half)
+        values = [value - mean for value in values]
+        spread = sum(jnp.sum(value * value, axis=-1, keepdims=True) for value in values) / (2 * half)
+        inverse = lax.rsqrt(spread + EPS)
+        for value, (_, at) in zip(values, pieces):
+            normed = value * inverse * (1.0 + mod_ref[1:2, at]) + mod_ref[0:1, at]
+            normed_ref[line, at] = normed.astype(jnp.bfloat16)
     project(normed_ref, wqk_ref, wv_ref, o_ref, kv_ref, rows)
     is_first = lax.axis_index("section") == 0
 
@@ -251,7 +264,7 @@
         + (pltpu.VMEM((total, span), jnp.bfloat16),) * CHUNKS,
         in_specs=[VMEM] * (4 + 3 * CHUNKS),
         out_specs=(VMEM,) * (2 + CHUNKS),
-        scratch_shapes=[pltpu.VMEM((total, 2 * CHUNKS * span), jnp.bfloat16)] * 2,
+        scratch_shapes=[pltpu.VMEM((total, 2 * CHUNKS * span), jnp.bfloat16)],
         compiler_params=PARAMS,
         name="second_qkv",
     )(mod, weight_qk, weight_v, kv_0, *mine, *other, *before)

time: 109 us -> 109 us (level)
  no operation moved by 1% of the time
where the time goes in v6:
time: 109 us
  blocking collectives  54 us (50%)
  starting transfers between devices  22.7 us (21%)
  Pallas kernels  19.1 us (18%)
  waiting for transfers between devices  9.47 us (9%)
  between operations  1.78 us (2%)
    ppermute x17, starting transfers between devices, swap(): return lax.ppermute(value, ('section', 'mp'), pairs)  22.7 us
    all_to_all x2, blocking collectives, body(): lax.all_to_all(attended, 'seq', 0, 0, tiled=True)  20.5 us
    all_to_all x1, blocking collectives, body(): recv_0 = lax.all_to_all(sent_0, 'seq', 0, 0, tiled=True)  20.4 us
    all_to_all x1, blocking collectives, body(): recv_1 = lax.all_to_all(sent_1, 'seq', 0, 0, tiled=True)  13.1 us
    ppermute x17, waiting for transfers between devices, swap(): return lax.ppermute(value, ('section', 'mp'), pairs)  9.47 us
    pallas_call x2, Pallas kernels, attention_call(): pl.pallas_call(lambda *refs: attention_kernel(*refs, rows=rows, per_dev=p...  4.77 us
    pallas_call x1, Pallas kernels, prepare_call(): pl.pallas_call(prepare_kernel, out_shape=(pltpu.VMEM((total, width), jnp....  3.98 us
    pallas_call x1, Pallas kernels, first_call(): pl.pallas_call(lambda *refs: first_kernel(*refs, rows=rows), out_shape=(j...  3.57 us
  transfers between devices with their start and end apart: 17, of which 9 were waited for; matrix products, arithmetic and copies ran while one was open for 0% of the time, Pallas kernels for 5%

profile of v6, /device:TPU:1, one launch (start us, length us, event | category | flops | bytes accessed | tf_op | source)
XLA Modules:
  0.0 108.7 jit_solution(12726863540338532514)
XLA Ops:
  0.6 0.0 copy-start
  1.5 0.8 copy-done
  2.3 0.4 fusion.refs_1_
  2.7 2.6 %collective-permute-start.2 = (f32[1,2304]{1,0:T(1,128)S(1)}, f32[1,2304]{1,0:T(1,128)S(1)}, u32[]{:S(2)}, u32[]{:S(2)}) collective-permute-start(f32[1,2304]{1,0:T(1,128)S(1)} %fusion.refs_1_), channel_id=1, source_target_pairs={{0,3},{1,2},{2,1},{3,0},{64,67},{65,66},{66,65},{67,64},{4,7},{5,6... | collective-permute-start | bytes 27656 | tf_op jit(solution)/shard_map/ppermute | solution.py:34
  5.3 0.2 collective-permute-start.1
  5.5 0.3 collective-permute-start
  5.8 4.0 %prepare.1 = (f32[80,3072]{1,0:T(8,128)S(1)}, bf16[12,48,128]{2,1,0:T(8,128)(2,1)S(1)}, bf16[2,3072,768]{2,1,0:T(8,128)(2,1)S(1)}, bf16[80,768]{1,0:T(8,128)(2,1)S(1)}, bf16[80,768]{1,0:T(8,128)(2,1)S(1)}) custom-call(bf16[2,4,8,3072]{3,2,1,0:T(8,128)(2,1)} %video_ref.1, bf16[2,8,3072]{2,1,0:T(8,128)(2,1)} %text_ref.1, bf16[3,3072,768]{2,1,0:T(8,128)(2,1)} %bitcast.24, ...), custom_call_target="tpu_custom_call" | custom-call | tf_op jit(solution)/shard_map/prepare/pallas_call | solution.py:108
  9.8 0.0 collective-permute-done.2.refs_4_
  9.8 0.0 collective-permute-done.1.refs_3_
  9.8 0.0 collective-permute-done.refs_2_
  9.8 0.0 slice-start
  9.8 0.0 copy-start.1
  9.8 0.0 copy-start.2
  9.9 0.0 slice-start.1
  9.9 3.6 %first_qkv.1 = (bf16[16,168,128]{2,1,0:T(8,128)(2,1)S(1)}, bf16[2,80,768]{2,1,0:T(8,128)(2,1)S(1)}, f32[3,3072]{1,0:T(4,128)S(1)}, bf16[3072,768]{1,0:T(8,128)(2,1)S(1)}) custom-call(f32[80,3072]{1,0:T(8,128)S(1)} %get-tuple-element.31.refs_0_, f32[1,2304]{1,0:T(1,128)S(1)} %fusion.refs_1_, f32[1,2304]{1,0:T(1,128)S(1)} %collective-permute-done.refs_2_, ...), custom_call_target="tpu_custom_call" | custom-call | tf_op jit(solution)/shard_map/first_qkv/pallas_call | solution.py:197
  13.4 20.4 %all_to_all.20.refs_2_.refs_3_ = bf16[16,168,128]{2,1,0:T(8,128)(2,1)S(1)} all-to-all(bf16[16,168,128]{2,1,0:T(8,128)(2,1)S(1)} %get-tuple-element.38), channel_id=1, replica_groups=mesh['section'=2,'seq'=16,'mp'=4] {'seq'}, dimensions={0} | all-to-all | bytes 1376256 | tf_op jit(solution)/shard_map/all_to_all | solution.py:510
  33.9 0.0 copy-done.1
  33.9 0.0 copy-done.2
  33.9 2.4 %attention.2 = bf16[16,40,128]{2,1,0:T(8,128)(2,1)S(1)} custom-call(s32[2,4]{1,0:T(2,128)S(1)} %copy-done.1, s32[2]{0:T(128)S(1)} %copy-done.2, bf16[16,168,128]{2,1,0:T(8,128)(2,1)S(1)} %all_to_all.20.refs_2_.refs_3_, bf16[16,168,128]{2,1,0:T(8,128)(2,1)S(1)} %all_to_all.20.refs_2_.refs_3_), custom_call_target="tpu_custom_call" | custom-call | tf_op jit(solution)/shard_map/attention/pallas_call | solution.py:342
  36.2 10.1 %all_to_all.21.refs_0_ = bf16[16,40,128]{2,1,0:T(8,128)(2,1)S(1)} all-to-all(bf16[16,40,128]{2,1,0:T(8,128)(2,1)S(1)} %attention.2), channel_id=1, replica_groups=mesh['section'=2,'seq'=16,'mp'=4] {'seq'}, dimensions={0} | all-to-all | bytes 327680 | tf_op jit(solution)/shard_map/all_to_all | solution.py:513
  46.4 0.0 slice-done
  46.4 0.0 slice-done.1
  46.4 0.6 out_projection.5
  46.9 2.5 %collective-permute-start.6 = (bf16[80,768]{1,0:T(8,128)(2,1)S(1)}, bf16[80,768]{1,0:T(8,128)(2,1)S(1)}, u32[]{:S(2)}, u32[]{:S(2)}) collective-permute-start(bf16[80,768]{1,0:T(8,128)(2,1)S(1)} %get-tuple-element.43), channel_id=1, source_target_pairs={{0,1},{1,0},{2,3},{3,2},{64,65},{65,64},{66,67},{67,66},{4,5},{5,4... | collective-permute-start | bytes 368648 | tf_op jit(solution)/shard_map/ppermute | solution.py:34
  49.5 0.1 collective-permute-start.3
  49.6 0.6 out_projection.4
  50.2 0.3 collective-permute-done.6
  50.5 1.2 %collective-permute-start.7 = (bf16[80,768]{1,0:T(8,128)(2,1)S(1)}, bf16[80,768]{1,0:T(8,128)(2,1)S(1)}, u32[]{:S(2)}, u32[]{:S(2)}) collective-permute-start(bf16[80,768]{1,0:T(8,128)(2,1)S(1)} %add_convert_fusion.5), channel_id=1, source_target_pairs={{0,2},{1,3},{2,0},{3,1},{64,66},{65,67},{66,64},{67,65},{4,6},{5,7... | collective-permute-start | bytes 368648 | tf_op jit(solution)/shard_map/ppermute | solution.py:34
  51.7 0.0 collective-permute-done.3
  51.7 1.9 %collective-permute-start.4 = (bf16[80,768]{1,0:T(8,128)(2,1)S(1)}, bf16[80,768]{1,0:T(8,128)(2,1)S(1)}, u32[]{:S(2)}, u32[]{:S(2)}) collective-permute-start(bf16[80,768]{1,0:T(8,128)(2,1)S(1)} %add_convert_fusion.7.own_ref), channel_id=1, source_target_pairs={{0,66},{1,67},{2,64},{3,65},{64,2},{65,3},{66,0},{67,1},{4,70},{5,... | collective-permute-start | bytes 368648 | tf_op jit(solution)/shard_map/ppermute | solution.py:34
  53.6 1.5 %collective-permute-done.7 = bf16[80,768]{1,0:T(8,128)(2,1)S(1)} collective-permute-done((bf16[80,768]{1,0:T(8,128)(2,1)S(1)}, bf16[80,768]{1,0:T(8,128)(2,1)S(1)}, u32[]{:S(2)}, u32[]{:S(2)}) %collective-permute-start.7) | collective-permute-done | bytes 122912 | tf_op jit(solution)/shard_map/ppermute | solution.py:34
  55.1 0.1 add_convert_fusion.4.refs_9_
  55.2 2.5 %collective-permute-start.8 = (bf16[80,768]{1,0:T(8,128)(2,1)S(1)}, bf16[80,768]{1,0:T(8,128)(2,1)S(1)}, u32[]{:S(2)}, u32[]{:S(2)}) collective-permute-start(bf16[80,768]{1,0:T(8,128)(2,1)S(1)} %add_convert_fusion.4.refs_9_), channel_id=1, source_target_pairs={{0,66},{1,67},{2,64},{3,65},{64,2},{65,3},{66,0},{67,1},{4,70},{5,... | collective-permute-start | bytes 368648 | tf_op jit(solution)/shard_map/ppermute | solution.py:34
  57.6 0.0 collective-permute-done.4.arrived_ref
  57.7 0.1 collective-permute-start.5
  57.8 2.4 %collective-permute-done.8.refs_5_ = bf16[80,768]{1,0:T(8,128)(2,1)S(1)} collective-permute-done((bf16[80,768]{1,0:T(8,128)(2,1)S(1)}, bf16[80,768]{1,0:T(8,128)(2,1)S(1)}, u32[]{:S(2)}, u32[]{:S(2)}) %collective-permute-start.8) | collective-permute-done | bytes 122912 | tf_op jit(solution)/shard_map/ppermute | solution.py:34
  60.2 2.3 %collective-permute-start.10 = (bf16[80,768]{1,0:T(8,128)(2,1)S(1)}, bf16[80,768]{1,0:T(8,128)(2,1)S(1)}, u32[]{:S(2)}, u32[]{:S(2)}) collective-permute-start(bf16[80,768]{1,0:T(8,128)(2,1)S(1)} %collective-permute-done.8.refs_5_), channel_id=1, source_target_pairs={{0,1},{1,0},{2,3},{3,2},{64,65},{65,64},{66,67},{67,66},{4,5},{5,4... | collective-permute-start | bytes 368648 | tf_op jit(solution)/shard_map/ppermute | solution.py:34
  62.5 0.0 collective-permute-done.5
  62.5 0.1 add_convert_fusion.6.refs_4_.refs_8_
  62.6 1.6 %collective-permute-start.9 = (bf16[80,768]{1,0:T(8,128)(2,1)S(1)}, bf16[80,768]{1,0:T(8,128)(2,1)S(1)}, u32[]{:S(2)}, u32[]{:S(2)}) collective-permute-start(bf16[80,768]{1,0:T(8,128)(2,1)S(1)} %add_convert_fusion.6.refs_4_.refs_8_), channel_id=1, source_target_pairs={{0,1},{1,0},{2,3},{3,2},{64,65},{65,64},{66,67},{67,66},{4,5},{5,4... | collective-permute-start | bytes 368648 | tf_op jit(solution)/shard_map/ppermute | solution.py:34
  64.2 0.0 collective-permute-done.10.refs_7_
  64.2 1.0 collective-permute-done.9.refs_6_
  65.2 2.9 %second_qkv.1 = (bf16[16,120,128]{2,1,0:T(8,128)(2,1)S(1)}, bf16[2,80,768]{2,1,0:T(8,128)(2,1)S(1)}, bf16[80,768]{1,0:T(8,128)(2,1)S(1)}, bf16[80,768]{1,0:T(8,128)(2,1)S(1)}) custom-call(f32[3,3072]{1,0:T(4,128)S(1)} %get-tuple-element.34.refs_1_.refs_0_, bf16[2,3072,768]{2,1,0:T(8,128)(2,1)S(1)} %get-tuple-element.32.refs_5_.refs_1_, ...), custom_call_target="tpu_custom_call" | custom-call | tf_op jit(solution)/shard_map/second_qkv/pallas_call | solution.py:258
  68.1 13.1 %all_to_all.22.refs_2_ = bf16[16,120,128]{2,1,0:T(8,128)(2,1)S(1)} all-to-all(bf16[16,120,128]{2,1,0:T(8,128)(2,1)S(1)} %get-tuple-element.45), channel_id=1, replica_groups=mesh['section'=2,'seq'=16,'mp'=4] {'seq'}, dimensions={0} | all-to-all | bytes 983040 | tf_op jit(solution)/shard_map/all_to_all | solution.py:521
  81.3 2.4 %attention.3 = bf16[16,40,128]{2,1,0:T(8,128)(2,1)S(1)} custom-call(s32[2,4]{1,0:T(2,128)S(1)} %copy-done.1, s32[2]{0:T(128)S(1)} %copy-done.2, bf16[16,120,128]{2,1,0:T(8,128)(2,1)S(1)} %all_to_all.22.refs_2_, bf16[16,168,128]{2,1,0:T(8,128)(2,1)S(1)} %all_to_all.20.refs_2_.refs_3_), custom_call_target="tpu_custom_call" | custom-call | tf_op jit(solution)/shard_map/attention/pallas_call | solution.py:342
  83.7 10.3 %all_to_all.23.refs_0_ = bf16[16,40,128]{2,1,0:T(8,128)(2,1)S(1)} all-to-all(bf16[16,40,128]{2,1,0:T(8,128)(2,1)S(1)} %attention.3), channel_id=1, replica_groups=mesh['section'=2,'seq'=16,'mp'=4] {'seq'}, dimensions={0} | all-to-all | bytes 327680 | tf_op jit(solution)/shard_map/all_to_all | solution.py:523
  94.0 0.6 out_projection.7
  94.6 2.6 %collective-permute-start.13 = (bf16[80,768]{1,0:T(8,128)(2,1)S(1)}, bf16[80,768]{1,0:T(8,128)(2,1)S(1)}, u32[]{:S(2)}, u32[]{:S(2)}) collective-permute-start(bf16[80,768]{1,0:T(8,128)(2,1)S(1)} %get-tuple-element.52), channel_id=1, source_target_pairs={{0,1},{1,0},{2,3},{3,2},{64,65},{65,64},{66,67},{67,66},{4,5},{5,4... | collective-permute-start | bytes 368648 | tf_op jit(solution)/shard_map/ppermute | solution.py:34
  97.2 0.1 collective-permute-start.11
  97.3 0.6 out_projection.6
  97.8 0.3 collective-permute-done.13
  98.2 0.1 collective-permute-start.14
  98.3 0.2 collective-permute-done.11
  98.5 1.3 %collective-permute-start.12 = (bf16[80,768]{1,0:T(8,128)(2,1)S(1)}, bf16[80,768]{1,0:T(8,128)(2,1)S(1)}, u32[]{:S(2)}, u32[]{:S(2)}) collective-permute-start(bf16[80,768]{1,0:T(8,128)(2,1)S(1)} %add_convert_fusion.3), channel_id=1, source_target_pairs={{0,2},{1,3},{2,0},{3,1},{64,66},{65,67},{66,64},{67,65},{4,6},{5,7... | collective-permute-start | bytes 368648 | tf_op jit(solution)/shard_map/ppermute | solution.py:34
  99.8 3.0 %collective-permute-done.14 = bf16[80,768]{1,0:T(8,128)(2,1)S(1)} collective-permute-done((bf16[80,768]{1,0:T(8,128)(2,1)S(1)}, bf16[80,768]{1,0:T(8,128)(2,1)S(1)}, u32[]{:S(2)}, u32[]{:S(2)}) %collective-permute-start.14) | collective-permute-done | bytes 122912 | tf_op jit(solution)/shard_map/ppermute | solution.py:34
  102.8 2.1 %collective-permute-start.16 = (bf16[80,768]{1,0:T(8,128)(2,1)S(1)}, bf16[80,768]{1,0:T(8,128)(2,1)S(1)}, u32[]{:S(2)}, u32[]{:S(2)}) collective-permute-start(bf16[80,768]{1,0:T(8,128)(2,1)S(1)} %add_convert_fusion), channel_id=1, source_target_pairs={{0,1},{1,0},{2,3},{3,2},{64,65},{65,64},{66,67},{67,66},{4,5},{5,4... | collective-permute-start | bytes 368648 | tf_op jit(solution)/shard_map/ppermute | solution.py:34
  104.9 0.5 collective-permute-done.12
  105.5 1.3 %collective-permute-start.15 = (bf16[80,768]{1,0:T(8,128)(2,1)S(1)}, bf16[80,768]{1,0:T(8,128)(2,1)S(1)}, u32[]{:S(2)}, u32[]{:S(2)}) collective-permute-start(bf16[80,768]{1,0:T(8,128)(2,1)S(1)} %add_convert_fusion.2), channel_id=1, source_target_pairs={{0,1},{1,0},{2,3},{3,2},{64,65},{65,64},{66,67},{67,66},{4,5},{5,4... | collective-permute-start | bytes 368648 | tf_op jit(solution)/shard_map/ppermute | solution.py:34
  106.8 0.8 cache.1
  107.5 0.0 collective-permute-done.16
  107.5 0.2 collective-permute-done.15
  107.7 0.8 store.1
  (11 shorter events, 0.3 us)
Async XLA Ops:
  0.6 1.7 %copy-start = (bf16[1,512,2304]{2,1,0:T(8,128)(2,1)S(1)}, bf16[1,512,2304]{2,1,0:T(8,128)(2,1)}, u32[]{:S(2)}) copy-start(bf16[1,512,2304]{2,1,0:T(8,128)(2,1)} %param.14) | copy-start | bytes 7077892
  2.7 7.1 %collective-permute-start.2 = (f32[1,2304]{1,0:T(1,128)S(1)}, f32[1,2304]{1,0:T(1,128)S(1)}, u32[]{:S(2)}, u32[]{:S(2)}) collective-permute-start(f32[1,2304]{1,0:T(1,128)S(1)} %fusion.refs_1_), channel_id=1, source_target_pairs={{0,3},{1,2},{2,1},{3,0},{64,67},{65,66},{66,65},{67,64},{4,7},{5,6... | collective-permute-start | bytes 27656 | tf_op jit(solution)/shard_map/ppermute | solution.py:34
  5.3 4.5 %collective-permute-start.1 = (f32[1,2304]{1,0:T(1,128)S(1)}, f32[1,2304]{1,0:T(1,128)S(1)}, u32[]{:S(2)}, u32[]{:S(2)}) collective-permute-start(f32[1,2304]{1,0:T(1,128)S(1)} %fusion.refs_1_), channel_id=1, source_target_pairs={{0,2},{1,3},{2,0},{3,1},{64,66},{65,67},{66,64},{67,65},{4,6},{5,7... | collective-permute-start | bytes 27656 | tf_op jit(solution)/shard_map/ppermute | solution.py:34
  5.5 4.3 %collective-permute-start = (f32[1,2304]{1,0:T(1,128)S(1)}, f32[1,2304]{1,0:T(1,128)S(1)}, u32[]{:S(2)}, u32[]{:S(2)}) collective-permute-start(f32[1,2304]{1,0:T(1,128)S(1)} %fusion.refs_1_), channel_id=1, source_target_pairs={{0,1},{1,0},{2,3},{3,2},{64,65},{65,64},{66,67},{67,66},{4,5},{5,4... | collective-permute-start | bytes 27656 | tf_op jit(solution)/shard_map/ppermute | solution.py:34
  9.8 36.6 %slice-start = ((s8[4718592]{0:T(1024)(128)(4,1)}), s8[4194304]{0:T(1024)(128)(4,1)S(1)}, s32[]{:S(2)}) async-start(s8[4718592]{0:T(1024)(128)(4,1)} %bitcast.14), calls=%async_computation.4 | async-start | bytes 8388608
  9.8 24.0 %copy-start.1 = (s32[2,4]{1,0:T(2,128)S(1)}, s32[2,4]{1,0:T(2,128)}, u32[]{:S(2)}) copy-start(s32[2,4]{1,0:T(2,128)} %refs_0_.3) | copy-start | bytes 100
  9.8 24.0 %copy-start.2 = (s32[2]{0:T(128)S(1)}, s32[2]{0:T(128)}, u32[]{:S(2)}) copy-start(s32[2]{0:T(128)} %refs_1_.3) | copy-start | bytes 28
  9.9 36.5 %slice-start.1 = ((s8[4718592]{0:T(1024)(128)(4,1)}), s8[524288]{0:T(1024)(128)(4,1)S(1)}, s32[]{:S(2)}) async-start(s8[4718592]{0:T(1024)(128)(4,1)} %bitcast.14), calls=%async_computation.5 | async-start | bytes 1048576
  46.9 3.5 %collective-permute-start.6 = (bf16[80,768]{1,0:T(8,128)(2,1)S(1)}, bf16[80,768]{1,0:T(8,128)(2,1)S(1)}, u32[]{:S(2)}, u32[]{:S(2)}) collective-permute-start(bf16[80,768]{1,0:T(8,128)(2,1)S(1)} %get-tuple-element.43), channel_id=1, source_target_pairs={{0,1},{1,0},{2,3},{3,2},{64,65},{65,64},{66,67},{67,66},{4,5},{5,4... | collective-permute-start | bytes 368648 | tf_op jit(solution)/shard_map/ppermute | solution.py:34
  49.5 2.2 %collective-permute-start.3 = (bf16[80,768]{1,0:T(8,128)(2,1)S(1)}, bf16[80,768]{1,0:T(8,128)(2,1)S(1)}, u32[]{:S(2)}, u32[]{:S(2)}) collective-permute-start(bf16[80,768]{1,0:T(8,128)(2,1)S(1)} %get-tuple-element.40), channel_id=1, source_target_pairs={{0,1},{1,0},{2,3},{3,2},{64,65},{65,64},{66,67},{67,66},{4,5},{5,4... | collective-permute-start | bytes 368648 | tf_op jit(solution)/shard_map/ppermute | solution.py:34
  50.5 4.6 %collective-permute-start.7 = (bf16[80,768]{1,0:T(8,128)(2,1)S(1)}, bf16[80,768]{1,0:T(8,128)(2,1)S(1)}, u32[]{:S(2)}, u32[]{:S(2)}) collective-permute-start(bf16[80,768]{1,0:T(8,128)(2,1)S(1)} %add_convert_fusion.5), channel_id=1, source_target_pairs={{0,2},{1,3},{2,0},{3,1},{64,66},{65,67},{66,64},{67,65},{4,6},{5,7... | collective-permute-start | bytes 368648 | tf_op jit(solution)/shard_map/ppermute | solution.py:34
  51.7 5.9 %collective-permute-start.4 = (bf16[80,768]{1,0:T(8,128)(2,1)S(1)}, bf16[80,768]{1,0:T(8,128)(2,1)S(1)}, u32[]{:S(2)}, u32[]{:S(2)}) collective-permute-start(bf16[80,768]{1,0:T(8,128)(2,1)S(1)} %add_convert_fusion.7.own_ref), channel_id=1, source_target_pairs={{0,66},{1,67},{2,64},{3,65},{64,2},{65,3},{66,0},{67,1},{4,70},{5,... | collective-permute-start | bytes 368648 | tf_op jit(solution)/shard_map/ppermute | solution.py:34
  55.2 5.0 %collective-permute-start.8 = (bf16[80,768]{1,0:T(8,128)(2,1)S(1)}, bf16[80,768]{1,0:T(8,128)(2,1)S(1)}, u32[]{:S(2)}, u32[]{:S(2)}) collective-permute-start(bf16[80,768]{1,0:T(8,128)(2,1)S(1)} %add_convert_fusion.4.refs_9_), channel_id=1, source_target_pairs={{0,66},{1,67},{2,64},{3,65},{64,2},{65,3},{66,0},{67,1},{4,70},{5,... | collective-permute-start | bytes 368648 | tf_op jit(solution)/shard_map/ppermute | solution.py:34
  57.7 4.9 %collective-permute-start.5 = (bf16[80,768]{1,0:T(8,128)(2,1)S(1)}, bf16[80,768]{1,0:T(8,128)(2,1)S(1)}, u32[]{:S(2)}, u32[]{:S(2)}) collective-permute-start(bf16[80,768]{1,0:T(8,128)(2,1)S(1)} %pick.1), channel_id=1, source_target_pairs={{0,2},{1,3},{2,0},{3,1},{64,66},{65,67},{66,64},{67,65},{4,6},{5,7... | collective-permute-start | bytes 368648 | tf_op jit(solution)/shard_map/ppermute | solution.py:34
  60.2 4.0 %collective-permute-start.10 = (bf16[80,768]{1,0:T(8,128)(2,1)S(1)}, bf16[80,768]{1,0:T(8,128)(2,1)S(1)}, u32[]{:S(2)}, u32[]{:S(2)}) collective-permute-start(bf16[80,768]{1,0:T(8,128)(2,1)S(1)} %collective-permute-done.8.refs_5_), channel_id=1, source_target_pairs={{0,1},{1,0},{2,3},{3,2},{64,65},{65,64},{66,67},{67,66},{4,5},{5,4... | collective-permute-start | bytes 368648 | tf_op jit(solution)/shard_map/ppermute | solution.py:34
  62.6 2.6 %collective-permute-start.9 = (bf16[80,768]{1,0:T(8,128)(2,1)S(1)}, bf16[80,768]{1,0:T(8,128)(2,1)S(1)}, u32[]{:S(2)}, u32[]{:S(2)}) collective-permute-start(bf16[80,768]{1,0:T(8,128)(2,1)S(1)} %add_convert_fusion.6.refs_4_.refs_8_), channel_id=1, source_target_pairs={{0,1},{1,0},{2,3},{3,2},{64,65},{65,64},{66,67},{67,66},{4,5},{5,4... | collective-permute-start | bytes 368648 | tf_op jit(solution)/shard_map/ppermute | solution.py:34
  94.6 3.6 %collective-permute-start.13 = (bf16[80,768]{1,0:T(8,128)(2,1)S(1)}, bf16[80,768]{1,0:T(8,128)(2,1)S(1)}, u32[]{:S(2)}, u32[]{:S(2)}) collective-permute-start(bf16[80,768]{1,0:T(8,128)(2,1)S(1)} %get-tuple-element.52), channel_id=1, source_target_pairs={{0,1},{1,0},{2,3},{3,2},{64,65},{65,64},{66,67},{67,66},{4,5},{5,4... | collective-permute-start | bytes 368648 | tf_op jit(solution)/shard_map/ppermute | solution.py:34
  97.2 1.3 %collective-permute-start.11 = (bf16[80,768]{1,0:T(8,128)(2,1)S(1)}, bf16[80,768]{1,0:T(8,128)(2,1)S(1)}, u32[]{:S(2)}, u32[]{:S(2)}) collective-permute-start(bf16[80,768]{1,0:T(8,128)(2,1)S(1)} %get-tuple-element.47), channel_id=1, source_target_pairs={{0,1},{1,0},{2,3},{3,2},{64,65},{65,64},{66,67},{67,66},{4,5},{5,4... | collective-permute-start | bytes 368648 | tf_op jit(solution)/shard_map/ppermute | solution.py:34
  98.2 4.6 %collective-permute-start.14 = (bf16[80,768]{1,0:T(8,128)(2,1)S(1)}, bf16[80,768]{1,0:T(8,128)(2,1)S(1)}, u32[]{:S(2)}, u32[]{:S(2)}) collective-permute-start(bf16[80,768]{1,0:T(8,128)(2,1)S(1)} %add_convert_fusion.1), channel_id=1, source_target_pairs={{0,2},{1,3},{2,0},{3,1},{64,66},{65,67},{66,64},{67,65},{4,6},{5,7... | collective-permute-start | bytes 368648 | tf_op jit(solution)/shard_map/ppermute | solution.py:34
  98.5 6.9 %collective-permute-start.12 = (bf16[80,768]{1,0:T(8,128)(2,1)S(1)}, bf16[80,768]{1,0:T(8,128)(2,1)S(1)}, u32[]{:S(2)}, u32[]{:S(2)}) collective-permute-start(bf16[80,768]{1,0:T(8,128)(2,1)S(1)} %add_convert_fusion.3), channel_id=1, source_target_pairs={{0,2},{1,3},{2,0},{3,1},{64,66},{65,67},{66,64},{67,65},{4,6},{5,7... | collective-permute-start | bytes 368648 | tf_op jit(solution)/shard_map/ppermute | solution.py:34
  102.8 4.7 %collective-permute-start.16 = (bf16[80,768]{1,0:T(8,128)(2,1)S(1)}, bf16[80,768]{1,0:T(8,128)(2,1)S(1)}, u32[]{:S(2)}, u32[]{:S(2)}) collective-permute-start(bf16[80,768]{1,0:T(8,128)(2,1)S(1)} %add_convert_fusion), channel_id=1, source_target_pairs={{0,1},{1,0},{2,3},{3,2},{64,65},{65,64},{66,67},{67,66},{4,5},{5,4... | collective-permute-start | bytes 368648 | tf_op jit(solution)/shard_map/ppermute | solution.py:34
  105.5 2.2 %collective-permute-start.15 = (bf16[80,768]{1,0:T(8,128)(2,1)S(1)}, bf16[80,768]{1,0:T(8,128)(2,1)S(1)}, u32[]{:S(2)}, u32[]{:S(2)}) collective-permute-start(bf16[80,768]{1,0:T(8,128)(2,1)S(1)} %add_convert_fusion.2), channel_id=1, source_target_pairs={{0,1},{1,0},{2,3},{3,2},{64,65},{65,64},{66,67},{67,66},{4,5},{5,4... | collective-permute-start | bytes 368648 | tf_op jit(solution)/shard_map/ppermute | solution.py:34

commit v7 on v6

--- a/solution.py
+++ b/solution.py
@@ -127,17 +127,17 @@
     )(*operands)
 
 
-def project(normed_ref, wqk_ref, wv_ref, o_ref, kv_ref, rows, load=None):
+def project(normed_ref, wqk_ref, wv_ref, o_ref, kv_ref, rows, loads=()):
     columns = wv_ref.shape[1]
     blocks = columns // LANES
     requests = normed_ref.shape[0] // rows
     for unit in range(requests * blocks, o_ref.shape[0]):
         o_ref[unit] = jnp.zeros(o_ref.shape[1:], o_ref.dtype)
     for part in range(3):
-        if part == 2 and load is not None:
-            load.wait()
         for wide in range(0, columns, WIDE):
             at = slice(wide, wide + WIDE)
+            if part == 2 and loads:
+                loads[wide // WIDE].wait()
             weight = wqk_ref[part, :, at] if part < 2 else wv_ref[:, at]
             acc = jnp.dot(normed_ref[...], weight, preferred_element_type=jnp.float32).astype(jnp.bfloat16)
             if part:
@@ -165,12 +165,16 @@
     wv_ref,
     pieces_ref,
     normed_ref,
-    sem,
+    sems,
     *,
     rows,
 ):
-    load = pltpu.make_async_copy(w_ref.at[2], wv_ref, sem)
-    load.start()
+    loads = []
+    for index in range(wv_ref.shape[1] // WIDE):
+        at = pl.ds(index * WIDE, WIDE)
+        copy = pltpu.make_async_copy(w_ref.at[2, :, at], wv_ref.at[:, at], sems.at[index])
+        copy.start()
+        loads.append(copy)
     for index, piece in enumerate((mod_0, mod_1, mod_2, mod_3)):
         pieces_ref[lax.axis_index("mp") ^ index, 0:1, :] = piece[...]
     total, width = unit_ref.shape
@@ -189,7 +193,7 @@
         normed_ref[start : start + step, :] = normed.astype(jnp.bfloat16)
     for unit in range(stale_ref.shape[0]):
         o_ref[unit, 3 * rows :, :] = stale_ref[unit]
-    project(normed_ref, wqk_ref, wv_ref, o_ref, kv_ref, rows, load)
+    project(normed_ref, wqk_ref, wv_ref, o_ref, kv_ref, rows, loads)
 
 
 def first_call(unit, mods, weight_qk, weight, stale, rows, devices):
@@ -207,7 +211,7 @@
         scratch_shapes=[
             pltpu.VMEM((4, 8, mods[0].shape[1]), jnp.float32),
             pltpu.VMEM((total, width), jnp.bfloat16),
-            pltpu.SemaphoreType.DMA,
+            pltpu.SemaphoreType.DMA((weight.shape[2] // WIDE,)),
         ],
         compiler_params=PARAMS,
         name="first_qkv",

time: 109 us -> 109 us (level)
  no operation moved by 1% of the time
where the time goes in v7:
time: 109 us
  blocking collectives  54 us (50%)
  starting transfers between devices  22.8 us (21%)
  Pallas kernels  19.1 us (18%)
  waiting for transfers between devices  9.46 us (9%)
  between operations  1.78 us (2%)
    ppermute x17, starting transfers between devices, swap(): return lax.ppermute(value, ('section', 'mp'), pairs)  22.8 us
    all_to_all x2, blocking collectives, body(): lax.all_to_all(attended, 'seq', 0, 0, tiled=True)  20.5 us
    all_to_all x1, blocking collectives, body(): recv_0 = lax.all_to_all(sent_0, 'seq', 0, 0, tiled=True)  20.4 us
    all_to_all x1, blocking collectives, body(): recv_1 = lax.all_to_all(sent_1, 'seq', 0, 0, tiled=True)  13.1 us
    ppermute x17, waiting for transfers between devices, swap(): return lax.ppermute(value, ('section', 'mp'), pairs)  9.46 us
    pallas_call x2, Pallas kernels, attention_call(): pl.pallas_call(lambda *refs: attention_kernel(*refs, rows=rows, per_dev=p...  4.77 us
    pallas_call x1, Pallas kernels, prepare_call(): pl.pallas_call(prepare_kernel, out_shape=(pltpu.VMEM((total, width), jnp....  3.98 us
    pallas_call x1, Pallas kernels, first_call(): pl.pallas_call(lambda *refs: first_kernel(*refs, rows=rows), out_shape=(j...  3.52 us
  transfers between devices with their start and end apart: 17, of which 9 were waited for; matrix products, arithmetic and copies ran while one was open for 0% of the time, Pallas kernels for 5%

profile of v7, /device:TPU:1, one launch (start us, length us, event | category | flops | bytes accessed | tf_op | source)
XLA Modules:
  0.0 108.7 jit_solution(18321932073060724886)
XLA Ops:
  0.6 0.0 copy-start
  1.5 0.8 copy-done
  2.3 0.4 fusion.refs_1_
  2.7 2.6 %collective-permute-start.2 = (f32[1,2304]{1,0:T(1,128)S(1)}, f32[1,2304]{1,0:T(1,128)S(1)}, u32[]{:S(2)}, u32[]{:S(2)}) collective-permute-start(f32[1,2304]{1,0:T(1,128)S(1)} %fusion.refs_1_), channel_id=1, source_target_pairs={{0,3},{1,2},{2,1},{3,0},{64,67},{65,66},{66,65},{67,64},{4,7},{5,6... | collective-permute-start | bytes 27656 | tf_op jit(solution)/shard_map/ppermute | solution.py:34
  5.3 0.2 collective-permute-start.1
  5.5 0.3 collective-permute-start
  5.8 4.0 %prepare.1 = (f32[80,3072]{1,0:T(8,128)S(1)}, bf16[12,48,128]{2,1,0:T(8,128)(2,1)S(1)}, bf16[2,3072,768]{2,1,0:T(8,128)(2,1)S(1)}, bf16[80,768]{1,0:T(8,128)(2,1)S(1)}, bf16[80,768]{1,0:T(8,128)(2,1)S(1)}) custom-call(bf16[2,4,8,3072]{3,2,1,0:T(8,128)(2,1)} %video_ref.1, bf16[2,8,3072]{2,1,0:T(8,128)(2,1)} %text_ref.1, bf16[3,3072,768]{2,1,0:T(8,128)(2,1)} %bitcast.24, ...), custom_call_target="tpu_custom_call" | custom-call | tf_op jit(solution)/shard_map/prepare/pallas_call | solution.py:108
  9.8 0.0 collective-permute-done.2.refs_4_
  9.8 0.0 collective-permute-done.1.refs_3_
  9.8 0.0 collective-permute-done.refs_2_
  9.8 0.0 slice-start
  9.8 0.0 copy-start.1
  9.8 0.0 copy-start.2
  9.9 0.0 slice-start.1
  9.9 3.5 %first_qkv.1 = (bf16[16,168,128]{2,1,0:T(8,128)(2,1)S(1)}, bf16[2,80,768]{2,1,0:T(8,128)(2,1)S(1)}, f32[3,3072]{1,0:T(4,128)S(1)}, bf16[3072,768]{1,0:T(8,128)(2,1)S(1)}) custom-call(f32[80,3072]{1,0:T(8,128)S(1)} %get-tuple-element.31.refs_0_, f32[1,2304]{1,0:T(1,128)S(1)} %fusion.refs_1_, f32[1,2304]{1,0:T(1,128)S(1)} %collective-permute-done.refs_2_, ...), custom_call_target="tpu_custom_call" | custom-call | tf_op jit(solution)/shard_map/first_qkv/pallas_call | solution.py:201
  13.4 20.4 %all_to_all.20.refs_2_.refs_3_ = bf16[16,168,128]{2,1,0:T(8,128)(2,1)S(1)} all-to-all(bf16[16,168,128]{2,1,0:T(8,128)(2,1)S(1)} %get-tuple-element.38), channel_id=1, replica_groups=mesh['section'=2,'seq'=16,'mp'=4] {'seq'}, dimensions={0} | all-to-all | bytes 1376256 | tf_op jit(solution)/shard_map/all_to_all | solution.py:514
  33.8 0.0 copy-done.1
  33.8 0.0 copy-done.2
  33.8 2.4 %attention.2 = bf16[16,40,128]{2,1,0:T(8,128)(2,1)S(1)} custom-call(s32[2,4]{1,0:T(2,128)S(1)} %copy-done.1, s32[2]{0:T(128)S(1)} %copy-done.2, bf16[16,168,128]{2,1,0:T(8,128)(2,1)S(1)} %all_to_all.20.refs_2_.refs_3_, bf16[16,168,128]{2,1,0:T(8,128)(2,1)S(1)} %all_to_all.20.refs_2_.refs_3_), custom_call_target="tpu_custom_call" | custom-call | tf_op jit(solution)/shard_map/attention/pallas_call | solution.py:346
  36.2 10.1 %all_to_all.21.refs_0_ = bf16[16,40,128]{2,1,0:T(8,128)(2,1)S(1)} all-to-all(bf16[16,40,128]{2,1,0:T(8,128)(2,1)S(1)} %attention.2), channel_id=1, replica_groups=mesh['section'=2,'seq'=16,'mp'=4] {'seq'}, dimensions={0} | all-to-all | bytes 327680 | tf_op jit(solution)/shard_map/all_to_all | solution.py:517
  46.3 0.0 slice-done
  46.3 0.0 slice-done.1
  46.4 0.6 out_projection.5
  46.9 2.5 %collective-permute-start.6 = (bf16[80,768]{1,0:T(8,128)(2,1)S(1)}, bf16[80,768]{1,0:T(8,128)(2,1)S(1)}, u32[]{:S(2)}, u32[]{:S(2)}) collective-permute-start(bf16[80,768]{1,0:T(8,128)(2,1)S(1)} %get-tuple-element.43), channel_id=1, source_target_pairs={{0,1},{1,0},{2,3},{3,2},{64,65},{65,64},{66,67},{67,66},{4,5},{5,4... | collective-permute-start | bytes 368648 | tf_op jit(solution)/shard_map/ppermute | solution.py:34
  49.5 0.1 collective-permute-start.3
  49.5 0.6 out_projection.4
  50.1 0.3 collective-permute-done.6
  50.5 1.2 %collective-permute-start.7 = (bf16[80,768]{1,0:T(8,128)(2,1)S(1)}, bf16[80,768]{1,0:T(8,128)(2,1)S(1)}, u32[]{:S(2)}, u32[]{:S(2)}) collective-permute-start(bf16[80,768]{1,0:T(8,128)(2,1)S(1)} %add_convert_fusion.5), channel_id=1, source_target_pairs={{0,2},{1,3},{2,0},{3,1},{64,66},{65,67},{66,64},{67,65},{4,6},{5,7... | collective-permute-start | bytes 368648 | tf_op jit(solution)/shard_map/ppermute | solution.py:34
  51.7 0.0 collective-permute-done.3
  51.7 1.9 %collective-permute-start.4 = (bf16[80,768]{1,0:T(8,128)(2,1)S(1)}, bf16[80,768]{1,0:T(8,128)(2,1)S(1)}, u32[]{:S(2)}, u32[]{:S(2)}) collective-permute-start(bf16[80,768]{1,0:T(8,128)(2,1)S(1)} %add_convert_fusion.7.own_ref), channel_id=1, source_target_pairs={{0,66},{1,67},{2,64},{3,65},{64,2},{65,3},{66,0},{67,1},{4,70},{5,... | collective-permute-start | bytes 368648 | tf_op jit(solution)/shard_map/ppermute | solution.py:34
  53.6 1.5 %collective-permute-done.7 = bf16[80,768]{1,0:T(8,128)(2,1)S(1)} collective-permute-done((bf16[80,768]{1,0:T(8,128)(2,1)S(1)}, bf16[80,768]{1,0:T(8,128)(2,1)S(1)}, u32[]{:S(2)}, u32[]{:S(2)}) %collective-permute-start.7) | collective-permute-done | bytes 122912 | tf_op jit(solution)/shard_map/ppermute | solution.py:34
  55.1 0.1 add_convert_fusion.4.refs_9_
  55.1 2.5 %collective-permute-start.8 = (bf16[80,768]{1,0:T(8,128)(2,1)S(1)}, bf16[80,768]{1,0:T(8,128)(2,1)S(1)}, u32[]{:S(2)}, u32[]{:S(2)}) collective-permute-start(bf16[80,768]{1,0:T(8,128)(2,1)S(1)} %add_convert_fusion.4.refs_9_), channel_id=1, source_target_pairs={{0,66},{1,67},{2,64},{3,65},{64,2},{65,3},{66,0},{67,1},{4,70},{5,... | collective-permute-start | bytes 368648 | tf_op jit(solution)/shard_map/ppermute | solution.py:34
  57.6 0.0 collective-permute-done.4.arrived_ref
  57.6 0.1 collective-permute-start.5
  57.7 2.4 %collective-permute-done.8.refs_5_ = bf16[80,768]{1,0:T(8,128)(2,1)S(1)} collective-permute-done((bf16[80,768]{1,0:T(8,128)(2,1)S(1)}, bf16[80,768]{1,0:T(8,128)(2,1)S(1)}, u32[]{:S(2)}, u32[]{:S(2)}) %collective-permute-start.8) | collective-permute-done | bytes 122912 | tf_op jit(solution)/shard_map/ppermute | solution.py:34
  60.2 2.3 %collective-permute-start.10 = (bf16[80,768]{1,0:T(8,128)(2,1)S(1)}, bf16[80,768]{1,0:T(8,128)(2,1)S(1)}, u32[]{:S(2)}, u32[]{:S(2)}) collective-permute-start(bf16[80,768]{1,0:T(8,128)(2,1)S(1)} %collective-permute-done.8.refs_5_), channel_id=1, source_target_pairs={{0,1},{1,0},{2,3},{3,2},{64,65},{65,64},{66,67},{67,66},{4,5},{5,4... | collective-permute-start | bytes 368648 | tf_op jit(solution)/shard_map/ppermute | solution.py:34
  62.5 0.0 collective-permute-done.5
  62.5 0.1 add_convert_fusion.6.refs_4_.refs_8_
  62.6 1.6 %collective-permute-start.9 = (bf16[80,768]{1,0:T(8,128)(2,1)S(1)}, bf16[80,768]{1,0:T(8,128)(2,1)S(1)}, u32[]{:S(2)}, u32[]{:S(2)}) collective-permute-start(bf16[80,768]{1,0:T(8,128)(2,1)S(1)} %add_convert_fusion.6.refs_4_.refs_8_), channel_id=1, source_target_pairs={{0,1},{1,0},{2,3},{3,2},{64,65},{65,64},{66,67},{67,66},{4,5},{5,4... | collective-permute-start | bytes 368648 | tf_op jit(solution)/shard_map/ppermute | solution.py:34
  64.2 0.0 collective-permute-done.10.refs_7_
  64.2 1.0 collective-permute-done.9.refs_6_
  65.2 2.9 %second_qkv.1 = (bf16[16,120,128]{2,1,0:T(8,128)(2,1)S(1)}, bf16[2,80,768]{2,1,0:T(8,128)(2,1)S(1)}, bf16[80,768]{1,0:T(8,128)(2,1)S(1)}, bf16[80,768]{1,0:T(8,128)(2,1)S(1)}) custom-call(f32[3,3072]{1,0:T(4,128)S(1)} %get-tuple-element.34.refs_1_.refs_0_, bf16[2,3072,768]{2,1,0:T(8,128)(2,1)S(1)} %get-tuple-element.32.refs_5_.refs_1_, ...), custom_call_target="tpu_custom_call" | custom-call | tf_op jit(solution)/shard_map/second_qkv/pallas_call | solution.py:262
  68.1 13.1 %all_to_all.22.refs_2_ = bf16[16,120,128]{2,1,0:T(8,128)(2,1)S(1)} all-to-all(bf16[16,120,128]{2,1,0:T(8,128)(2,1)S(1)} %get-tuple-element.45), channel_id=1, replica_groups=mesh['section'=2,'seq'=16,'mp'=4] {'seq'}, dimensions={0} | all-to-all | bytes 983040 | tf_op jit(solution)/shard_map/all_to_all | solution.py:525
  81.2 2.4 %attention.3 = bf16[16,40,128]{2,1,0:T(8,128)(2,1)S(1)} custom-call(s32[2,4]{1,0:T(2,128)S(1)} %copy-done.1, s32[2]{0:T(128)S(1)} %copy-done.2, bf16[16,120,128]{2,1,0:T(8,128)(2,1)S(1)} %all_to_all.22.refs_2_, bf16[16,168,128]{2,1,0:T(8,128)(2,1)S(1)} %all_to_all.20.refs_2_.refs_3_), custom_call_target="tpu_custom_call" | custom-call | tf_op jit(solution)/shard_map/attention/pallas_call | solution.py:346
  83.6 10.3 %all_to_all.23.refs_0_ = bf16[16,40,128]{2,1,0:T(8,128)(2,1)S(1)} all-to-all(bf16[16,40,128]{2,1,0:T(8,128)(2,1)S(1)} %attention.3), channel_id=1, replica_groups=mesh['section'=2,'seq'=16,'mp'=4] {'seq'}, dimensions={0} | all-to-all | bytes 327680 | tf_op jit(solution)/shard_map/all_to_all | solution.py:527
  94.0 0.6 out_projection.7
  94.5 2.6 %collective-permute-start.13 = (bf16[80,768]{1,0:T(8,128)(2,1)S(1)}, bf16[80,768]{1,0:T(8,128)(2,1)S(1)}, u32[]{:S(2)}, u32[]{:S(2)}) collective-permute-start(bf16[80,768]{1,0:T(8,128)(2,1)S(1)} %get-tuple-element.52), channel_id=1, source_target_pairs={{0,1},{1,0},{2,3},{3,2},{64,65},{65,64},{66,67},{67,66},{4,5},{5,4... | collective-permute-start | bytes 368648 | tf_op jit(solution)/shard_map/ppermute | solution.py:34
  97.1 0.1 collective-permute-start.11
  97.2 0.6 out_projection.6
  97.8 0.3 collective-permute-done.13
  98.1 0.1 collective-permute-start.14
  98.2 0.2 collective-permute-done.11
  98.5 1.3 %collective-permute-start.12 = (bf16[80,768]{1,0:T(8,128)(2,1)S(1)}, bf16[80,768]{1,0:T(8,128)(2,1)S(1)}, u32[]{:S(2)}, u32[]{:S(2)}) collective-permute-start(bf16[80,768]{1,0:T(8,128)(2,1)S(1)} %add_convert_fusion.3), channel_id=1, source_target_pairs={{0,2},{1,3},{2,0},{3,1},{64,66},{65,67},{66,64},{67,65},{4,6},{5,7... | collective-permute-start | bytes 368648 | tf_op jit(solution)/shard_map/ppermute | solution.py:34
  99.8 3.0 %collective-permute-done.14 = bf16[80,768]{1,0:T(8,128)(2,1)S(1)} collective-permute-done((bf16[80,768]{1,0:T(8,128)(2,1)S(1)}, bf16[80,768]{1,0:T(8,128)(2,1)S(1)}, u32[]{:S(2)}, u32[]{:S(2)}) %collective-permute-start.14) | collective-permute-done | bytes 122912 | tf_op jit(solution)/shard_map/ppermute | solution.py:34
  102.8 2.1 %collective-permute-start.16 = (bf16[80,768]{1,0:T(8,128)(2,1)S(1)}, bf16[80,768]{1,0:T(8,128)(2,1)S(1)}, u32[]{:S(2)}, u32[]{:S(2)}) collective-permute-start(bf16[80,768]{1,0:T(8,128)(2,1)S(1)} %add_convert_fusion), channel_id=1, source_target_pairs={{0,1},{1,0},{2,3},{3,2},{64,65},{65,64},{66,67},{67,66},{4,5},{5,4... | collective-permute-start | bytes 368648 | tf_op jit(solution)/shard_map/ppermute | solution.py:34
  104.9 0.5 collective-permute-done.12
  105.4 1.3 %collective-permute-start.15 = (bf16[80,768]{1,0:T(8,128)(2,1)S(1)}, bf16[80,768]{1,0:T(8,128)(2,1)S(1)}, u32[]{:S(2)}, u32[]{:S(2)}) collective-permute-start(bf16[80,768]{1,0:T(8,128)(2,1)S(1)} %add_convert_fusion.2), channel_id=1, source_target_pairs={{0,1},{1,0},{2,3},{3,2},{64,65},{65,64},{66,67},{67,66},{4,5},{5,4... | collective-permute-start | bytes 368648 | tf_op jit(solution)/shard_map/ppermute | solution.py:34
  106.7 0.8 cache.1
  107.5 0.0 collective-permute-done.16
  107.5 0.2 collective-permute-done.15
  107.7 0.8 store.1
  (11 shorter events, 0.3 us)
Async XLA Ops:
  0.6 1.7 %copy-start = (bf16[1,512,2304]{2,1,0:T(8,128)(2,1)S(1)}, bf16[1,512,2304]{2,1,0:T(8,128)(2,1)}, u32[]{:S(2)}) copy-start(bf16[1,512,2304]{2,1,0:T(8,128)(2,1)} %param.14) | copy-start | bytes 7077892
  2.7 7.1 %collective-permute-start.2 = (f32[1,2304]{1,0:T(1,128)S(1)}, f32[1,2304]{1,0:T(1,128)S(1)}, u32[]{:S(2)}, u32[]{:S(2)}) collective-permute-start(f32[1,2304]{1,0:T(1,128)S(1)} %fusion.refs_1_), channel_id=1, source_target_pairs={{0,3},{1,2},{2,1},{3,0},{64,67},{65,66},{66,65},{67,64},{4,7},{5,6... | collective-permute-start | bytes 27656 | tf_op jit(solution)/shard_map/ppermute | solution.py:34
  5.3 4.5 %collective-permute-start.1 = (f32[1,2304]{1,0:T(1,128)S(1)}, f32[1,2304]{1,0:T(1,128)S(1)}, u32[]{:S(2)}, u32[]{:S(2)}) collective-permute-start(f32[1,2304]{1,0:T(1,128)S(1)} %fusion.refs_1_), channel_id=1, source_target_pairs={{0,2},{1,3},{2,0},{3,1},{64,66},{65,67},{66,64},{67,65},{4,6},{5,7... | collective-permute-start | bytes 27656 | tf_op jit(solution)/shard_map/ppermute | solution.py:34
  5.5 4.3 %collective-permute-start = (f32[1,2304]{1,0:T(1,128)S(1)}, f32[1,2304]{1,0:T(1,128)S(1)}, u32[]{:S(2)}, u32[]{:S(2)}) collective-permute-start(f32[1,2304]{1,0:T(1,128)S(1)} %fusion.refs_1_), channel_id=1, source_target_pairs={{0,1},{1,0},{2,3},{3,2},{64,65},{65,64},{66,67},{67,66},{4,5},{5,4... | collective-permute-start | bytes 27656 | tf_op jit(solution)/shard_map/ppermute | solution.py:34
  9.8 36.5 %slice-start = ((s8[4718592]{0:T(1024)(128)(4,1)}), s8[4194304]{0:T(1024)(128)(4,1)S(1)}, s32[]{:S(2)}) async-start(s8[4718592]{0:T(1024)(128)(4,1)} %bitcast.14), calls=%async_computation.4 | async-start | bytes 8388608
  9.8 24.0 %copy-start.1 = (s32[2,4]{1,0:T(2,128)S(1)}, s32[2,4]{1,0:T(2,128)}, u32[]{:S(2)}) copy-start(s32[2,4]{1,0:T(2,128)} %refs_0_.3) | copy-start | bytes 100
  9.8 24.0 %copy-start.2 = (s32[2]{0:T(128)S(1)}, s32[2]{0:T(128)}, u32[]{:S(2)}) copy-start(s32[2]{0:T(128)} %refs_1_.3) | copy-start | bytes 28
  9.9 36.5 %slice-start.1 = ((s8[4718592]{0:T(1024)(128)(4,1)}), s8[524288]{0:T(1024)(128)(4,1)S(1)}, s32[]{:S(2)}) async-start(s8[4718592]{0:T(1024)(128)(4,1)} %bitcast.14), calls=%async_computation.5 | async-start | bytes 1048576
  46.9 3.5 %collective-permute-start.6 = (bf16[80,768]{1,0:T(8,128)(2,1)S(1)}, bf16[80,768]{1,0:T(8,128)(2,1)S(1)}, u32[]{:S(2)}, u32[]{:S(2)}) collective-permute-start(bf16[80,768]{1,0:T(8,128)(2,1)S(1)} %get-tuple-element.43), channel_id=1, source_target_pairs={{0,1},{1,0},{2,3},{3,2},{64,65},{65,64},{66,67},{67,66},{4,5},{5,4... | collective-permute-start | bytes 368648 | tf_op jit(solution)/shard_map/ppermute | solution.py:34
  49.5 2.2 %collective-permute-start.3 = (bf16[80,768]{1,0:T(8,128)(2,1)S(1)}, bf16[80,768]{1,0:T(8,128)(2,1)S(1)}, u32[]{:S(2)}, u32[]{:S(2)}) collective-permute-start(bf16[80,768]{1,0:T(8,128)(2,1)S(1)} %get-tuple-element.40), channel_id=1, source_target_pairs={{0,1},{1,0},{2,3},{3,2},{64,65},{65,64},{66,67},{67,66},{4,5},{5,4... | collective-permute-start | bytes 368648 | tf_op jit(solution)/shard_map/ppermute | solution.py:34
  50.5 4.6 %collective-permute-start.7 = (bf16[80,768]{1,0:T(8,128)(2,1)S(1)}, bf16[80,768]{1,0:T(8,128)(2,1)S(1)}, u32[]{:S(2)}, u32[]{:S(2)}) collective-permute-start(bf16[80,768]{1,0:T(8,128)(2,1)S(1)} %add_convert_fusion.5), channel_id=1, source_target_pairs={{0,2},{1,3},{2,0},{3,1},{64,66},{65,67},{66,64},{67,65},{4,6},{5,7... | collective-permute-start | bytes 368648 | tf_op jit(solution)/shard_map/ppermute | solution.py:34
  51.7 5.9 %collective-permute-start.4 = (bf16[80,768]{1,0:T(8,128)(2,1)S(1)}, bf16[80,768]{1,0:T(8,128)(2,1)S(1)}, u32[]{:S(2)}, u32[]{:S(2)}) collective-permute-start(bf16[80,768]{1,0:T(8,128)(2,1)S(1)} %add_convert_fusion.7.own_ref), channel_id=1, source_target_pairs={{0,66},{1,67},{2,64},{3,65},{64,2},{65,3},{66,0},{67,1},{4,70},{5,... | collective-permute-start | bytes 368648 | tf_op jit(solution)/shard_map/ppermute | solution.py:34
  55.1 5.0 %collective-permute-start.8 = (bf16[80,768]{1,0:T(8,128)(2,1)S(1)}, bf16[80,768]{1,0:T(8,128)(2,1)S(1)}, u32[]{:S(2)}, u32[]{:S(2)}) collective-permute-start(bf16[80,768]{1,0:T(8,128)(2,1)S(1)} %add_convert_fusion.4.refs_9_), channel_id=1, source_target_pairs={{0,66},{1,67},{2,64},{3,65},{64,2},{65,3},{66,0},{67,1},{4,70},{5,... | collective-permute-start | bytes 368648 | tf_op jit(solution)/shard_map/ppermute | solution.py:34
  57.6 4.9 %collective-permute-start.5 = (bf16[80,768]{1,0:T(8,128)(2,1)S(1)}, bf16[80,768]{1,0:T(8,128)(2,1)S(1)}, u32[]{:S(2)}, u32[]{:S(2)}) collective-permute-start(bf16[80,768]{1,0:T(8,128)(2,1)S(1)} %pick.1), channel_id=1, source_target_pairs={{0,2},{1,3},{2,0},{3,1},{64,66},{65,67},{66,64},{67,65},{4,6},{5,7... | collective-permute-start | bytes 368648 | tf_op jit(solution)/shard_map/ppermute | solution.py:34
  60.2 4.0 %collective-permute-start.10 = (bf16[80,768]{1,0:T(8,128)(2,1)S(1)}, bf16[80,768]{1,0:T(8,128)(2,1)S(1)}, u32[]{:S(2)}, u32[]{:S(2)}) collective-permute-start(bf16[80,768]{1,0:T(8,128)(2,1)S(1)} %collective-permute-done.8.refs_5_), channel_id=1, source_target_pairs={{0,1},{1,0},{2,3},{3,2},{64,65},{65,64},{66,67},{67,66},{4,5},{5,4... | collective-permute-start | bytes 368648 | tf_op jit(solution)/shard_map/ppermute | solution.py:34
  62.6 2.6 %collective-permute-start.9 = (bf16[80,768]{1,0:T(8,128)(2,1)S(1)}, bf16[80,768]{1,0:T(8,128)(2,1)S(1)}, u32[]{:S(2)}, u32[]{:S(2)}) collective-permute-start(bf16[80,768]{1,0:T(8,128)(2,1)S(1)} %add_convert_fusion.6.refs_4_.refs_8_), channel_id=1, source_target_pairs={{0,1},{1,0},{2,3},{3,2},{64,65},{65,64},{66,67},{67,66},{4,5},{5,4... | collective-permute-start | bytes 368648 | tf_op jit(solution)/shard_map/ppermute | solution.py:34
  94.5 3.6 %collective-permute-start.13 = (bf16[80,768]{1,0:T(8,128)(2,1)S(1)}, bf16[80,768]{1,0:T(8,128)(2,1)S(1)}, u32[]{:S(2)}, u32[]{:S(2)}) collective-permute-start(bf16[80,768]{1,0:T(8,128)(2,1)S(1)} %get-tuple-element.52), channel_id=1, source_target_pairs={{0,1},{1,0},{2,3},{3,2},{64,65},{65,64},{66,67},{67,66},{4,5},{5,4... | collective-permute-start | bytes 368648 | tf_op jit(solution)/shard_map/ppermute | solution.py:34
  97.1 1.3 %collective-permute-start.11 = (bf16[80,768]{1,0:T(8,128)(2,1)S(1)}, bf16[80,768]{1,0:T(8,128)(2,1)S(1)}, u32[]{:S(2)}, u32[]{:S(2)}) collective-permute-start(bf16[80,768]{1,0:T(8,128)(2,1)S(1)} %get-tuple-element.47), channel_id=1, source_target_pairs={{0,1},{1,0},{2,3},{3,2},{64,65},{65,64},{66,67},{67,66},{4,5},{5,4... | collective-permute-start | bytes 368648 | tf_op jit(solution)/shard_map/ppermute | solution.py:34
  98.1 4.6 %collective-permute-start.14 = (bf16[80,768]{1,0:T(8,128)(2,1)S(1)}, bf16[80,768]{1,0:T(8,128)(2,1)S(1)}, u32[]{:S(2)}, u32[]{:S(2)}) collective-permute-start(bf16[80,768]{1,0:T(8,128)(2,1)S(1)} %add_convert_fusion.1), channel_id=1, source_target_pairs={{0,2},{1,3},{2,0},{3,1},{64,66},{65,67},{66,64},{67,65},{4,6},{5,7... | collective-permute-start | bytes 368648 | tf_op jit(solution)/shard_map/ppermute | solution.py:34
  98.5 6.9 %collective-permute-start.12 = (bf16[80,768]{1,0:T(8,128)(2,1)S(1)}, bf16[80,768]{1,0:T(8,128)(2,1)S(1)}, u32[]{:S(2)}, u32[]{:S(2)}) collective-permute-start(bf16[80,768]{1,0:T(8,128)(2,1)S(1)} %add_convert_fusion.3), channel_id=1, source_target_pairs={{0,2},{1,3},{2,0},{3,1},{64,66},{65,67},{66,64},{67,65},{4,6},{5,7... | collective-permute-start | bytes 368648 | tf_op jit(solution)/shard_map/ppermute | solution.py:34
  102.8 4.7 %collective-permute-start.16 = (bf16[80,768]{1,0:T(8,128)(2,1)S(1)}, bf16[80,768]{1,0:T(8,128)(2,1)S(1)}, u32[]{:S(2)}, u32[]{:S(2)}) collective-permute-start(bf16[80,768]{1,0:T(8,128)(2,1)S(1)} %add_convert_fusion), channel_id=1, source_target_pairs={{0,1},{1,0},{2,3},{3,2},{64,65},{65,64},{66,67},{67,66},{4,5},{5,4... | collective-permute-start | bytes 368648 | tf_op jit(solution)/shard_map/ppermute | solution.py:34
  105.4 2.2 %collective-permute-start.15 = (bf16[80,768]{1,0:T(8,128)(2,1)S(1)}, bf16[80,768]{1,0:T(8,128)(2,1)S(1)}, u32[]{:S(2)}, u32[]{:S(2)}) collective-permute-start(bf16[80,768]{1,0:T(8,128)(2,1)S(1)} %add_convert_fusion.2), channel_id=1, source_target_pairs={{0,1},{1,0},{2,3},{3,2},{64,65},{65,64},{66,67},{67,66},{4,5},{5,4... | collective-permute-start | bytes 368648 | tf_op jit(solution)/shard_map/ppermute | solution.py:34
